TPU v7x, 256 devices: a whole 4x4x8 slice. The times are simulated.
256 devices in a mesh: ctx: 32 (over z, y_lo, core), head: 8 (over x, y_hi).
Axes of the slice: x: 4, y: 4 (y_hi: 2, y_lo: 2; y = y_hi * 2 + y_lo), z: 8, core: 2. Of those that a mesh axis runs over, the one named last changes fastest.
Arguments:
- queries: bfloat16 [16384, 4096], P('ctx', 'head'), may hold values from -48 to 48
- keys: bfloat16 [16384, 1024], P('ctx', 'head'), may hold values from -4 to 4
- values: bfloat16 [16384, 1024], P('ctx', 'head'), may hold values from -6 to 6
- doc_start: int32 [16384], P('ctx'), may hold values from 0 to 16383, as said below
- out_weight: bfloat16 [4096, 4096], P('head'), may hold values from -0.09375 to 0.09375
Outputs:
- mixed: bfloat16 [16384, 4096], P(('ctx', 'head'))
Inputs may be any that keep to these rules, and one draw needn't show every extreme that they name: doc_start is non-decreasing, doc_start[i] <= i, and all tokens of a document share its first position; every document has at most 4096 tokens and one document has exactly 4096; the 4096-token document starts at a multiple of 1024, and all other documents lie inside aligned cells of 1024 tokens.
All inputs are finite; a program needn't handle non-finite values.
Results may differ from a plain program's by a relative error of at most 0.015.
Values may be sent and summed in bfloat16 or wider, within the bound.
No kernel may reach another device: no remote copies, remote signals or barrier semaphores. Data moves between devices by JAX's collectives and lax.ppermute only.
A program may use at most 192 MiB of HBM per device.

v0:
```python
import jax
import jax.numpy as jnp
from jax import lax
from jax.sharding import PartitionSpec as P

HD = 128
GROUP = 4


NEG_FILL = -1e30


def shifted(value, axis, steps):
    count = lax.axis_size(axis)
    leading, last = (max(0, -steps), min(count, count - steps))
    return lax.ppermute(value, axis, [(source, source + steps) for source in range(leading, last)])


def attend_block(state, queries, keys, values, key_start, doc_rows, query_pos):
    count = keys.shape[0]
    kv_heads = queries.shape[1]
    key_pos = key_start + jnp.arange(count, dtype=jnp.int32)
    needed = (key_start + count - 1 >= doc_rows[0]) & (key_start <= query_pos[-1])

    def compute(carry):
        running, total, accum = carry
        key_tile = keys.reshape(count, kv_heads, HD)
        value_tile = values.reshape(count, kv_heads, HD)
        scores = jnp.einsum(
            "tkgd,skd->kgts", queries, key_tile, preferred_element_type=jnp.float32
        ) * HD ** (-0.5)
        allowed = (key_pos[None, :] >= doc_rows[:, None]) & (key_pos[None, :] <= query_pos[:, None])
        scores = jnp.where(allowed, scores, NEG_FILL)
        newmax = jnp.maximum(running, jnp.max(scores, axis=-1))
        weights = jnp.where(allowed, jnp.exp(scores - newmax[..., None]), 0.0)
        factor = jnp.exp(running - newmax)
        total = total * factor + jnp.sum(weights, axis=-1)
        low_weight = weights.astype(jnp.bfloat16)
        accum = accum * factor[..., None] + jnp.einsum(
            "kgts,skd->kgtd", low_weight, value_tile, preferred_element_type=jnp.float32
        )
        return (newmax, total, accum)

    return lax.cond(needed, compute, lambda carry: carry, state)


def on_device(queries, keys, values, doc_start, out_weight):
    tok_rows = queries.shape[0]
    kv_heads = keys.shape[1] // HD
    my_index = lax.axis_index("ctx")
    cycle_size = lax.axis_size("ctx")
    query_pos = my_index * tok_rows + jnp.arange(tok_rows, dtype=jnp.int32)
    grouped = queries.reshape(tok_rows, kv_heads, GROUP, HD)
    initial = (
        jnp.full((kv_heads, GROUP, tok_rows), NEG_FILL, jnp.float32),
        jnp.zeros((kv_heads, GROUP, tok_rows), jnp.float32),
        jnp.zeros((kv_heads, GROUP, tok_rows, HD), jnp.float32),
    )
    stacked = jnp.stack([keys, values])

    def visit(state, tile, start):
        return attend_block(state, grouped, tile[0], tile[1], start, doc_start, query_pos)

    state = visit(initial, stacked, my_index * tok_rows)

    def whole_turn(step, packed):
        carry, tile = packed
        tile = shifted(tile, "ctx", 1)
        source = my_index - step
        return (visit(carry, tile, source * tok_rows), tile)

    state, unused = lax.fori_loop(1, cycle_size, whole_turn, (state, stacked))
    running, total, accum = state
    attended = (
        (accum / total[..., None])
        .transpose(2, 0, 1, 3)
        .reshape(tok_rows, kv_heads * GROUP * HD)
        .astype(jnp.bfloat16)
    )
    return lax.psum_scatter(
        jnp.dot(attended, out_weight, preferred_element_type=jnp.float32).astype(jnp.bfloat16),
        "head",
        scatter_dimension=0,
        tiled=True,
    )


def solution(mesh):
    return jax.shard_map(
        on_device,
        mesh=mesh,
        in_specs=(P("ctx", "head"), P("ctx", "head"), P("ctx", "head"), P("ctx"), P("head", None)),
        out_specs=P(("ctx", "head"), None),
        check_vma=False,
    )
```

profile of v0, /device:TPU:2, one launch (start us, length us, event | category | flops | bytes accessed | tf_op | source)
XLA Modules:
  0.0 430.3 jit_solution(12940831361897150521)
XLA Ops:
  9.6 1.3 copy.10
  12.2 5.5 %conditional.2 = (f32[1,4,512]{2,1,0:T(4,128)S(1)}, f32[1,4,512]{2,1,0:T(4,128)S(1)}, f32[1,4,512,128]{3,2,1,0:T(8,128)S(1)}) conditional(s32[]{:T(128)} %convert_element_type.34, () %tuple.50, (s32[512]{0:T(512)S(1)}, s32[512]{0:T(512)}, bf16[512,1,4,128]{0,3,2,1:T(8,128)(2,1)S(1)}, bf16[512,128]{1,0:T(8,128)(2,1)}, bf16[512,128]{1,0:T(8,128)(2,1)}) %tuple.83), branch_computations={%region_0.0_spmd, %region_1.4_spmd} | conditional | flops 551561216 | bytes 16093236 | solution.py:44
  13.2 1.8 fusion
  15.0 1.6 fusion.10
  17.7 258.8 %while.23 = (s32[]{:T(128)}, f32[1,4,512]{2,1,0:T(4,128)S(1)}, f32[1,4,512]{2,1,0:T(4,128)S(1)}, f32[1,4,512,128]{3,2,1,0:T(8,128)S(1)}, bf16[2,512,128]{2,1,0:T...) while((s32[]{:T(128)}, f32[1,4,512]{2,1,0:T(4,128)S(1)}, ...), condition=%wide.region_9.10_spmd, body=%wide.region_4.9_spmd.sunk | while | flops 551819776 | bytes 18231664 | solution.py:72
  17.7 1.8 collective-permute-start
  22.6 8.8 %collective-permute-start = (bf16[2,512,128]{2,1,0:T(8,128)(2,1)S(1)}, bf16[2,512,128]{2,1,0:T(8,128)(2,1)S(1)}, u32[]{:S(2)}, u32[]{:S(2)}) collective-permute-start(bf16[2,512,128]{2,1,0:T(8,128)(2,1)S(1)} %get-tuple-element.512), channel_id=1, source_target_pairs={{0,8},{8,16},{16,24},{24,32},{32,40},{40,48},{48,56},{56,64},{64,7... | collective-permute-start | bytes 786440 | tf_op jit(solution)/shard_map/while/body/eval_jaxpr/ppermute | solution.py:16
  31.5 1.2 slice.64
  34.6 2.1 collective-permute-start
  39.9 4.6 %collective-permute-start = (bf16[2,512,128]{2,1,0:T(8,128)(2,1)S(1)}, bf16[2,512,128]{2,1,0:T(8,128)(2,1)S(1)}, u32[]{:S(2)}, u32[]{:S(2)}) collective-permute-start(bf16[2,512,128]{2,1,0:T(8,128)(2,1)S(1)} %get-tuple-element.512), channel_id=1, source_target_pairs={{0,8},{8,16},{16,24},{24,32},{32,40},{40,48},{48,56},{56,64},{64,7... | collective-permute-start | bytes 786440 | tf_op jit(solution)/shard_map/while/body/eval_jaxpr/ppermute | solution.py:16
  44.5 1.2 slice.64
  47.6 4.6 %collective-permute-start = (bf16[2,512,128]{2,1,0:T(8,128)(2,1)S(1)}, bf16[2,512,128]{2,1,0:T(8,128)(2,1)S(1)}, u32[]{:S(2)}, u32[]{:S(2)}) collective-permute-start(bf16[2,512,128]{2,1,0:T(8,128)(2,1)S(1)} %get-tuple-element.512), channel_id=1, source_target_pairs={{0,8},{8,16},{16,24},{24,32},{32,40},{40,48},{48,56},{56,64},{64,7... | collective-permute-start | bytes 786440 | tf_op jit(solution)/shard_map/while/body/eval_jaxpr/ppermute | solution.py:16
  52.2 1.2 slice.64
  55.3 4.6 %collective-permute-start = (bf16[2,512,128]{2,1,0:T(8,128)(2,1)S(1)}, bf16[2,512,128]{2,1,0:T(8,128)(2,1)S(1)}, u32[]{:S(2)}, u32[]{:S(2)}) collective-permute-start(bf16[2,512,128]{2,1,0:T(8,128)(2,1)S(1)} %get-tuple-element.512), channel_id=1, source_target_pairs={{0,8},{8,16},{16,24},{24,32},{32,40},{40,48},{48,56},{56,64},{64,7... | collective-permute-start | bytes 786440 | tf_op jit(solution)/shard_map/while/body/eval_jaxpr/ppermute | solution.py:16
  59.9 1.2 slice.64
  63.1 4.6 %collective-permute-start = (bf16[2,512,128]{2,1,0:T(8,128)(2,1)S(1)}, bf16[2,512,128]{2,1,0:T(8,128)(2,1)S(1)}, u32[]{:S(2)}, u32[]{:S(2)}) collective-permute-start(bf16[2,512,128]{2,1,0:T(8,128)(2,1)S(1)} %get-tuple-element.512), channel_id=1, source_target_pairs={{0,8},{8,16},{16,24},{24,32},{32,40},{40,48},{48,56},{56,64},{64,7... | collective-permute-start | bytes 786440 | tf_op jit(solution)/shard_map/while/body/eval_jaxpr/ppermute | solution.py:16
  70.8 4.6 %collective-permute-start = (bf16[2,512,128]{2,1,0:T(8,128)(2,1)S(1)}, bf16[2,512,128]{2,1,0:T(8,128)(2,1)S(1)}, u32[]{:S(2)}, u32[]{:S(2)}) collective-permute-start(bf16[2,512,128]{2,1,0:T(8,128)(2,1)S(1)} %get-tuple-element.512), channel_id=1, source_target_pairs={{0,8},{8,16},{16,24},{24,32},{32,40},{40,48},{48,56},{56,64},{64,7... | collective-permute-start | bytes 786440 | tf_op jit(solution)/shard_map/while/body/eval_jaxpr/ppermute | solution.py:16
  75.4 1.2 slice.64
  78.5 4.9 %collective-permute-start = (bf16[2,512,128]{2,1,0:T(8,128)(2,1)S(1)}, bf16[2,512,128]{2,1,0:T(8,128)(2,1)S(1)}, u32[]{:S(2)}, u32[]{:S(2)}) collective-permute-start(bf16[2,512,128]{2,1,0:T(8,128)(2,1)S(1)} %get-tuple-element.512), channel_id=1, source_target_pairs={{0,8},{8,16},{16,24},{24,32},{32,40},{40,48},{48,56},{56,64},{64,7... | collective-permute-start | bytes 786440 | tf_op jit(solution)/shard_map/while/body/eval_jaxpr/ppermute | solution.py:16
  83.5 1.2 slice.64
  86.6 5.5 %collective-permute-start = (bf16[2,512,128]{2,1,0:T(8,128)(2,1)S(1)}, bf16[2,512,128]{2,1,0:T(8,128)(2,1)S(1)}, u32[]{:S(2)}, u32[]{:S(2)}) collective-permute-start(bf16[2,512,128]{2,1,0:T(8,128)(2,1)S(1)} %get-tuple-element.512), channel_id=1, source_target_pairs={{0,8},{8,16},{16,24},{24,32},{32,40},{40,48},{48,56},{56,64},{64,7... | collective-permute-start | bytes 786440 | tf_op jit(solution)/shard_map/while/body/eval_jaxpr/ppermute | solution.py:16
  95.3 5.5 %collective-permute-start = (bf16[2,512,128]{2,1,0:T(8,128)(2,1)S(1)}, bf16[2,512,128]{2,1,0:T(8,128)(2,1)S(1)}, u32[]{:S(2)}, u32[]{:S(2)}) collective-permute-start(bf16[2,512,128]{2,1,0:T(8,128)(2,1)S(1)} %get-tuple-element.512), channel_id=1, source_target_pairs={{0,8},{8,16},{16,24},{24,32},{32,40},{40,48},{48,56},{56,64},{64,7... | collective-permute-start | bytes 786440 | tf_op jit(solution)/shard_map/while/body/eval_jaxpr/ppermute | solution.py:16
  100.8 1.2 slice.64
  103.9 5.5 %collective-permute-start = (bf16[2,512,128]{2,1,0:T(8,128)(2,1)S(1)}, bf16[2,512,128]{2,1,0:T(8,128)(2,1)S(1)}, u32[]{:S(2)}, u32[]{:S(2)}) collective-permute-start(bf16[2,512,128]{2,1,0:T(8,128)(2,1)S(1)} %get-tuple-element.512), channel_id=1, source_target_pairs={{0,8},{8,16},{16,24},{24,32},{32,40},{40,48},{48,56},{56,64},{64,7... | collective-permute-start | bytes 786440 | tf_op jit(solution)/shard_map/while/body/eval_jaxpr/ppermute | solution.py:16
  109.4 1.2 slice.64
  112.5 5.5 %collective-permute-start = (bf16[2,512,128]{2,1,0:T(8,128)(2,1)S(1)}, bf16[2,512,128]{2,1,0:T(8,128)(2,1)S(1)}, u32[]{:S(2)}, u32[]{:S(2)}) collective-permute-start(bf16[2,512,128]{2,1,0:T(8,128)(2,1)S(1)} %get-tuple-element.512), channel_id=1, source_target_pairs={{0,8},{8,16},{16,24},{24,32},{32,40},{40,48},{48,56},{56,64},{64,7... | collective-permute-start | bytes 786440 | tf_op jit(solution)/shard_map/while/body/eval_jaxpr/ppermute | solution.py:16
  118.0 1.2 slice.64
  121.2 5.5 %collective-permute-start = (bf16[2,512,128]{2,1,0:T(8,128)(2,1)S(1)}, bf16[2,512,128]{2,1,0:T(8,128)(2,1)S(1)}, u32[]{:S(2)}, u32[]{:S(2)}) collective-permute-start(bf16[2,512,128]{2,1,0:T(8,128)(2,1)S(1)} %get-tuple-element.512), channel_id=1, source_target_pairs={{0,8},{8,16},{16,24},{24,32},{32,40},{40,48},{48,56},{56,64},{64,7... | collective-permute-start | bytes 786440 | tf_op jit(solution)/shard_map/while/body/eval_jaxpr/ppermute | solution.py:16
  126.6 1.2 slice.64
  129.8 5.5 %collective-permute-start = (bf16[2,512,128]{2,1,0:T(8,128)(2,1)S(1)}, bf16[2,512,128]{2,1,0:T(8,128)(2,1)S(1)}, u32[]{:S(2)}, u32[]{:S(2)}) collective-permute-start(bf16[2,512,128]{2,1,0:T(8,128)(2,1)S(1)} %get-tuple-element.512), channel_id=1, source_target_pairs={{0,8},{8,16},{16,24},{24,32},{32,40},{40,48},{48,56},{56,64},{64,7... | collective-permute-start | bytes 786440 | tf_op jit(solution)/shard_map/while/body/eval_jaxpr/ppermute | solution.py:16
  138.4 5.5 %collective-permute-start = (bf16[2,512,128]{2,1,0:T(8,128)(2,1)S(1)}, bf16[2,512,128]{2,1,0:T(8,128)(2,1)S(1)}, u32[]{:S(2)}, u32[]{:S(2)}) collective-permute-start(bf16[2,512,128]{2,1,0:T(8,128)(2,1)S(1)} %get-tuple-element.512), channel_id=1, source_target_pairs={{0,8},{8,16},{16,24},{24,32},{32,40},{40,48},{48,56},{56,64},{64,7... | collective-permute-start | bytes 786440 | tf_op jit(solution)/shard_map/while/body/eval_jaxpr/ppermute | solution.py:16
  147.0 5.5 %collective-permute-start = (bf16[2,512,128]{2,1,0:T(8,128)(2,1)S(1)}, bf16[2,512,128]{2,1,0:T(8,128)(2,1)S(1)}, u32[]{:S(2)}, u32[]{:S(2)}) collective-permute-start(bf16[2,512,128]{2,1,0:T(8,128)(2,1)S(1)} %get-tuple-element.512), channel_id=1, source_target_pairs={{0,8},{8,16},{16,24},{24,32},{32,40},{40,48},{48,56},{56,64},{64,7... | collective-permute-start | bytes 786440 | tf_op jit(solution)/shard_map/while/body/eval_jaxpr/ppermute | solution.py:16
  155.7 5.5 %collective-permute-start = (bf16[2,512,128]{2,1,0:T(8,128)(2,1)S(1)}, bf16[2,512,128]{2,1,0:T(8,128)(2,1)S(1)}, u32[]{:S(2)}, u32[]{:S(2)}) collective-permute-start(bf16[2,512,128]{2,1,0:T(8,128)(2,1)S(1)} %get-tuple-element.512), channel_id=1, source_target_pairs={{0,8},{8,16},{16,24},{24,32},{32,40},{40,48},{48,56},{56,64},{64,7... | collective-permute-start | bytes 786440 | tf_op jit(solution)/shard_map/while/body/eval_jaxpr/ppermute | solution.py:16
  164.3 5.5 %collective-permute-start = (bf16[2,512,128]{2,1,0:T(8,128)(2,1)S(1)}, bf16[2,512,128]{2,1,0:T(8,128)(2,1)S(1)}, u32[]{:S(2)}, u32[]{:S(2)}) collective-permute-start(bf16[2,512,128]{2,1,0:T(8,128)(2,1)S(1)} %get-tuple-element.512), channel_id=1, source_target_pairs={{0,8},{8,16},{16,24},{24,32},{32,40},{40,48},{48,56},{56,64},{64,7... | collective-permute-start | bytes 786440 | tf_op jit(solution)/shard_map/while/body/eval_jaxpr/ppermute | solution.py:16
  172.9 5.5 %collective-permute-start = (bf16[2,512,128]{2,1,0:T(8,128)(2,1)S(1)}, bf16[2,512,128]{2,1,0:T(8,128)(2,1)S(1)}, u32[]{:S(2)}, u32[]{:S(2)}) collective-permute-start(bf16[2,512,128]{2,1,0:T(8,128)(2,1)S(1)} %get-tuple-element.512), channel_id=1, source_target_pairs={{0,8},{8,16},{16,24},{24,32},{32,40},{40,48},{48,56},{56,64},{64,7... | collective-permute-start | bytes 786440 | tf_op jit(solution)/shard_map/while/body/eval_jaxpr/ppermute | solution.py:16
  181.6 5.5 %collective-permute-start = (bf16[2,512,128]{2,1,0:T(8,128)(2,1)S(1)}, bf16[2,512,128]{2,1,0:T(8,128)(2,1)S(1)}, u32[]{:S(2)}, u32[]{:S(2)}) collective-permute-start(bf16[2,512,128]{2,1,0:T(8,128)(2,1)S(1)} %get-tuple-element.512), channel_id=1, source_target_pairs={{0,8},{8,16},{16,24},{24,32},{32,40},{40,48},{48,56},{56,64},{64,7... | collective-permute-start | bytes 786440 | tf_op jit(solution)/shard_map/while/body/eval_jaxpr/ppermute | solution.py:16
  190.2 5.5 %collective-permute-start = (bf16[2,512,128]{2,1,0:T(8,128)(2,1)S(1)}, bf16[2,512,128]{2,1,0:T(8,128)(2,1)S(1)}, u32[]{:S(2)}, u32[]{:S(2)}) collective-permute-start(bf16[2,512,128]{2,1,0:T(8,128)(2,1)S(1)} %get-tuple-element.512), channel_id=1, source_target_pairs={{0,8},{8,16},{16,24},{24,32},{32,40},{40,48},{48,56},{56,64},{64,7... | collective-permute-start | bytes 786440 | tf_op jit(solution)/shard_map/while/body/eval_jaxpr/ppermute | solution.py:16
  198.8 5.5 %collective-permute-start = (bf16[2,512,128]{2,1,0:T(8,128)(2,1)S(1)}, bf16[2,512,128]{2,1,0:T(8,128)(2,1)S(1)}, u32[]{:S(2)}, u32[]{:S(2)}) collective-permute-start(bf16[2,512,128]{2,1,0:T(8,128)(2,1)S(1)} %get-tuple-element.512), channel_id=1, source_target_pairs={{0,8},{8,16},{16,24},{24,32},{32,40},{40,48},{48,56},{56,64},{64,7... | collective-permute-start | bytes 786440 | tf_op jit(solution)/shard_map/while/body/eval_jaxpr/ppermute | solution.py:16
  207.5 5.5 %collective-permute-start = (bf16[2,512,128]{2,1,0:T(8,128)(2,1)S(1)}, bf16[2,512,128]{2,1,0:T(8,128)(2,1)S(1)}, u32[]{:S(2)}, u32[]{:S(2)}) collective-permute-start(bf16[2,512,128]{2,1,0:T(8,128)(2,1)S(1)} %get-tuple-element.512), channel_id=1, source_target_pairs={{0,8},{8,16},{16,24},{24,32},{32,40},{40,48},{48,56},{56,64},{64,7... | collective-permute-start | bytes 786440 | tf_op jit(solution)/shard_map/while/body/eval_jaxpr/ppermute | solution.py:16
  216.1 5.5 %collective-permute-start = (bf16[2,512,128]{2,1,0:T(8,128)(2,1)S(1)}, bf16[2,512,128]{2,1,0:T(8,128)(2,1)S(1)}, u32[]{:S(2)}, u32[]{:S(2)}) collective-permute-start(bf16[2,512,128]{2,1,0:T(8,128)(2,1)S(1)} %get-tuple-element.512), channel_id=1, source_target_pairs={{0,8},{8,16},{16,24},{24,32},{32,40},{40,48},{48,56},{56,64},{64,7... | collective-permute-start | bytes 786440 | tf_op jit(solution)/shard_map/while/body/eval_jaxpr/ppermute | solution.py:16
  224.7 5.5 %collective-permute-start = (bf16[2,512,128]{2,1,0:T(8,128)(2,1)S(1)}, bf16[2,512,128]{2,1,0:T(8,128)(2,1)S(1)}, u32[]{:S(2)}, u32[]{:S(2)}) collective-permute-start(bf16[2,512,128]{2,1,0:T(8,128)(2,1)S(1)} %get-tuple-element.512), channel_id=1, source_target_pairs={{0,8},{8,16},{16,24},{24,32},{32,40},{40,48},{48,56},{56,64},{64,7... | collective-permute-start | bytes 786440 | tf_op jit(solution)/shard_map/while/body/eval_jaxpr/ppermute | solution.py:16
  233.4 5.5 %collective-permute-start = (bf16[2,512,128]{2,1,0:T(8,128)(2,1)S(1)}, bf16[2,512,128]{2,1,0:T(8,128)(2,1)S(1)}, u32[]{:S(2)}, u32[]{:S(2)}) collective-permute-start(bf16[2,512,128]{2,1,0:T(8,128)(2,1)S(1)} %get-tuple-element.512), channel_id=1, source_target_pairs={{0,8},{8,16},{16,24},{24,32},{32,40},{40,48},{48,56},{56,64},{64,7... | collective-permute-start | bytes 786440 | tf_op jit(solution)/shard_map/while/body/eval_jaxpr/ppermute | solution.py:16
  242.0 5.5 %collective-permute-start = (bf16[2,512,128]{2,1,0:T(8,128)(2,1)S(1)}, bf16[2,512,128]{2,1,0:T(8,128)(2,1)S(1)}, u32[]{:S(2)}, u32[]{:S(2)}) collective-permute-start(bf16[2,512,128]{2,1,0:T(8,128)(2,1)S(1)} %get-tuple-element.512), channel_id=1, source_target_pairs={{0,8},{8,16},{16,24},{24,32},{32,40},{40,48},{48,56},{56,64},{64,7... | collective-permute-start | bytes 786440 | tf_op jit(solution)/shard_map/while/body/eval_jaxpr/ppermute | solution.py:16
  250.6 5.5 %collective-permute-start = (bf16[2,512,128]{2,1,0:T(8,128)(2,1)S(1)}, bf16[2,512,128]{2,1,0:T(8,128)(2,1)S(1)}, u32[]{:S(2)}, u32[]{:S(2)}) collective-permute-start(bf16[2,512,128]{2,1,0:T(8,128)(2,1)S(1)} %get-tuple-element.512), channel_id=1, source_target_pairs={{0,8},{8,16},{16,24},{24,32},{32,40},{40,48},{48,56},{56,64},{64,7... | collective-permute-start | bytes 786440 | tf_op jit(solution)/shard_map/while/body/eval_jaxpr/ppermute | solution.py:16
  259.2 5.5 %collective-permute-start = (bf16[2,512,128]{2,1,0:T(8,128)(2,1)S(1)}, bf16[2,512,128]{2,1,0:T(8,128)(2,1)S(1)}, u32[]{:S(2)}, u32[]{:S(2)}) collective-permute-start(bf16[2,512,128]{2,1,0:T(8,128)(2,1)S(1)} %get-tuple-element.512), channel_id=1, source_target_pairs={{0,8},{8,16},{16,24},{24,32},{32,40},{40,48},{48,56},{56,64},{64,7... | collective-permute-start | bytes 786440 | tf_op jit(solution)/shard_map/while/body/eval_jaxpr/ppermute | solution.py:16
  267.9 5.5 %collective-permute-start = (bf16[2,512,128]{2,1,0:T(8,128)(2,1)S(1)}, bf16[2,512,128]{2,1,0:T(8,128)(2,1)S(1)}, u32[]{:S(2)}, u32[]{:S(2)}) collective-permute-start(bf16[2,512,128]{2,1,0:T(8,128)(2,1)S(1)} %get-tuple-element.512), channel_id=1, source_target_pairs={{0,8},{8,16},{16,24},{24,32},{32,40},{40,48},{48,56},{56,64},{64,7... | collective-permute-start | bytes 786440 | tf_op jit(solution)/shard_map/while/body/eval_jaxpr/ppermute | solution.py:16
  277.0 6.5 %convolution_convert_fusion = bf16[512,4096]{1,0:T(8,128)(2,1)} fusion(bf16[512,512]{0,1:T(8,128)(2,1)S(1)} %bitcast.121, bf16[512,4096]{1,0:T(8,128)(2,1)} %param.15), kind=kOutput, calls=%fused_computation.47 | convolution fusion | flops 2149580800 | bytes 8912896 | tf_op jit(solution)/shard_map/dot_general | solution.py:81
  283.5 139.9 %reduce-scatter.2.cloned.1.call-done = bf16[64,4096]{1,0:T(8,128)(2,1)} async-done(((bf16[512,4096]{1,0:T(8,128)(2,1)}), bf16[64,4096]{1,0:T(8,128)(2,1)}) %reduce-scatter.2.cloned.1.call-update) | async-done | bytes 524304 | tf_op jit(solution)/shard_map/reduce_scatter | solution.py:80
  (191 shorter events, 50.9 us)
Async XLA Ops:
  6.5 416.9 %reduce-scatter.2.cloned.1.call-start = ((), (), s32[]{:S(2)}) async-start(), calls=%async_computation.1 | async-start | bytes 4718592 | tf_op jit(solution)/shard_map/reduce_scatter | solution.py:80
  12.2 2.8 copy-start
  17.7 4.8 %collective-permute-start = (bf16[2,512,128]{2,1,0:T(8,128)(2,1)S(1)}, bf16[2,512,128]{2,1,0:T(8,128)(2,1)S(1)}, u32[]{:S(2)}, u32[]{:S(2)}) collective-permute-start(bf16[2,512,128]{2,1,0:T(8,128)(2,1)S(1)} %get-tuple-element.512), channel_id=1, source_target_pairs={{0,8},{8,16},{16,24},{24,32},{32,40},{40,48},{48,56},{56,64},{64,7... | collective-permute-start | bytes 786440 | tf_op jit(solution)/shard_map/while/body/eval_jaxpr/ppermute | solution.py:16
  22.6 11.9 %collective-permute-start = (bf16[2,512,128]{2,1,0:T(8,128)(2,1)S(1)}, bf16[2,512,128]{2,1,0:T(8,128)(2,1)S(1)}, u32[]{:S(2)}, u32[]{:S(2)}) collective-permute-start(bf16[2,512,128]{2,1,0:T(8,128)(2,1)S(1)} %get-tuple-element.512), channel_id=1, source_target_pairs={{0,8},{8,16},{16,24},{24,32},{32,40},{40,48},{48,56},{56,64},{64,7... | collective-permute-start | bytes 786440 | tf_op jit(solution)/shard_map/while/body/eval_jaxpr/ppermute | solution.py:16
  34.6 5.2 %collective-permute-start = (bf16[2,512,128]{2,1,0:T(8,128)(2,1)S(1)}, bf16[2,512,128]{2,1,0:T(8,128)(2,1)S(1)}, u32[]{:S(2)}, u32[]{:S(2)}) collective-permute-start(bf16[2,512,128]{2,1,0:T(8,128)(2,1)S(1)} %get-tuple-element.512), channel_id=1, source_target_pairs={{0,8},{8,16},{16,24},{24,32},{32,40},{40,48},{48,56},{56,64},{64,7... | collective-permute-start | bytes 786440 | tf_op jit(solution)/shard_map/while/body/eval_jaxpr/ppermute | solution.py:16
  39.9 7.6 %collective-permute-start = (bf16[2,512,128]{2,1,0:T(8,128)(2,1)S(1)}, bf16[2,512,128]{2,1,0:T(8,128)(2,1)S(1)}, u32[]{:S(2)}, u32[]{:S(2)}) collective-permute-start(bf16[2,512,128]{2,1,0:T(8,128)(2,1)S(1)} %get-tuple-element.512), channel_id=1, source_target_pairs={{0,8},{8,16},{16,24},{24,32},{32,40},{40,48},{48,56},{56,64},{64,7... | collective-permute-start | bytes 786440 | tf_op jit(solution)/shard_map/while/body/eval_jaxpr/ppermute | solution.py:16
  47.6 7.6 %collective-permute-start = (bf16[2,512,128]{2,1,0:T(8,128)(2,1)S(1)}, bf16[2,512,128]{2,1,0:T(8,128)(2,1)S(1)}, u32[]{:S(2)}, u32[]{:S(2)}) collective-permute-start(bf16[2,512,128]{2,1,0:T(8,128)(2,1)S(1)} %get-tuple-element.512), channel_id=1, source_target_pairs={{0,8},{8,16},{16,24},{24,32},{32,40},{40,48},{48,56},{56,64},{64,7... | collective-permute-start | bytes 786440 | tf_op jit(solution)/shard_map/while/body/eval_jaxpr/ppermute | solution.py:16
  55.3 7.6 %collective-permute-start = (bf16[2,512,128]{2,1,0:T(8,128)(2,1)S(1)}, bf16[2,512,128]{2,1,0:T(8,128)(2,1)S(1)}, u32[]{:S(2)}, u32[]{:S(2)}) collective-permute-start(bf16[2,512,128]{2,1,0:T(8,128)(2,1)S(1)} %get-tuple-element.512), channel_id=1, source_target_pairs={{0,8},{8,16},{16,24},{24,32},{32,40},{40,48},{48,56},{56,64},{64,7... | collective-permute-start | bytes 786440 | tf_op jit(solution)/shard_map/while/body/eval_jaxpr/ppermute | solution.py:16
  63.1 7.6 %collective-permute-start = (bf16[2,512,128]{2,1,0:T(8,128)(2,1)S(1)}, bf16[2,512,128]{2,1,0:T(8,128)(2,1)S(1)}, u32[]{:S(2)}, u32[]{:S(2)}) collective-permute-start(bf16[2,512,128]{2,1,0:T(8,128)(2,1)S(1)} %get-tuple-element.512), channel_id=1, source_target_pairs={{0,8},{8,16},{16,24},{24,32},{32,40},{40,48},{48,56},{56,64},{64,7... | collective-permute-start | bytes 786440 | tf_op jit(solution)/shard_map/while/body/eval_jaxpr/ppermute | solution.py:16
  70.8 7.6 %collective-permute-start = (bf16[2,512,128]{2,1,0:T(8,128)(2,1)S(1)}, bf16[2,512,128]{2,1,0:T(8,128)(2,1)S(1)}, u32[]{:S(2)}, u32[]{:S(2)}) collective-permute-start(bf16[2,512,128]{2,1,0:T(8,128)(2,1)S(1)} %get-tuple-element.512), channel_id=1, source_target_pairs={{0,8},{8,16},{16,24},{24,32},{32,40},{40,48},{48,56},{56,64},{64,7... | collective-permute-start | bytes 786440 | tf_op jit(solution)/shard_map/while/body/eval_jaxpr/ppermute | solution.py:16
  78.5 8.0 %collective-permute-start = (bf16[2,512,128]{2,1,0:T(8,128)(2,1)S(1)}, bf16[2,512,128]{2,1,0:T(8,128)(2,1)S(1)}, u32[]{:S(2)}, u32[]{:S(2)}) collective-permute-start(bf16[2,512,128]{2,1,0:T(8,128)(2,1)S(1)} %get-tuple-element.512), channel_id=1, source_target_pairs={{0,8},{8,16},{16,24},{24,32},{32,40},{40,48},{48,56},{56,64},{64,7... | collective-permute-start | bytes 786440 | tf_op jit(solution)/shard_map/while/body/eval_jaxpr/ppermute | solution.py:16
  86.6 8.5 %collective-permute-start = (bf16[2,512,128]{2,1,0:T(8,128)(2,1)S(1)}, bf16[2,512,128]{2,1,0:T(8,128)(2,1)S(1)}, u32[]{:S(2)}, u32[]{:S(2)}) collective-permute-start(bf16[2,512,128]{2,1,0:T(8,128)(2,1)S(1)} %get-tuple-element.512), channel_id=1, source_target_pairs={{0,8},{8,16},{16,24},{24,32},{32,40},{40,48},{48,56},{56,64},{64,7... | collective-permute-start | bytes 786440 | tf_op jit(solution)/shard_map/while/body/eval_jaxpr/ppermute | solution.py:16
  95.3 8.5 %collective-permute-start = (bf16[2,512,128]{2,1,0:T(8,128)(2,1)S(1)}, bf16[2,512,128]{2,1,0:T(8,128)(2,1)S(1)}, u32[]{:S(2)}, u32[]{:S(2)}) collective-permute-start(bf16[2,512,128]{2,1,0:T(8,128)(2,1)S(1)} %get-tuple-element.512), channel_id=1, source_target_pairs={{0,8},{8,16},{16,24},{24,32},{32,40},{40,48},{48,56},{56,64},{64,7... | collective-permute-start | bytes 786440 | tf_op jit(solution)/shard_map/while/body/eval_jaxpr/ppermute | solution.py:16
  103.9 8.5 %collective-permute-start = (bf16[2,512,128]{2,1,0:T(8,128)(2,1)S(1)}, bf16[2,512,128]{2,1,0:T(8,128)(2,1)S(1)}, u32[]{:S(2)}, u32[]{:S(2)}) collective-permute-start(bf16[2,512,128]{2,1,0:T(8,128)(2,1)S(1)} %get-tuple-element.512), channel_id=1, source_target_pairs={{0,8},{8,16},{16,24},{24,32},{32,40},{40,48},{48,56},{56,64},{64,7... | collective-permute-start | bytes 786440 | tf_op jit(solution)/shard_map/while/body/eval_jaxpr/ppermute | solution.py:16
  112.5 8.5 %collective-permute-start = (bf16[2,512,128]{2,1,0:T(8,128)(2,1)S(1)}, bf16[2,512,128]{2,1,0:T(8,128)(2,1)S(1)}, u32[]{:S(2)}, u32[]{:S(2)}) collective-permute-start(bf16[2,512,128]{2,1,0:T(8,128)(2,1)S(1)} %get-tuple-element.512), channel_id=1, source_target_pairs={{0,8},{8,16},{16,24},{24,32},{32,40},{40,48},{48,56},{56,64},{64,7... | collective-permute-start | bytes 786440 | tf_op jit(solution)/shard_map/while/body/eval_jaxpr/ppermute | solution.py:16
  121.2 8.5 %collective-permute-start = (bf16[2,512,128]{2,1,0:T(8,128)(2,1)S(1)}, bf16[2,512,128]{2,1,0:T(8,128)(2,1)S(1)}, u32[]{:S(2)}, u32[]{:S(2)}) collective-permute-start(bf16[2,512,128]{2,1,0:T(8,128)(2,1)S(1)} %get-tuple-element.512), channel_id=1, source_target_pairs={{0,8},{8,16},{16,24},{24,32},{32,40},{40,48},{48,56},{56,64},{64,7... | collective-permute-start | bytes 786440 | tf_op jit(solution)/shard_map/while/body/eval_jaxpr/ppermute | solution.py:16
  129.8 8.5 %collective-permute-start = (bf16[2,512,128]{2,1,0:T(8,128)(2,1)S(1)}, bf16[2,512,128]{2,1,0:T(8,128)(2,1)S(1)}, u32[]{:S(2)}, u32[]{:S(2)}) collective-permute-start(bf16[2,512,128]{2,1,0:T(8,128)(2,1)S(1)} %get-tuple-element.512), channel_id=1, source_target_pairs={{0,8},{8,16},{16,24},{24,32},{32,40},{40,48},{48,56},{56,64},{64,7... | collective-permute-start | bytes 786440 | tf_op jit(solution)/shard_map/while/body/eval_jaxpr/ppermute | solution.py:16
  138.4 8.5 %collective-permute-start = (bf16[2,512,128]{2,1,0:T(8,128)(2,1)S(1)}, bf16[2,512,128]{2,1,0:T(8,128)(2,1)S(1)}, u32[]{:S(2)}, u32[]{:S(2)}) collective-permute-start(bf16[2,512,128]{2,1,0:T(8,128)(2,1)S(1)} %get-tuple-element.512), channel_id=1, source_target_pairs={{0,8},{8,16},{16,24},{24,32},{32,40},{40,48},{48,56},{56,64},{64,7... | collective-permute-start | bytes 786440 | tf_op jit(solution)/shard_map/while/body/eval_jaxpr/ppermute | solution.py:16
  147.0 8.5 %collective-permute-start = (bf16[2,512,128]{2,1,0:T(8,128)(2,1)S(1)}, bf16[2,512,128]{2,1,0:T(8,128)(2,1)S(1)}, u32[]{:S(2)}, u32[]{:S(2)}) collective-permute-start(bf16[2,512,128]{2,1,0:T(8,128)(2,1)S(1)} %get-tuple-element.512), channel_id=1, source_target_pairs={{0,8},{8,16},{16,24},{24,32},{32,40},{40,48},{48,56},{56,64},{64,7... | collective-permute-start | bytes 786440 | tf_op jit(solution)/shard_map/while/body/eval_jaxpr/ppermute | solution.py:16
  155.7 8.5 %collective-permute-start = (bf16[2,512,128]{2,1,0:T(8,128)(2,1)S(1)}, bf16[2,512,128]{2,1,0:T(8,128)(2,1)S(1)}, u32[]{:S(2)}, u32[]{:S(2)}) collective-permute-start(bf16[2,512,128]{2,1,0:T(8,128)(2,1)S(1)} %get-tuple-element.512), channel_id=1, source_target_pairs={{0,8},{8,16},{16,24},{24,32},{32,40},{40,48},{48,56},{56,64},{64,7... | collective-permute-start | bytes 786440 | tf_op jit(solution)/shard_map/while/body/eval_jaxpr/ppermute | solution.py:16
  164.3 8.5 %collective-permute-start = (bf16[2,512,128]{2,1,0:T(8,128)(2,1)S(1)}, bf16[2,512,128]{2,1,0:T(8,128)(2,1)S(1)}, u32[]{:S(2)}, u32[]{:S(2)}) collective-permute-start(bf16[2,512,128]{2,1,0:T(8,128)(2,1)S(1)} %get-tuple-element.512), channel_id=1, source_target_pairs={{0,8},{8,16},{16,24},{24,32},{32,40},{40,48},{48,56},{56,64},{64,7... | collective-permute-start | bytes 786440 | tf_op jit(solution)/shard_map/while/body/eval_jaxpr/ppermute | solution.py:16
  172.9 8.5 %collective-permute-start = (bf16[2,512,128]{2,1,0:T(8,128)(2,1)S(1)}, bf16[2,512,128]{2,1,0:T(8,128)(2,1)S(1)}, u32[]{:S(2)}, u32[]{:S(2)}) collective-permute-start(bf16[2,512,128]{2,1,0:T(8,128)(2,1)S(1)} %get-tuple-element.512), channel_id=1, source_target_pairs={{0,8},{8,16},{16,24},{24,32},{32,40},{40,48},{48,56},{56,64},{64,7... | collective-permute-start | bytes 786440 | tf_op jit(solution)/shard_map/while/body/eval_jaxpr/ppermute | solution.py:16
  181.6 8.5 %collective-permute-start = (bf16[2,512,128]{2,1,0:T(8,128)(2,1)S(1)}, bf16[2,512,128]{2,1,0:T(8,128)(2,1)S(1)}, u32[]{:S(2)}, u32[]{:S(2)}) collective-permute-start(bf16[2,512,128]{2,1,0:T(8,128)(2,1)S(1)} %get-tuple-element.512), channel_id=1, source_target_pairs={{0,8},{8,16},{16,24},{24,32},{32,40},{40,48},{48,56},{56,64},{64,7... | collective-permute-start | bytes 786440 | tf_op jit(solution)/shard_map/while/body/eval_jaxpr/ppermute | solution.py:16
  190.2 8.5 %collective-permute-start = (bf16[2,512,128]{2,1,0:T(8,128)(2,1)S(1)}, bf16[2,512,128]{2,1,0:T(8,128)(2,1)S(1)}, u32[]{:S(2)}, u32[]{:S(2)}) collective-permute-start(bf16[2,512,128]{2,1,0:T(8,128)(2,1)S(1)} %get-tuple-element.512), channel_id=1, source_target_pairs={{0,8},{8,16},{16,24},{24,32},{32,40},{40,48},{48,56},{56,64},{64,7... | collective-permute-start | bytes 786440 | tf_op jit(solution)/shard_map/while/body/eval_jaxpr/ppermute | solution.py:16
  198.8 8.5 %collective-permute-start = (bf16[2,512,128]{2,1,0:T(8,128)(2,1)S(1)}, bf16[2,512,128]{2,1,0:T(8,128)(2,1)S(1)}, u32[]{:S(2)}, u32[]{:S(2)}) collective-permute-start(bf16[2,512,128]{2,1,0:T(8,128)(2,1)S(1)} %get-tuple-element.512), channel_id=1, source_target_pairs={{0,8},{8,16},{16,24},{24,32},{32,40},{40,48},{48,56},{56,64},{64,7... | collective-permute-start | bytes 786440 | tf_op jit(solution)/shard_map/while/body/eval_jaxpr/ppermute | solution.py:16
  207.5 8.5 %collective-permute-start = (bf16[2,512,128]{2,1,0:T(8,128)(2,1)S(1)}, bf16[2,512,128]{2,1,0:T(8,128)(2,1)S(1)}, u32[]{:S(2)}, u32[]{:S(2)}) collective-permute-start(bf16[2,512,128]{2,1,0:T(8,128)(2,1)S(1)} %get-tuple-element.512), channel_id=1, source_target_pairs={{0,8},{8,16},{16,24},{24,32},{32,40},{40,48},{48,56},{56,64},{64,7... | collective-permute-start | bytes 786440 | tf_op jit(solution)/shard_map/while/body/eval_jaxpr/ppermute | solution.py:16
  216.1 8.5 %collective-permute-start = (bf16[2,512,128]{2,1,0:T(8,128)(2,1)S(1)}, bf16[2,512,128]{2,1,0:T(8,128)(2,1)S(1)}, u32[]{:S(2)}, u32[]{:S(2)}) collective-permute-start(bf16[2,512,128]{2,1,0:T(8,128)(2,1)S(1)} %get-tuple-element.512), channel_id=1, source_target_pairs={{0,8},{8,16},{16,24},{24,32},{32,40},{40,48},{48,56},{56,64},{64,7... | collective-permute-start | bytes 786440 | tf_op jit(solution)/shard_map/while/body/eval_jaxpr/ppermute | solution.py:16
  224.7 8.5 %collective-permute-start = (bf16[2,512,128]{2,1,0:T(8,128)(2,1)S(1)}, bf16[2,512,128]{2,1,0:T(8,128)(2,1)S(1)}, u32[]{:S(2)}, u32[]{:S(2)}) collective-permute-start(bf16[2,512,128]{2,1,0:T(8,128)(2,1)S(1)} %get-tuple-element.512), channel_id=1, source_target_pairs={{0,8},{8,16},{16,24},{24,32},{32,40},{40,48},{48,56},{56,64},{64,7... | collective-permute-start | bytes 786440 | tf_op jit(solution)/shard_map/while/body/eval_jaxpr/ppermute | solution.py:16
  233.4 8.5 %collective-permute-start = (bf16[2,512,128]{2,1,0:T(8,128)(2,1)S(1)}, bf16[2,512,128]{2,1,0:T(8,128)(2,1)S(1)}, u32[]{:S(2)}, u32[]{:S(2)}) collective-permute-start(bf16[2,512,128]{2,1,0:T(8,128)(2,1)S(1)} %get-tuple-element.512), channel_id=1, source_target_pairs={{0,8},{8,16},{16,24},{24,32},{32,40},{40,48},{48,56},{56,64},{64,7... | collective-permute-start | bytes 786440 | tf_op jit(solution)/shard_map/while/body/eval_jaxpr/ppermute | solution.py:16
  242.0 8.5 %collective-permute-start = (bf16[2,512,128]{2,1,0:T(8,128)(2,1)S(1)}, bf16[2,512,128]{2,1,0:T(8,128)(2,1)S(1)}, u32[]{:S(2)}, u32[]{:S(2)}) collective-permute-start(bf16[2,512,128]{2,1,0:T(8,128)(2,1)S(1)} %get-tuple-element.512), channel_id=1, source_target_pairs={{0,8},{8,16},{16,24},{24,32},{32,40},{40,48},{48,56},{56,64},{64,7... | collective-permute-start | bytes 786440 | tf_op jit(solution)/shard_map/while/body/eval_jaxpr/ppermute | solution.py:16
  250.6 8.5 %collective-permute-start = (bf16[2,512,128]{2,1,0:T(8,128)(2,1)S(1)}, bf16[2,512,128]{2,1,0:T(8,128)(2,1)S(1)}, u32[]{:S(2)}, u32[]{:S(2)}) collective-permute-start(bf16[2,512,128]{2,1,0:T(8,128)(2,1)S(1)} %get-tuple-element.512), channel_id=1, source_target_pairs={{0,8},{8,16},{16,24},{24,32},{32,40},{40,48},{48,56},{56,64},{64,7... | collective-permute-start | bytes 786440 | tf_op jit(solution)/shard_map/while/body/eval_jaxpr/ppermute | solution.py:16
  259.2 8.5 %collective-permute-start = (bf16[2,512,128]{2,1,0:T(8,128)(2,1)S(1)}, bf16[2,512,128]{2,1,0:T(8,128)(2,1)S(1)}, u32[]{:S(2)}, u32[]{:S(2)}) collective-permute-start(bf16[2,512,128]{2,1,0:T(8,128)(2,1)S(1)} %get-tuple-element.512), channel_id=1, source_target_pairs={{0,8},{8,16},{16,24},{24,32},{32,40},{40,48},{48,56},{56,64},{64,7... | collective-permute-start | bytes 786440 | tf_op jit(solution)/shard_map/while/body/eval_jaxpr/ppermute | solution.py:16
  267.9 8.5 %collective-permute-start = (bf16[2,512,128]{2,1,0:T(8,128)(2,1)S(1)}, bf16[2,512,128]{2,1,0:T(8,128)(2,1)S(1)}, u32[]{:S(2)}, u32[]{:S(2)}) collective-permute-start(bf16[2,512,128]{2,1,0:T(8,128)(2,1)S(1)} %get-tuple-element.512), channel_id=1, source_target_pairs={{0,8},{8,16},{16,24},{24,32},{32,40},{40,48},{48,56},{56,64},{64,7... | collective-permute-start | bytes 786440 | tf_op jit(solution)/shard_map/while/body/eval_jaxpr/ppermute | solution.py:16
Sparse Core Ops, SparseCore 0:
  283.6 139.7 reduce-scatter.1
where the time goes:
time: 433 us; the launch traced here: 430 us
  starting transfers between devices  161 us (37%)
  waiting for transfers between devices  140 us (32%)
  local copies, waits for them, and re-layouts  60.6 us (14%)
  loops' own time  40.8 us (9%)
  between operations  14.7 us (3%)
  matrix products  9.9 us (2%)
    ppermute x31, starting transfers between devices, shifted(): lax.ppermute(value, axis, [(source, source + steps) for source in range(l...  161 us
    reduce_scatter x1, waiting for transfers between devices, on_device(): lax.psum_scatter(jnp.dot(attended, out_weight, preferred_element_type=jnp...  140 us
    another operation x1, loops' own time, on_device(): state, unused = lax.fori_loop(1, cycle_size, whole_turn, (state, stacked))  40.2 us
    slice x32, local copies, waits for them, and re-layouts, attend_block(): doc_rows[0]  39.2 us
    slice x32, local copies, waits for them, and re-layouts, attend_block(): query_pos[-1]  18.9 us
  transfers between devices with their start and end apart: 32, of which 1 were waited for; matrix products, arithmetic and copies ran while one was open for 13% of the time, Pallas kernels for 0%

commit v1 on v0

v1 whole, which is shorter than its diff:
```python
import jax
import jax.numpy as jnp
from jax import lax
from jax.experimental import pallas as pl
from jax.experimental.pallas import tpu as pltpu
from jax.sharding import PartitionSpec as P


HD = 128
GROUP = 4
NX = 4
NHEAD = 8
CHUNKS = 2
NEG = -1.0e30
SCALE2 = HD ** -0.5 * 1.4426950408889634
F32 = jnp.float32
BF16 = jnp.bfloat16


VMEM = pl.BlockSpec(memory_space=pltpu.VMEM)
SMEM = pl.BlockSpec(memory_space=pltpu.SMEM)
PARAMS = pltpu.CompilerParams(vmem_limit_bytes=56 << 20)


def x_ring(d):
    return [(h, (h // 2 + d) % NX * 2 + h % 2) for h in range(NHEAD)]


def visit(q_ref, k, v, ok, m_sc, acc_sc, first):
    rows = q_ref.shape[0]
    v = jnp.concatenate([v, jnp.ones_like(v)], axis=1)
    scores = [
        lax.dot_general(
            q_ref[:, g * HD:(g + 1) * HD], k, (((1,), (1,)), ((), ())), preferred_element_type=F32
        )
        for g in range(GROUP)
    ]
    for g, s in enumerate(scores):
        if ok is not None:
            s = jnp.where(ok, s, NEG)
        top = jnp.max(s, axis=1, keepdims=True)
        if first:
            m_new = jnp.broadcast_to(top, (rows, HD))
        else:
            m_old = m_sc[g]
            m_new = jnp.maximum(m_old, top)
        base = m_new * SCALE2
        p = jnp.exp2(s * SCALE2 - jnp.tile(base, (1, s.shape[1] // HD)))
        pv = jnp.dot(p.astype(BF16), v, preferred_element_type=F32)
        if first:
            acc_sc[g] = pv
        else:
            factor = jnp.exp2(m_old * SCALE2 - base)
            acc_sc[g] = acc_sc[g] * jnp.tile(factor, (1, 2)) + pv
        m_sc[g] = m_new


def own_kernel(info, q_ref, doc_ref, own, partner, m_ref, acc_ref):
    rows = q_ref.shape[0]
    r = lax.broadcasted_iota(jnp.int32, (rows, rows), 0)
    c = lax.broadcasted_iota(jnp.int32, (rows, rows), 1)
    doc = doc_ref[...] - info[0]
    visit(q_ref, own[0], own[1], (c >= doc) & (c <= r), m_ref, acc_ref, True)

    @pl.when(info[1] == 1)
    def _():
        visit(q_ref, partner[0], partner[1], c - rows >= doc, m_ref, acc_ref, False)


def rest_kernel(info, q_ref, m_in, acc_in, *refs):
    blocks, (o0, o1, m_sc, acc_sc) = refs[:6], refs[6:]
    m_sc[...] = m_in[...]
    acc_sc[...] = acc_in[...]
    for i in range(3):
        a, b = blocks[2 * i:2 * i + 2]

        @pl.when(info[i] == 1)
        def _(a=a, b=b):
            k = jnp.concatenate([a[0], b[0]], axis=0)
            v = jnp.concatenate([a[1], b[1]], axis=0)
            visit(q_ref, k, v, None, m_sc, acc_sc, False)

    for g in range(GROUP):
        acc = acc_sc[g]
        out = (acc[:, :HD] / acc[:, HD:]).astype(BF16)
        out = out.reshape(NHEAD, CHUNKS, -1, HD)
        o0[:, :, g * HD:(g + 1) * HD] = out[:, 0]
        o1[:, :, g * HD:(g + 1) * HD] = out[:, 1]


def project_kernel(info, a0, a1, a2, a3, w_own, w_mine, w_other, o_ref):
    core = info[0]
    depth = w_mine.shape[1]
    left = a0[...].reshape(-1, a0.shape[2])
    total = jnp.dot(left, w_own[...], preferred_element_type=F32)
    for d, a in enumerate((a1, a2, a3)):
        for half, w in ((core, w_mine), (1 - core, w_other)):
            cols = pl.ds(pl.multiple_of(half * depth, depth), depth)
            left = a[:, :, cols].reshape(-1, depth)
            total = total + jnp.dot(left, w[d], preferred_element_type=F32)
    o_ref[...] = total.reshape(o_ref.shape).astype(o_ref.dtype)


def project(info, attended, w_own, w_mine, w_other):
    heads, rows, _ = attended[0].shape
    width = w_own.shape[1]
    step = width // 4
    return pl.pallas_call(
        project_kernel,
        grid=(width // step,),
        out_shape=jax.ShapeDtypeStruct((heads, rows, width), BF16),
        in_specs=[SMEM] + [VMEM] * NX + [
            pl.BlockSpec((w_own.shape[0], step), lambda n: (0, n)),
            pl.BlockSpec((NX - 1, w_mine.shape[1], step), lambda n: (0, 0, n)),
            pl.BlockSpec((NX - 1, w_mine.shape[1], step), lambda n: (0, 0, n)),
        ],
        out_specs=pl.BlockSpec((heads, rows, step), lambda n: (0, 0, n)),
        compiler_params=PARAMS,
        cost_estimate=pl.CostEstimate(flops=2 * heads * rows * 2048 * width, transcendentals=0, bytes_accessed=6 << 20),
    )(info, *attended, w_own, w_mine, w_other)


def finish_kernel(r0, r1, o_ref):
    _, rows, width = r0.shape
    for k, r in enumerate((r0, r1)):
        for x in range(NX):
            both = r[2 * x].astype(F32) + r[2 * x + 1].astype(F32)
            o_ref[k * rows:(k + 1) * rows, x * width:(x + 1) * width] = both.astype(BF16)


def on_device(queries, keys, values, doc_start, out_weight):
    rows = queries.shape[0]
    ctx = lax.axis_index("ctx")
    head = lax.axis_index("head")
    n_ctx = lax.axis_size("ctx")
    core, cell = ctx % 2, ctx // 2
    odd = cell % 2
    x = head // 2
    swap = [(c, c ^ 1) for c in range(n_ctx)]
    own = jnp.stack([keys, values])

    near = lax.ppermute(own, "ctx", [(c, c + 4) for c in range(n_ctx - 4)])
    far = lax.ppermute(
        own, "ctx",
        [(c, c + (6 if c // 2 % 2 else 2)) for c in range(n_ctx) if c + (6 if c // 2 % 2 else 2) < n_ctx],
    )
    partner = lax.ppermute(own, "ctx", swap)

    state = (
        jax.ShapeDtypeStruct((GROUP, rows, HD), F32),
        jax.ShapeDtypeStruct((GROUP, rows, 2 * HD), F32),
    )
    info = jnp.stack([ctx * rows, core]).astype(jnp.int32)
    m, acc = pl.pallas_call(
        own_kernel,
        out_shape=state,
        in_specs=[SMEM] + [VMEM] * 4,
        out_specs=[VMEM] * 2,
        compiler_params=PARAMS,
        cost_estimate=pl.CostEstimate(flops=1 << 30, transcendentals=2 << 20, bytes_accessed=4 << 20),
    )(info, queries, doc_start[:, None], own, partner)

    weight = lax.optimization_barrier((out_weight, partner))[0]
    width = weight.shape[1] // NX
    depth = weight.shape[0] // 2
    half = lax.dynamic_slice_in_dim(weight, core * depth, depth, 0)
    w_mine = [
        lax.ppermute(lax.dynamic_slice_in_dim(half, (x + d) % NX * width, width, 1), "head", x_ring(d))
        for d in range(1, NX)
    ]

    cross = lax.ppermute(near, "ctx", [(c, c ^ 2) for c in range(n_ctx)])
    far_o, near_o, cross_o = (lax.ppermute(t, "ctx", swap) for t in (far, near, cross))
    cells = jnp.stack([
        jnp.where(odd == 1, cell - 1, cell - 3), cell - 2, jnp.where(odd == 1, cell - 3, cell - 1)
    ])
    seen = ((cells >= 0) & (cells * 2 * rows >= doc_start[0])).astype(jnp.int32)
    chunk = jax.ShapeDtypeStruct((NHEAD, rows // NHEAD // CHUNKS, GROUP * HD), BF16)
    chunks = pl.pallas_call(
        rest_kernel,
        out_shape=[chunk] * CHUNKS,
        in_specs=[SMEM] + [VMEM] * 9,
        out_specs=[VMEM] * CHUNKS,
        scratch_shapes=[pltpu.VMEM(t.shape, t.dtype) for t in state],
        compiler_params=PARAMS,
        cost_estimate=pl.CostEstimate(flops=4 << 30, transcendentals=6 << 20, bytes_accessed=6 << 20),
    )(seen, queries, m, acc, far, far_o, near, near_o, cross, cross_o)

    gathered = [[a] + [lax.ppermute(a, "head", x_ring(d)) for d in (1, 3, 2)] for a in chunks]
    gathered = [[g[0], g[1], g[3], g[2]] for g in gathered]
    w_mine = jnp.stack(lax.optimization_barrier((*w_mine, chunks[0]))[:3])
    w_other = lax.ppermute(w_mine, "ctx", swap)
    w_own = lax.dynamic_slice_in_dim(weight, x * width, width, 1)
    received = [lax.all_to_all(project(core[None], g, w_own, w_mine, w_other), "head", 0, 0) for g in gathered]
    return pl.pallas_call(
        finish_kernel,
        out_shape=jax.ShapeDtypeStruct((rows // NHEAD, NX * width), BF16),
        in_specs=[VMEM] * CHUNKS,
        out_specs=VMEM,
    )(*received)


def solution(mesh):
    return jax.shard_map(
        on_device,
        mesh=mesh,
        in_specs=(P("ctx", "head"), P("ctx", "head"), P("ctx", "head"), P("ctx"), P("head", None)),
        out_specs=P(("ctx", "head"), None),
        check_vma=False,
    )
```

time: 433 us -> 133 us (0.31)
  the two profiles are of different devices: /device:TPU:2 before, /device:TPU:96 now
where the time goes in v1:
time: 133 us; the launch traced here: 132 us
  waiting for transfers between devices  43.9 us (33%)
  starting transfers between devices  40.5 us (30%)
  Pallas kernels  20.7 us (16%)
  blocking collectives  14.7 us (11%)
  local copies, waits for them, and re-layouts  9.37 us (7%)
  other arithmetic  3.05 us (2%)
    ppermute x6, waiting for transfers between devices, on_device(): lax.ppermute(a, 'head', x_ring(d))  23.6 us
    all_to_all x1, blocking collectives, on_device(): lax.all_to_all(project(core[None], g, w_own, w_mine, w_other), 'head', 0, 0)  14.7 us
    ppermute x3, waiting for transfers between devices, on_device(): lax.ppermute(lax.dynamic_slice_in_dim(half, (x + d) % NX * width, width,...  11.6 us
    ppermute x6, starting transfers between devices, on_device(): lax.ppermute(a, 'head', x_ring(d))  11.5 us
    pallas_call x2, Pallas kernels, project(): pl.pallas_call(project_kernel, grid=(width // step,), out_shape=jax.Shape...  10.3 us
    ppermute x1, starting transfers between devices, on_device(): cross = lax.ppermute(near, 'ctx', [(c, c ^ 2) for c in range(n_ctx)])  7.81 us
    all_to_all x1, starting transfers between devices, on_device(): lax.all_to_all(project(core[None], g, w_own, w_mine, w_other), 'head', 0, 0)  6.25 us
    ppermute x3, starting transfers between devices, on_device(): lax.ppermute(lax.dynamic_slice_in_dim(half, (x + d) % NX * width, width,...  5.73 us
  transfers between devices with their start and end apart: 18, of which 9 were waited for; matrix products, arithmetic and copies ran while one was open for 7% of the time, Pallas kernels for 10%

profile of v1, /device:TPU:96, one launch (start us, length us, event | category | flops | bytes accessed | tf_op | source)
XLA Modules:
  0.0 132.4 jit_solution(3146167117990582701)
XLA Ops:
  0.0 1.0 pad_maximum_fusion.1.own
  1.0 5.0 %collective-permute-start.3 = (bf16[2,512,128]{2,1,0:T(8,128)(2,1)S(1)}, bf16[2,512,128]{2,1,0:T(8,128)(2,1)}, u32[]{:S(2)}, u32[]{:S(2)}) collective-permute-start(bf16[2,512,128]{2,1,0:T(8,128)(2,1)S(1)} %pad_maximum_fusion.1.own), channel_id=1, source_target_pairs={{0,32},{8,40},{16,48},{24,56},{32,64},{40,72},{48,80},{56,88},{64,... | collective-permute-start | bytes 786440 | tf_op jit(solution)/shard_map/ppermute | solution.py:142
  6.1 3.5 %collective-permute-start.1 = (bf16[2,512,128]{2,1,0:T(8,128)(2,1)S(1)}, bf16[2,512,128]{2,1,0:T(8,128)(2,1)S(1)}, u32[]{:S(2)}, u32[]{:S(2)}) collective-permute-start(bf16[2,512,128]{2,1,0:T(8,128)(2,1)S(1)} %pad_maximum_fusion.1.own), channel_id=1, source_target_pairs={{0,16},{8,24},{16,64},{24,72},{32,48},{40,56},{48,96},{56,104},{64... | collective-permute-start | bytes 786440 | tf_op jit(solution)/shard_map/ppermute | solution.py:143
  9.5 0.1 collective-permute-start
  9.6 1.9 %collective-permute-done.3.refs_2_ = bf16[2,512,128]{2,1,0:T(8,128)(2,1)} collective-permute-done((bf16[2,512,128]{2,1,0:T(8,128)(2,1)S(1)}, bf16[2,512,128]{2,1,0:T(8,128)(2,1)}, u32[]{:S(2)}, u32[]{:S(2)}) %collective-permute-start.3) | collective-permute-done | bytes 262176 | tf_op jit(solution)/shard_map/ppermute | solution.py:142
  11.6 7.8 %collective-permute-start.5 = (bf16[2,512,128]{2,1,0:T(8,128)(2,1)}, bf16[2,512,128]{2,1,0:T(8,128)(2,1)}, u32[]{:S(2)}, u32[]{:S(2)}) collective-permute-start(bf16[2,512,128]{2,1,0:T(8,128)(2,1)} %collective-permute-done.3.refs_2_), channel_id=1, source_target_pairs={{0,16},{8,24},{16,0},{24,8},{32,48},{40,56},{48,32},{56,40},{64,80... | collective-permute-start | bytes 786440 | tf_op jit(solution)/shard_map/ppermute | solution.py:172
  19.4 1.3 slice.3
  20.7 2.3 %collective-permute-done.1.refs_0_ = bf16[2,512,128]{2,1,0:T(8,128)(2,1)S(1)} collective-permute-done((bf16[2,512,128]{2,1,0:T(8,128)(2,1)S(1)}, bf16[2,512,128]{2,1,0:T(8,128)(2,1)S(1)}, u32[]{:S(2)}, u32[]{:S(2)}) %collective-permute-start.1) | collective-permute-done | bytes 262176 | tf_op jit(solution)/shard_map/ppermute | solution.py:143
  22.9 0.0 collective-permute-start.2
  22.9 0.6 pad_add_fusion.1.info
  23.6 0.5 collective-permute-start.4
  24.1 4.5 %collective-permute-done.5.refs_4_ = bf16[2,512,128]{2,1,0:T(8,128)(2,1)} collective-permute-done((bf16[2,512,128]{2,1,0:T(8,128)(2,1)}, bf16[2,512,128]{2,1,0:T(8,128)(2,1)}, u32[]{:S(2)}, u32[]{:S(2)}) %collective-permute-start.5) | collective-permute-done | bytes 262176 | tf_op jit(solution)/shard_map/ppermute | solution.py:172
  28.6 0.0 collective-permute-start.6
  28.6 2.4 %fusion = (bf16[256,1024]{1,0:T(8,128)(2,1)S(1)}, bf16[256,1024]{1,0:T(8,128)(2,1)S(1)}, bf16[256,1024]{1,0:T(8,128)(2,1)S(1)}) fusion(bf16[512,4096]{1,0:T(8,128)(2,1)} %param.9, s32[]{:T(128)S(6)} %select_n.67, s32[]{:T(128)S(6)} %select_n.76, s32[]{:T(128)S(6)} %select_n.73, s32[]{:T(128)S(6)} %select_n.70), kind=kLoop, calls=%fused_computation.6 | loop fusion | bytes 3145744 | tf_op jit(solution)/shard_map/dynamic_slice | solution.py:168
  31.0 1.6 %collective-permute-start.10 = (bf16[256,1024]{1,0:T(8,128)(2,1)S(1)}, bf16[256,1024]{1,0:T(8,128)(2,1)S(1)}, u32[]{:S(2)}, u32[]{:S(2)}) collective-permute-start(bf16[256,1024]{1,0:T(8,128)(2,1)S(1)} %get-tuple-element.23), channel_id=1, source_target_pairs={{0,2},{1,3},{2,4},{3,5},{4,6},{5,7},{6,0},{7,1},{8,10},{9,11},{10,... | collective-permute-start | bytes 1572872 | tf_op jit(solution)/shard_map/ppermute | solution.py:168
  32.6 2.8 %collective-permute-start.11 = (bf16[256,1024]{1,0:T(8,128)(2,1)S(1)}, bf16[256,1024]{1,0:T(8,128)(2,1)S(1)}, u32[]{:S(2)}, u32[]{:S(2)}) collective-permute-start(bf16[256,1024]{1,0:T(8,128)(2,1)S(1)} %get-tuple-element.22), channel_id=1, source_target_pairs={{0,4},{1,5},{2,6},{3,7},{4,0},{5,1},{6,2},{7,3},{8,12},{9,13},{10,... | collective-permute-start | bytes 1572872 | tf_op jit(solution)/shard_map/ppermute | solution.py:168
  35.3 1.4 %collective-permute-start.12 = (bf16[256,1024]{1,0:T(8,128)(2,1)S(1)}, bf16[256,1024]{1,0:T(8,128)(2,1)S(1)}, u32[]{:S(2)}, u32[]{:S(2)}) collective-permute-start(bf16[256,1024]{1,0:T(8,128)(2,1)S(1)} %get-tuple-element.21), channel_id=1, source_target_pairs={{0,6},{1,7},{2,0},{3,1},{4,2},{5,3},{6,4},{7,5},{8,14},{9,15},{10,... | collective-permute-start | bytes 1572872 | tf_op jit(solution)/shard_map/ppermute | solution.py:168
  36.7 1.3 and_convert_fusion.info
  38.0 0.9 copy.6.doc_ref
  38.9 4.6 %shard_map.55 = (f32[4,512,128]{2,1,0:T(8,128)}, f32[4,512,256]{2,1,0:T(8,128)}) custom-call(s32[2]{0:T(128)} %pad_add_fusion.1.info, bf16[512,512]{1,0:T(8,128)(2,1)} %q_ref.3, s32[512,1]{1,0:T(8,128)} %copy.6.doc_ref, bf16[2,512,128]{2,1,0:T(8,128)(2,1)} %copy-done.7, bf16[2,512,128]{2,1,0:T(8,128)(2,1)} %copy-done.10), custom_call_target="tpu_custom_call" | custom-call | flops 1073741824 | bytes 4194304 | tf_op jit(solution)/shard_map/pallas_call | solution.py:154
  43.4 0.0 collective-permute-done.4.refs_3_
  43.4 0.0 collective-permute-done.6.refs_5_
  43.4 3.8 %shard_map.56 = (bf16[8,32,512]{2,1,0:T(8,128)(2,1)}, bf16[8,32,512]{2,1,0:T(8,128)(2,1)}) custom-call(s32[3]{0:T(128)} %and_convert_fusion.info, bf16[512,512]{1,0:T(8,128)(2,1)} %q_ref.3, f32[4,512,128]{2,1,0:T(8,128)} %get-tuple-element.13.m_in, f32[4,512,256]{2,1,0:T(8,128)} %get-tuple-element.14.acc_in, bf16[2,512,128]{2,1,0:T(8,128)(2,1)} %copy-done.9, ...), custom_call_target="tpu_custom_call" | custom-call | flops 4294967296 | bytes 6291456 | tf_op jit(solution)/shard_map/pallas_call | solution.py:179
  47.3 0.0 collective-permute-done.10
  47.3 11.6 %collective-permute-done.11 = bf16[256,1024]{1,0:T(8,128)(2,1)S(1)} collective-permute-done((bf16[256,1024]{1,0:T(8,128)(2,1)S(1)}, bf16[256,1024]{1,0:T(8,128)(2,1)S(1)}, u32[]{:S(2)}, u32[]{:S(2)}) %collective-permute-start.11) | collective-permute-done | bytes 524320 | tf_op jit(solution)/shard_map/ppermute | solution.py:168
  58.8 0.0 collective-permute-done.12
  58.8 0.2 pad_maximum_fusion.w_mine
  59.0 0.1 collective-permute-start.13
  59.1 1.4 %collective-permute-start.7 = (bf16[8,32,512]{2,1,0:T(8,128)(2,1)}, bf16[8,32,512]{2,1,0:T(8,128)(2,1)}, u32[]{:S(2)}, u32[]{:S(2)}) collective-permute-start(bf16[8,32,512]{2,1,0:T(8,128)(2,1)} %get-tuple-element.15.a0), channel_id=1, source_target_pairs={{0,2},{1,3},{2,4},{3,5},{4,6},{5,7},{6,0},{7,1},{8,10},{9,11},{10,... | collective-permute-start | bytes 786440 | tf_op jit(solution)/shard_map/ppermute | solution.py:189
  60.5 2.4 %collective-permute-start.8 = (bf16[8,32,512]{2,1,0:T(8,128)(2,1)}, bf16[8,32,512]{2,1,0:T(8,128)(2,1)}, u32[]{:S(2)}, u32[]{:S(2)}) collective-permute-start(bf16[8,32,512]{2,1,0:T(8,128)(2,1)} %get-tuple-element.15.a0), channel_id=1, source_target_pairs={{0,4},{1,5},{2,6},{3,7},{4,0},{5,1},{6,2},{7,3},{8,12},{9,13},{10,... | collective-permute-start | bytes 786440 | tf_op jit(solution)/shard_map/ppermute | solution.py:189
  62.9 1.6 %collective-permute-start.9 = (bf16[8,32,512]{2,1,0:T(8,128)(2,1)}, bf16[8,32,512]{2,1,0:T(8,128)(2,1)}, u32[]{:S(2)}, u32[]{:S(2)}) collective-permute-start(bf16[8,32,512]{2,1,0:T(8,128)(2,1)} %get-tuple-element.15.a0), channel_id=1, source_target_pairs={{0,6},{1,7},{2,0},{3,1},{4,2},{5,3},{6,4},{7,5},{8,14},{9,15},{10,... | collective-permute-start | bytes 786440 | tf_op jit(solution)/shard_map/ppermute | solution.py:189
  64.5 2.3 %constant_dynamic-slice_fusion.w_own = bf16[512,1024]{1,0:T(8,128)(2,1)} fusion(bf16[512,4096]{1,0:T(8,128)(2,1)} %param.9, s32[]{:T(128)S(6)} %select_n.65), kind=kLoop, calls=%fused_computation.5 | loop fusion | bytes 2097156 | tf_op jit(solution)/shard_map/dynamic_slice | solution.py:193
  66.7 2.7 %collective-permute-done.7.a1 = bf16[8,32,512]{2,1,0:T(8,128)(2,1)} collective-permute-done((bf16[8,32,512]{2,1,0:T(8,128)(2,1)}, bf16[8,32,512]{2,1,0:T(8,128)(2,1)}, u32[]{:S(2)}, u32[]{:S(2)}) %collective-permute-start.7) | collective-permute-done | bytes 262176 | tf_op jit(solution)/shard_map/ppermute | solution.py:189
  69.4 6.0 %collective-permute-done.8.a2 = bf16[8,32,512]{2,1,0:T(8,128)(2,1)} collective-permute-done((bf16[8,32,512]{2,1,0:T(8,128)(2,1)}, bf16[8,32,512]{2,1,0:T(8,128)(2,1)}, u32[]{:S(2)}, u32[]{:S(2)}) %collective-permute-start.8) | collective-permute-done | bytes 262176 | tf_op jit(solution)/shard_map/ppermute | solution.py:189
  75.4 0.2 collective-permute-done.9.a3
  75.6 1.1 copy-done.1
  76.7 5.1 %shard_map.57 = bf16[8,32,1024]{2,1,0:T(8,128)(2,1)} custom-call(s32[1]{0:T(128)} %bitcast.info, bf16[8,32,512]{2,1,0:T(8,128)(2,1)} %get-tuple-element.15.a0, bf16[8,32,512]{2,1,0:T(8,128)(2,1)} %collective-permute-done.7.a1, bf16[8,32,512]{2,1,0:T(8,128)(2,1)} %collective-permute-done.8.a2, bf16[8,32,512]{2,1,0:T(8,128)(2,1)} %collective-permute-done.9.a3, ...), custom_call_target="tpu_custom_call" | custom-call | flops 1073741824 | bytes 6291456 | tf_op jit(solution)/shard_map/pallas_call | solution.py:108
  81.9 6.2 %all-to-all-start = ((bf16[8,32,1024]{2,1,0:T(8,128)(2,1)}), bf16[8,32,1024]{2,1,0:T(8,128)(2,1)S(1)}, u32[]{:S(2)}, u32[]{:S(2)}) async-start(bf16[8,32,1024]{2,1,0:T(8,128)(2,1)} %shard_map.57), calls=%async_computation | async-start | bytes 1048576 | tf_op jit(solution)/shard_map/all_to_all | solution.py:194
  88.1 2.0 %collective-permute-start.14 = (bf16[8,32,512]{2,1,0:T(8,128)(2,1)S(1)}, bf16[8,32,512]{2,1,0:T(8,128)(2,1)S(1)}, u32[]{:S(2)}, u32[]{:S(2)}) collective-permute-start(bf16[8,32,512]{2,1,0:T(8,128)(2,1)S(1)} %copy-done.3), channel_id=1, source_target_pairs={{0,2},{1,3},{2,4},{3,5},{4,6},{5,7},{6,0},{7,1},{8,10},{9,11},{10,... | collective-permute-start | bytes 786440 | tf_op jit(solution)/shard_map/ppermute | solution.py:189
  90.1 2.7 %collective-permute-start.15 = (bf16[8,32,512]{2,1,0:T(8,128)(2,1)S(1)}, bf16[8,32,512]{2,1,0:T(8,128)(2,1)S(1)}, u32[]{:S(2)}, u32[]{:S(2)}) collective-permute-start(bf16[8,32,512]{2,1,0:T(8,128)(2,1)S(1)} %copy-done.3), channel_id=1, source_target_pairs={{0,4},{1,5},{2,6},{3,7},{4,0},{5,1},{6,2},{7,3},{8,12},{9,13},{10,... | collective-permute-start | bytes 786440 | tf_op jit(solution)/shard_map/ppermute | solution.py:189
  92.8 1.5 %collective-permute-start.16 = (bf16[8,32,512]{2,1,0:T(8,128)(2,1)S(1)}, bf16[8,32,512]{2,1,0:T(8,128)(2,1)S(1)}, u32[]{:S(2)}, u32[]{:S(2)}) collective-permute-start(bf16[8,32,512]{2,1,0:T(8,128)(2,1)S(1)} %copy-done.3), channel_id=1, source_target_pairs={{0,6},{1,7},{2,0},{3,1},{4,2},{5,3},{6,4},{7,5},{8,14},{9,15},{10,... | collective-permute-start | bytes 786440 | tf_op jit(solution)/shard_map/ppermute | solution.py:189
  94.3 9.8 %collective-permute-done.14.a1 = bf16[8,32,512]{2,1,0:T(8,128)(2,1)S(1)} collective-permute-done((bf16[8,32,512]{2,1,0:T(8,128)(2,1)S(1)}, bf16[8,32,512]{2,1,0:T(8,128)(2,1)S(1)}, u32[]{:S(2)}, u32[]{:S(2)}) %collective-permute-start.14) | collective-permute-done | bytes 262176 | tf_op jit(solution)/shard_map/ppermute | solution.py:189
  104.0 5.0 %collective-permute-done.15.a2 = bf16[8,32,512]{2,1,0:T(8,128)(2,1)S(1)} collective-permute-done((bf16[8,32,512]{2,1,0:T(8,128)(2,1)S(1)}, bf16[8,32,512]{2,1,0:T(8,128)(2,1)S(1)}, u32[]{:S(2)}, u32[]{:S(2)}) %collective-permute-start.15) | collective-permute-done | bytes 262176 | tf_op jit(solution)/shard_map/ppermute | solution.py:189
  109.0 0.7 copy-done.5
  109.7 0.7 copy-done.6
  110.4 5.1 %shard_map.58 = bf16[8,32,1024]{2,1,0:T(8,128)(2,1)} custom-call(s32[1]{0:T(128)} %bitcast.info, bf16[8,32,512]{2,1,0:T(8,128)(2,1)} %get-tuple-element.20.a0, bf16[8,32,512]{2,1,0:T(8,128)(2,1)} %copy-done.4, bf16[8,32,512]{2,1,0:T(8,128)(2,1)} %copy-done.5, bf16[8,32,512]{2,1,0:T(8,128)(2,1)} %copy-done.6, ...), custom_call_target="tpu_custom_call" | custom-call | flops 1073741824 | bytes 6291456 | tf_op jit(solution)/shard_map/pallas_call | solution.py:108
  115.6 14.7 %all_to_all.10.r1 = bf16[8,32,1024]{2,1,0:T(8,128)(2,1)} all-to-all(bf16[8,32,1024]{2,1,0:T(8,128)(2,1)} %shard_map.58), channel_id=1, replica_groups=mesh['ctx'=32,'head'=8] {'head'}, dimensions={0} | all-to-all | bytes 1048576 | tf_op jit(solution)/shard_map/all_to_all | solution.py:194
  130.3 2.1 %shard_map.59 = bf16[64,4096]{1,0:T(8,128)(2,1)} custom-call(bf16[8,32,1024]{2,1,0:T(8,128)(2,1)} %copy-done.2, bf16[8,32,1024]{2,1,0:T(8,128)(2,1)} %all_to_all.10.r1), custom_call_target="tpu_custom_call" | custom-call | tf_op jit(solution)/shard_map/pallas_call | solution.py:195
  (26 shorter events, 0.1 us)
Async XLA Ops:
  1.0 30.0 %copy-start.7 = (bf16[2,512,128]{2,1,0:T(8,128)(2,1)}, bf16[2,512,128]{2,1,0:T(8,128)(2,1)S(1)}, u32[]{:S(2)}) copy-start(bf16[2,512,128]{2,1,0:T(8,128)(2,1)S(1)} %pad_maximum_fusion.1.own) | copy-start | bytes 786436
  1.0 10.6 %collective-permute-start.3 = (bf16[2,512,128]{2,1,0:T(8,128)(2,1)S(1)}, bf16[2,512,128]{2,1,0:T(8,128)(2,1)}, u32[]{:S(2)}, u32[]{:S(2)}) collective-permute-start(bf16[2,512,128]{2,1,0:T(8,128)(2,1)S(1)} %pad_maximum_fusion.1.own), channel_id=1, source_target_pairs={{0,32},{8,40},{16,48},{24,56},{32,64},{40,72},{48,80},{56,88},{64,... | collective-permute-start | bytes 786440 | tf_op jit(solution)/shard_map/ppermute | solution.py:142
  6.1 16.9 %collective-permute-start.1 = (bf16[2,512,128]{2,1,0:T(8,128)(2,1)S(1)}, bf16[2,512,128]{2,1,0:T(8,128)(2,1)S(1)}, u32[]{:S(2)}, u32[]{:S(2)}) collective-permute-start(bf16[2,512,128]{2,1,0:T(8,128)(2,1)S(1)} %pad_maximum_fusion.1.own), channel_id=1, source_target_pairs={{0,16},{8,24},{16,64},{24,72},{32,48},{40,56},{48,96},{56,104},{64... | collective-permute-start | bytes 786440 | tf_op jit(solution)/shard_map/ppermute | solution.py:143
  9.5 14.0 %collective-permute-start = (bf16[2,512,128]{2,1,0:T(8,128)(2,1)S(1)}, bf16[2,512,128]{2,1,0:T(8,128)(2,1)S(1)}, u32[]{:S(2)}, u32[]{:S(2)}) collective-permute-start(bf16[2,512,128]{2,1,0:T(8,128)(2,1)S(1)} %pad_maximum_fusion.1.own), channel_id=1, source_target_pairs={{0,8},{8,0},{16,24},{24,16},{32,40},{40,32},{48,56},{56,48},{64,72... | collective-permute-start | bytes 786440 | tf_op jit(solution)/shard_map/ppermute | solution.py:147
  11.6 17.0 %collective-permute-start.5 = (bf16[2,512,128]{2,1,0:T(8,128)(2,1)}, bf16[2,512,128]{2,1,0:T(8,128)(2,1)}, u32[]{:S(2)}, u32[]{:S(2)}) collective-permute-start(bf16[2,512,128]{2,1,0:T(8,128)(2,1)} %collective-permute-done.3.refs_2_), channel_id=1, source_target_pairs={{0,16},{8,24},{16,0},{24,8},{32,48},{40,56},{48,32},{56,40},{64,80... | collective-permute-start | bytes 786440 | tf_op jit(solution)/shard_map/ppermute | solution.py:172
  22.9 8.0 %copy-start.9 = (bf16[2,512,128]{2,1,0:T(8,128)(2,1)}, bf16[2,512,128]{2,1,0:T(8,128)(2,1)S(1)}, u32[]{:S(2)}) copy-start(bf16[2,512,128]{2,1,0:T(8,128)(2,1)S(1)} %collective-permute-done.1.refs_0_) | copy-start | bytes 786436
  22.9 12.4 %collective-permute-start.2 = (bf16[2,512,128]{2,1,0:T(8,128)(2,1)S(1)}, bf16[2,512,128]{2,1,0:T(8,128)(2,1)S(1)}, u32[]{:S(2)}, u32[]{:S(2)}) collective-permute-start(bf16[2,512,128]{2,1,0:T(8,128)(2,1)S(1)} %collective-permute-done.1.refs_0_), channel_id=1, source_target_pairs={{0,8},{8,0},{16,24},{24,16},{32,40},{40,32},{48,56},{56,48},{64,72... | collective-permute-start | bytes 786440 | tf_op jit(solution)/shard_map/ppermute | solution.py:173
  23.6 14.4 %copy-start.8 = (s32[512]{0:T(512)S(1)}, s32[512]{0:T(512)}, u32[]{:S(2)}) copy-start(s32[512]{0:T(512)} %param.8) | copy-start | bytes 6148
  23.6 7.4 %copy-start.10 = (bf16[2,512,128]{2,1,0:T(8,128)(2,1)}, bf16[2,512,128]{2,1,0:T(8,128)(2,1)S(1)}, u32[]{:S(2)}) copy-start(bf16[2,512,128]{2,1,0:T(8,128)(2,1)S(1)} %collective-permute-done.partner) | copy-start | bytes 786436
  23.6 19.9 %collective-permute-start.4 = (bf16[2,512,128]{2,1,0:T(8,128)(2,1)}, bf16[2,512,128]{2,1,0:T(8,128)(2,1)}, u32[]{:S(2)}, u32[]{:S(2)}) collective-permute-start(bf16[2,512,128]{2,1,0:T(8,128)(2,1)} %collective-permute-done.3.refs_2_), channel_id=1, source_target_pairs={{0,8},{8,0},{16,24},{24,16},{32,40},{40,32},{48,56},{56,48},{64,72... | collective-permute-start | bytes 786440 | tf_op jit(solution)/shard_map/ppermute | solution.py:173
  28.6 14.9 %collective-permute-start.6 = (bf16[2,512,128]{2,1,0:T(8,128)(2,1)}, bf16[2,512,128]{2,1,0:T(8,128)(2,1)}, u32[]{:S(2)}, u32[]{:S(2)}) collective-permute-start(bf16[2,512,128]{2,1,0:T(8,128)(2,1)} %collective-permute-done.5.refs_4_), channel_id=1, source_target_pairs={{0,8},{8,0},{16,24},{24,16},{32,40},{40,32},{48,56},{56,48},{64,72... | collective-permute-start | bytes 786440 | tf_op jit(solution)/shard_map/ppermute | solution.py:173
  31.0 16.3 %collective-permute-start.10 = (bf16[256,1024]{1,0:T(8,128)(2,1)S(1)}, bf16[256,1024]{1,0:T(8,128)(2,1)S(1)}, u32[]{:S(2)}, u32[]{:S(2)}) collective-permute-start(bf16[256,1024]{1,0:T(8,128)(2,1)S(1)} %get-tuple-element.23), channel_id=1, source_target_pairs={{0,2},{1,3},{2,4},{3,5},{4,6},{5,7},{6,0},{7,1},{8,10},{9,11},{10,... | collective-permute-start | bytes 1572872 | tf_op jit(solution)/shard_map/ppermute | solution.py:168
  32.6 26.3 %collective-permute-start.11 = (bf16[256,1024]{1,0:T(8,128)(2,1)S(1)}, bf16[256,1024]{1,0:T(8,128)(2,1)S(1)}, u32[]{:S(2)}, u32[]{:S(2)}) collective-permute-start(bf16[256,1024]{1,0:T(8,128)(2,1)S(1)} %get-tuple-element.22), channel_id=1, source_target_pairs={{0,4},{1,5},{2,6},{3,7},{4,0},{5,1},{6,2},{7,3},{8,12},{9,13},{10,... | collective-permute-start | bytes 1572872 | tf_op jit(solution)/shard_map/ppermute | solution.py:168
  35.3 1.4 %copy-start.11 = (bf16[2,512,128]{2,1,0:T(8,128)(2,1)}, bf16[2,512,128]{2,1,0:T(8,128)(2,1)S(1)}, u32[]{:S(2)}) copy-start(bf16[2,512,128]{2,1,0:T(8,128)(2,1)S(1)} %collective-permute-done.2.refs_1_) | copy-start | bytes 786436
  35.3 23.5 %collective-permute-start.12 = (bf16[256,1024]{1,0:T(8,128)(2,1)S(1)}, bf16[256,1024]{1,0:T(8,128)(2,1)S(1)}, u32[]{:S(2)}, u32[]{:S(2)}) collective-permute-start(bf16[256,1024]{1,0:T(8,128)(2,1)S(1)} %get-tuple-element.21), channel_id=1, source_target_pairs={{0,6},{1,7},{2,0},{3,1},{4,2},{5,3},{6,4},{7,5},{8,14},{9,15},{10,... | collective-permute-start | bytes 1572872 | tf_op jit(solution)/shard_map/ppermute | solution.py:168
  59.0 16.6 %copy-start = (bf16[3,256,1024]{2,1,0:T(8,128)(2,1)}, bf16[3,256,1024]{2,1,0:T(8,128)(2,1)S(1)}, u32[]{:S(2)}) copy-start(bf16[3,256,1024]{2,1,0:T(8,128)(2,1)S(1)} %pad_maximum_fusion.w_mine) | copy-start | bytes 4718596
  59.0 16.6 %collective-permute-start.13 = (bf16[3,256,1024]{2,1,0:T(8,128)(2,1)S(1)}, bf16[3,256,1024]{2,1,0:T(8,128)(2,1)S(1)}, u32[]{:S(2)}, u32[]{:S(2)}) collective-permute-start(bf16[3,256,1024]{2,1,0:T(8,128)(2,1)S(1)} %pad_maximum_fusion.w_mine), channel_id=1, source_target_pairs={{0,8},{8,0},{16,24},{24,16},{32,40},{40,32},{48,56},{56,48},{64,72... | collective-permute-start | bytes 4718600 | tf_op jit(solution)/shard_map/ppermute | solution.py:192
  59.1 10.3 %collective-permute-start.7 = (bf16[8,32,512]{2,1,0:T(8,128)(2,1)}, bf16[8,32,512]{2,1,0:T(8,128)(2,1)}, u32[]{:S(2)}, u32[]{:S(2)}) collective-permute-start(bf16[8,32,512]{2,1,0:T(8,128)(2,1)} %get-tuple-element.15.a0), channel_id=1, source_target_pairs={{0,2},{1,3},{2,4},{3,5},{4,6},{5,7},{6,0},{7,1},{8,10},{9,11},{10,... | collective-permute-start | bytes 786440 | tf_op jit(solution)/shard_map/ppermute | solution.py:189
  60.5 14.9 %collective-permute-start.8 = (bf16[8,32,512]{2,1,0:T(8,128)(2,1)}, bf16[8,32,512]{2,1,0:T(8,128)(2,1)}, u32[]{:S(2)}, u32[]{:S(2)}) collective-permute-start(bf16[8,32,512]{2,1,0:T(8,128)(2,1)} %get-tuple-element.15.a0), channel_id=1, source_target_pairs={{0,4},{1,5},{2,6},{3,7},{4,0},{5,1},{6,2},{7,3},{8,12},{9,13},{10,... | collective-permute-start | bytes 786440 | tf_op jit(solution)/shard_map/ppermute | solution.py:189
  62.9 12.7 %collective-permute-start.9 = (bf16[8,32,512]{2,1,0:T(8,128)(2,1)}, bf16[8,32,512]{2,1,0:T(8,128)(2,1)}, u32[]{:S(2)}, u32[]{:S(2)}) collective-permute-start(bf16[8,32,512]{2,1,0:T(8,128)(2,1)} %get-tuple-element.15.a0), channel_id=1, source_target_pairs={{0,6},{1,7},{2,0},{3,1},{4,2},{5,3},{6,4},{7,5},{8,14},{9,15},{10,... | collective-permute-start | bytes 786440 | tf_op jit(solution)/shard_map/ppermute | solution.py:189
  66.7 21.4 %copy-start.3 = (bf16[8,32,512]{2,1,0:T(8,128)(2,1)S(1)}, bf16[8,32,512]{2,1,0:T(8,128)(2,1)}, u32[]{:S(2)}) copy-start(bf16[8,32,512]{2,1,0:T(8,128)(2,1)} %get-tuple-element.20.a0) | copy-start | bytes 786436
  75.6 1.1 copy-start.1
  81.9 33.7 %all-to-all-start = ((bf16[8,32,1024]{2,1,0:T(8,128)(2,1)}), bf16[8,32,1024]{2,1,0:T(8,128)(2,1)S(1)}, u32[]{:S(2)}, u32[]{:S(2)}) async-start(bf16[8,32,1024]{2,1,0:T(8,128)(2,1)} %shard_map.57), calls=%async_computation | async-start | bytes 1048576 | tf_op jit(solution)/shard_map/all_to_all | solution.py:194
  88.1 15.9 %collective-permute-start.14 = (bf16[8,32,512]{2,1,0:T(8,128)(2,1)S(1)}, bf16[8,32,512]{2,1,0:T(8,128)(2,1)S(1)}, u32[]{:S(2)}, u32[]{:S(2)}) collective-permute-start(bf16[8,32,512]{2,1,0:T(8,128)(2,1)S(1)} %copy-done.3), channel_id=1, source_target_pairs={{0,2},{1,3},{2,4},{3,5},{4,6},{5,7},{6,0},{7,1},{8,10},{9,11},{10,... | collective-permute-start | bytes 786440 | tf_op jit(solution)/shard_map/ppermute | solution.py:189
  90.1 18.9 %collective-permute-start.15 = (bf16[8,32,512]{2,1,0:T(8,128)(2,1)S(1)}, bf16[8,32,512]{2,1,0:T(8,128)(2,1)S(1)}, u32[]{:S(2)}, u32[]{:S(2)}) collective-permute-start(bf16[8,32,512]{2,1,0:T(8,128)(2,1)S(1)} %copy-done.3), channel_id=1, source_target_pairs={{0,4},{1,5},{2,6},{3,7},{4,0},{5,1},{6,2},{7,3},{8,12},{9,13},{10,... | collective-permute-start | bytes 786440 | tf_op jit(solution)/shard_map/ppermute | solution.py:189
  92.8 16.2 %collective-permute-start.16 = (bf16[8,32,512]{2,1,0:T(8,128)(2,1)S(1)}, bf16[8,32,512]{2,1,0:T(8,128)(2,1)S(1)}, u32[]{:S(2)}, u32[]{:S(2)}) collective-permute-start(bf16[8,32,512]{2,1,0:T(8,128)(2,1)S(1)} %copy-done.3), channel_id=1, source_target_pairs={{0,6},{1,7},{2,0},{3,1},{4,2},{5,3},{6,4},{7,5},{8,14},{9,15},{10,... | collective-permute-start | bytes 786440 | tf_op jit(solution)/shard_map/ppermute | solution.py:189
  104.0 5.0 %copy-start.4 = (bf16[8,32,512]{2,1,0:T(8,128)(2,1)}, bf16[8,32,512]{2,1,0:T(8,128)(2,1)S(1)}, u32[]{:S(2)}) copy-start(bf16[8,32,512]{2,1,0:T(8,128)(2,1)S(1)} %collective-permute-done.14.a1) | copy-start | bytes 786436
  109.0 0.7 copy-start.5
  109.7 0.7 copy-start.6
  115.6 14.7 %copy-start.2 = (bf16[8,32,1024]{2,1,0:T(8,128)(2,1)}, bf16[8,32,1024]{2,1,0:T(8,128)(2,1)S(1)}, u32[]{:S(2)}) copy-start(bf16[8,32,1024]{2,1,0:T(8,128)(2,1)S(1)} %all-to-all-done.r0) | copy-start | bytes 1572868

commit v2 on v1

v2 whole, which is shorter than its diff:
```python
import jax
import jax.numpy as jnp
from jax import lax
from jax.experimental import pallas as pl
from jax.experimental.pallas import tpu as pltpu
from jax.sharding import PartitionSpec as P


HD = 128
GROUP = 4
NX = 4
NHEAD = 8
NEG = -1.0e30
SCALE2 = HD ** -0.5 * 1.4426950408889634
F32 = jnp.float32
BF16 = jnp.bfloat16


VMEM = pl.BlockSpec(memory_space=pltpu.VMEM)
SMEM = pl.BlockSpec(memory_space=pltpu.SMEM)
PARAMS = pltpu.CompilerParams(vmem_limit_bytes=56 << 20)


def x_ring(d):
    return [(h, (h // 2 + d) % NX * 2 + h % 2) for h in range(NHEAD)]


def visit(q_ref, k, v, ok, m_sc, acc_sc, first):
    rows = q_ref.shape[0]
    v = jnp.concatenate([v, jnp.ones_like(v)], axis=1)
    scores = [
        lax.dot_general(
            q_ref[:, g * HD:(g + 1) * HD], k, (((1,), (1,)), ((), ())), preferred_element_type=F32
        )
        for g in range(GROUP)
    ]
    for g, s in enumerate(scores):
        if ok is not None:
            s = jnp.where(ok, s, NEG)
        top = jnp.max(s, axis=1, keepdims=True)
        if first:
            m_new = jnp.broadcast_to(top, (rows, HD))
        else:
            m_old = m_sc[g]
            m_new = jnp.maximum(m_old, top)
        base = m_new * SCALE2
        p = jnp.exp2(s * SCALE2 - jnp.tile(base, (1, s.shape[1] // HD)))
        pv = jnp.dot(p.astype(BF16), v, preferred_element_type=F32)
        if first:
            acc_sc[g] = pv
        else:
            factor = jnp.exp2(m_old * SCALE2 - base)
            acc_sc[g] = acc_sc[g] * jnp.tile(factor, (1, 2)) + pv
        m_sc[g] = m_new


def own_kernel(q_ref, doc_ref, own, partner, m_ref, acc_ref):
    rows = q_ref.shape[0]
    ctx = lax.axis_index("ctx")
    r = lax.broadcasted_iota(jnp.int32, (rows, rows), 0)
    c = lax.broadcasted_iota(jnp.int32, (rows, rows), 1)
    groups, lanes = doc_ref.shape
    doc = jnp.concatenate([
        jnp.broadcast_to(doc_ref[i:i + 1], (lanes, lanes)).T for i in range(groups)
    ]) - ctx * rows
    doc = jnp.tile(doc, (1, rows // lanes))
    visit(q_ref, own[0], own[1], (c >= doc) & (c <= r), m_ref, acc_ref, True)

    @pl.when(lax.rem(ctx, 2) == 1)
    def _():
        visit(q_ref, partner[0], partner[1], c - rows >= doc, m_ref, acc_ref, False)


def rest_kernel(doc, q_ref, m_in, acc_in, *refs):
    blocks, (o0, o1, m_sc, acc_sc) = refs[:6], refs[6:]
    m_sc[...] = m_in[...]
    acc_sc[...] = acc_in[...]
    cell = lax.div(lax.axis_index("ctx"), 2)
    odd = lax.rem(cell, 2)
    size = 2 * q_ref.shape[0]
    for i, other in enumerate((cell - 3 + 2 * odd, cell - 2, cell - 1 - 2 * odd)):
        a, b = blocks[2 * i:2 * i + 2]

        @pl.when((other >= 0) & (other * size >= doc[0]))
        def _(a=a, b=b):
            k = jnp.concatenate([a[0], b[0]], axis=0)
            v = jnp.concatenate([a[1], b[1]], axis=0)
            visit(q_ref, k, v, None, m_sc, acc_sc, False)

    for g in range(GROUP):
        acc = acc_sc[g]
        out = (acc[:, :HD] / acc[:, HD:]).astype(BF16)
        out = out.reshape(NHEAD, 2, -1, HD)
        o0[:, :, g * HD:(g + 1) * HD] = out[:, 0]
        o1[:, :, g * HD:(g + 1) * HD] = out[:, 1]


def project_kernel(info, *refs):
    left, (w_own, w_mine, w_other, o_ref, a_sc) = refs[:2 * NX], refs[2 * NX:]
    depth = w_mine.shape[1]
    core = info[1]

    @pl.when(pl.program_id(0) == 0)
    def _():
        for d in range(NX):
            for k in range(2):
                a = left[2 * d + k]
                for j, half in enumerate((core, 1 - core) if d else (0, 1)):
                    part = a[:, :, pl.ds(pl.multiple_of(half * depth, depth), depth)]
                    part = part.reshape(-1, depth)
                    rows = part.shape[0]
                    a_sc[k * rows:(k + 1) * rows, (2 * d + j) * depth:(2 * d + j + 1) * depth] = part

    total = jnp.dot(a_sc[:, :2 * depth], w_own[...], preferred_element_type=F32)
    for d in range(1, NX):
        for j, w in enumerate((w_mine, w_other)):
            cols = slice((2 * d + j) * depth, (2 * d + j + 1) * depth)
            total = total + jnp.dot(a_sc[:, cols], w[d - 1], preferred_element_type=F32)
    rows = total.shape[0] // 2
    for k in range(2):
        part = total[k * rows:(k + 1) * rows].astype(BF16).reshape(NHEAD, -1, total.shape[1])
        o_ref[:, k * part.shape[1]:(k + 1) * part.shape[1]] = part


def project(info, attended, weight, w_mine, w_other):
    rows = attended[0].shape[1] * 2
    width = w_mine.shape[2]
    steps = 4
    step = width // steps
    mine = pl.BlockSpec((NX - 1, w_mine.shape[1], step), lambda n, info: (0, 0, n))
    return pl.pallas_call(
        project_kernel,
        out_shape=jax.ShapeDtypeStruct((NHEAD, rows, width), BF16),
        grid_spec=pltpu.PrefetchScalarGridSpec(
            num_scalar_prefetch=1,
            grid=(steps,),
            in_specs=[VMEM] * (2 * NX) + [
                pl.BlockSpec((weight.shape[0], step), lambda n, info: (0, info[0] * steps + n)),
                mine,
                mine,
            ],
            out_specs=pl.BlockSpec((NHEAD, rows, step), lambda n, info: (0, 0, n)),
            scratch_shapes=[pltpu.VMEM((NHEAD * rows, NX * weight.shape[0]), BF16)],
        ),
        compiler_params=PARAMS,
    )(info, *attended, weight, w_mine, w_other)


def finish_kernel(r, o_ref):
    width = r.shape[2]
    for x in range(NX):
        both = r[2 * x].astype(F32) + r[2 * x + 1].astype(F32)
        o_ref[:, x * width:(x + 1) * width] = both.astype(BF16)


def on_device(queries, keys, values, doc_start, out_weight):
    rows = queries.shape[0]
    ctx = lax.axis_index("ctx")
    head = lax.axis_index("head")
    n_ctx = lax.axis_size("ctx")
    core, x = ctx % 2, head // 2
    swap = [(c, c ^ 1) for c in range(n_ctx)]
    own = jnp.stack([keys, values])

    near = lax.ppermute(own, "ctx", [(c, c + 4) for c in range(n_ctx - 4)])
    jump = [(c, c + (6 if c // 2 % 2 else 2)) for c in range(n_ctx)]
    far = lax.ppermute(own, "ctx", [(c, t) for c, t in jump if t < n_ctx])
    partner = lax.ppermute(own, "ctx", swap)

    width = out_weight.shape[1] // NX
    depth = out_weight.shape[0] // 2
    w_mine = [
        lax.ppermute(w, "head", x_ring(d))
        for d, w in (
            (d, lax.dynamic_slice(out_weight, (core * depth, (x + d) % NX * width), (depth, width)))
            for d in range(1, NX)
        )
    ]

    state = (
        jax.ShapeDtypeStruct((GROUP, rows, HD), F32),
        jax.ShapeDtypeStruct((GROUP, rows, 2 * HD), F32),
    )
    m, acc = pl.pallas_call(
        own_kernel,
        out_shape=state,
        in_specs=[VMEM] * 4,
        out_specs=[VMEM] * 2,
        compiler_params=PARAMS,
    )(queries, doc_start.reshape(-1, HD), own, partner)

    cross = lax.ppermute(near, "ctx", [(c, c ^ 2) for c in range(n_ctx)])
    far_o = lax.ppermute(far, "ctx", swap)
    near_o = lax.ppermute(near, "ctx", swap)
    cross_o = lax.ppermute(cross, "ctx", swap)
    half = jax.ShapeDtypeStruct((NHEAD, rows // NHEAD // 2, GROUP * HD), BF16)
    a0, a1 = pl.pallas_call(
        rest_kernel,
        out_shape=[half] * 2,
        in_specs=[SMEM] + [VMEM] * 9,
        out_specs=[VMEM] * 2,
        scratch_shapes=[pltpu.VMEM(t.shape, t.dtype) for t in state],
        compiler_params=PARAMS,
    )(doc_start, queries, m, acc, far, far_o, near, near_o, cross, cross_o)

    up0 = lax.ppermute(a0, "head", x_ring(1))
    down1 = lax.ppermute(a1, "head", x_ring(3))
    down0 = lax.ppermute(a0, "head", x_ring(3))
    up1 = lax.ppermute(a1, "head", x_ring(1))
    across0 = lax.ppermute(up0, "head", x_ring(1))
    across1 = lax.ppermute(down1, "head", x_ring(3))
    w_mine = jnp.stack(lax.optimization_barrier((*w_mine, up0))[:-1])
    w_other = lax.ppermute(w_mine, "ctx", swap)
    attended = (a0, a1, up0, up1, across0, across1, down0, down1)
    info = jnp.stack([x, core]).astype(jnp.int32)
    partial = project(info, attended, out_weight, w_mine, w_other)
    received = lax.all_to_all(partial, "head", 0, 0)
    return pl.pallas_call(
        finish_kernel,
        out_shape=jax.ShapeDtypeStruct((rows // NHEAD, NX * width), BF16),
        in_specs=[VMEM],
        out_specs=VMEM,
    )(received)


def solution(mesh):
    return jax.shard_map(
        on_device,
        mesh=mesh,
        in_specs=(P("ctx", "head"), P("ctx", "head"), P("ctx", "head"), P("ctx"), P("head", None)),
        out_specs=P(("ctx", "head"), None),
        check_vma=False,
    )
```

time: 133 us -> 113 us (0.85)
  the two profiles are of different devices: /device:TPU:96 before, /device:TPU:160 now
where the time goes in v2:
time: 113 us
  waiting for transfers between devices  38.5 us (34%)
  starting transfers between devices  26.1 us (23%)
  blocking collectives  21.1 us (19%)
  Pallas kernels  20.3 us (18%)
  local copies, waits for them, and re-layouts  4.82 us (4%)
  other arithmetic  1.74 us (2%)
    all_to_all x1, blocking collectives, on_device(): received = lax.all_to_all(partial, 'head', 0, 0)  21.1 us
    ppermute x3, waiting for transfers between devices, on_device(): lax.ppermute(w, 'head', x_ring(d))  9.8 us
    pallas_call x1, Pallas kernels, project(): pl.pallas_call(project_kernel, out_shape=jax.ShapeDtypeStruct((NHEAD, row...  7.23 us
    ppermute x1, waiting for transfers between devices, on_device(): far = lax.ppermute(own, 'ctx', [(c, t) for c, t in jump if t < n_ctx])  7.18 us
    ppermute x1, starting transfers between devices, on_device(): cross = lax.ppermute(near, 'ctx', [(c, c ^ 2) for c in range(n_ctx)])  6.72 us
    pallas_call x1, Pallas kernels, on_device(): pl.pallas_call(rest_kernel, out_shape=[half] * 2, in_specs=[SMEM] + [VMEM...  6.42 us
    ppermute x3, starting transfers between devices, on_device(): lax.ppermute(w, 'head', x_ring(d))  5.73 us
    ppermute x1, waiting for transfers between devices, on_device(): down1 = lax.ppermute(a1, 'head', x_ring(3))  5.12 us
  transfers between devices with their start and end apart: 17, of which 8 were waited for; matrix products, arithmetic and copies ran while one was open for 2% of the time, Pallas kernels for 10%

profile of v2, /device:TPU:160, one launch (start us, length us, event | category | flops | bytes accessed | tf_op | source)
XLA Modules:
  0.0 112.7 jit_solution(6404805331222120221)
XLA Ops:
  0.0 1.0 pad_maximum_fusion.1.own
  1.0 0.0 copy-start.2
  1.0 2.9 %collective-permute-start.3 = (bf16[2,512,128]{2,1,0:T(8,128)(2,1)S(1)}, bf16[2,512,128]{2,1,0:T(8,128)(2,1)S(1)}, u32[]{:S(2)}, u32[]{:S(2)}) collective-permute-start(bf16[2,512,128]{2,1,0:T(8,128)(2,1)S(1)} %pad_maximum_fusion.1.own), channel_id=1, source_target_pairs={{0,32},{8,40},{16,48},{24,56},{32,64},{40,72},{48,80},{56,88},{64,... | collective-permute-start | bytes 786440 | tf_op jit(solution)/shard_map/ppermute | solution.py:165
  3.9 3.5 %collective-permute-start.1 = (bf16[2,512,128]{2,1,0:T(8,128)(2,1)S(1)}, bf16[2,512,128]{2,1,0:T(8,128)(2,1)S(1)}, u32[]{:S(2)}, u32[]{:S(2)}) collective-permute-start(bf16[2,512,128]{2,1,0:T(8,128)(2,1)S(1)} %pad_maximum_fusion.1.own), channel_id=1, source_target_pairs={{0,16},{8,24},{16,64},{24,72},{32,48},{40,56},{48,96},{56,104},{64... | collective-permute-start | bytes 786440 | tf_op jit(solution)/shard_map/ppermute | solution.py:167
  7.4 3.5 %collective-permute-done.3.refs_2_ = bf16[2,512,128]{2,1,0:T(8,128)(2,1)S(1)} collective-permute-done((bf16[2,512,128]{2,1,0:T(8,128)(2,1)S(1)}, bf16[2,512,128]{2,1,0:T(8,128)(2,1)S(1)}, u32[]{:S(2)}, u32[]{:S(2)}) %collective-permute-start.3) | collective-permute-done | bytes 262176 | tf_op jit(solution)/shard_map/ppermute | solution.py:165
  11.0 6.7 %collective-permute-start.5 = (bf16[2,512,128]{2,1,0:T(8,128)(2,1)S(1)}, bf16[2,512,128]{2,1,0:T(8,128)(2,1)S(1)}, u32[]{:S(2)}, u32[]{:S(2)}) collective-permute-start(bf16[2,512,128]{2,1,0:T(8,128)(2,1)S(1)} %collective-permute-done.3.refs_2_), channel_id=1, source_target_pairs={{0,16},{8,24},{16,0},{24,8},{32,48},{40,56},{48,32},{56,40},{64,80... | collective-permute-start | bytes 786440 | tf_op jit(solution)/shard_map/ppermute | solution.py:192
  17.7 0.0 collective-permute-start
  17.7 7.2 %collective-permute-done.1.refs_0_ = bf16[2,512,128]{2,1,0:T(8,128)(2,1)S(1)} collective-permute-done((bf16[2,512,128]{2,1,0:T(8,128)(2,1)S(1)}, bf16[2,512,128]{2,1,0:T(8,128)(2,1)S(1)}, u32[]{:S(2)}, u32[]{:S(2)}) %collective-permute-start.1) | collective-permute-done | bytes 262176 | tf_op jit(solution)/shard_map/ppermute | solution.py:167
  24.9 0.0 collective-permute-start.2
  24.9 1.6 %fusion = (bf16[256,1024]{1,0:T(8,128)(2,1)S(1)}, bf16[256,1024]{1,0:T(8,128)(2,1)S(1)}, bf16[256,1024]{1,0:T(8,128)(2,1)S(1)}) fusion(bf16[512,4096]{1,0:T(8,128)(2,1)} %refs_8_.1, s32[]{:T(128)S(6)} %select_n.39, s32[]{:T(128)S(6)} %select_n.45, s32[]{:T(128)S(6)} %select_n.43, s32[]{:T(128)S(6)} %select_n.41), kind=kLoop, calls=%fused_computation.3 | loop fusion | bytes 3145744 | tf_op jit(solution)/shard_map/dynamic_slice | solution.py:175
  26.5 1.6 %collective-permute-start.13 = (bf16[256,1024]{1,0:T(8,128)(2,1)S(1)}, bf16[256,1024]{1,0:T(8,128)(2,1)S(1)}, u32[]{:S(2)}, u32[]{:S(2)}) collective-permute-start(bf16[256,1024]{1,0:T(8,128)(2,1)S(1)} %get-tuple-element.21), channel_id=1, source_target_pairs={{0,2},{1,3},{2,4},{3,5},{4,6},{5,7},{6,0},{7,1},{8,10},{9,11},{10,... | collective-permute-start | bytes 1572872 | tf_op jit(solution)/shard_map/ppermute | solution.py:173
  28.0 0.1 collective-permute-start.4
  28.2 0.0 collective-permute-done.5.refs_4_
  28.2 0.4 collective-permute-start.6
  28.5 0.0 collective-permute-done.partner
  28.6 2.7 %collective-permute-start.14 = (bf16[256,1024]{1,0:T(8,128)(2,1)S(1)}, bf16[256,1024]{1,0:T(8,128)(2,1)S(1)}, u32[]{:S(2)}, u32[]{:S(2)}) collective-permute-start(bf16[256,1024]{1,0:T(8,128)(2,1)S(1)} %get-tuple-element.20), channel_id=1, source_target_pairs={{0,4},{1,5},{2,6},{3,7},{4,0},{5,1},{6,2},{7,3},{8,12},{9,13},{10,... | collective-permute-start | bytes 1572872 | tf_op jit(solution)/shard_map/ppermute | solution.py:173
  31.3 0.0 collective-permute-done.2.refs_1_
  31.3 1.4 %collective-permute-start.15 = (bf16[256,1024]{1,0:T(8,128)(2,1)S(1)}, bf16[256,1024]{1,0:T(8,128)(2,1)S(1)}, u32[]{:S(2)}, u32[]{:S(2)}) collective-permute-start(bf16[256,1024]{1,0:T(8,128)(2,1)S(1)} %get-tuple-element.19), channel_id=1, source_target_pairs={{0,6},{1,7},{2,0},{3,1},{4,2},{5,3},{6,4},{7,5},{8,14},{9,15},{10,... | collective-permute-start | bytes 1572872 | tf_op jit(solution)/shard_map/ppermute | solution.py:173
  32.7 4.5 %shard_map.55 = (f32[4,512,128]{2,1,0:T(8,128)}, f32[4,512,256]{2,1,0:T(8,128)}) custom-call(bf16[512,512]{1,0:T(8,128)(2,1)} %q_ref.3, s32[4,128]{1,0:T(4,128)} %bitcast.13, bf16[2,512,128]{2,1,0:T(8,128)(2,1)} %copy-done.2, bf16[2,512,128]{2,1,0:T(8,128)(2,1)} %copy-done.9), custom_call_target="tpu_custom_call" | custom-call | tf_op jit(solution)/shard_map/pallas_call | solution.py:184
  37.2 0.0 collective-permute-done.4.refs_3_
  37.2 0.0 collective-permute-done.6.refs_5_
  37.2 0.7 copy-done.7
  37.9 0.1 copy-done.8
  38.0 6.4 %shard_map.56 = (bf16[8,32,512]{2,1,0:T(8,128)(2,1)}, bf16[8,32,512]{2,1,0:T(8,128)(2,1)}) custom-call(s32[512]{0:T(512)} %doc.1, bf16[512,512]{1,0:T(8,128)(2,1)} %q_ref.3, f32[4,512,128]{2,1,0:T(8,128)} %get-tuple-element.12.m_in, f32[4,512,256]{2,1,0:T(8,128)} %get-tuple-element.13.acc_in, bf16[2,512,128]{2,1,0:T(8,128)(2,1)} %copy-done.4, ...), custom_call_target="tpu_custom_call" | custom-call | tf_op jit(solution)/shard_map/pallas_call | solution.py:197
  44.4 0.6 collective-permute-start.7
  45.0 0.0 collective-permute-done.13
  45.0 9.8 %collective-permute-done.14 = bf16[256,1024]{1,0:T(8,128)(2,1)S(1)} collective-permute-done((bf16[256,1024]{1,0:T(8,128)(2,1)S(1)}, bf16[256,1024]{1,0:T(8,128)(2,1)S(1)}, u32[]{:S(2)}, u32[]{:S(2)}) %collective-permute-start.14) | collective-permute-done | bytes 524320 | tf_op jit(solution)/shard_map/ppermute | solution.py:173
  54.8 0.0 collective-permute-done.15
  54.8 5.0 %collective-permute-done.7.refs_2_ = bf16[8,32,512]{2,1,0:T(8,128)(2,1)S(1)} collective-permute-done((bf16[8,32,512]{2,1,0:T(8,128)(2,1)}, bf16[8,32,512]{2,1,0:T(8,128)(2,1)S(1)}, u32[]{:S(2)}, u32[]{:S(2)}) %collective-permute-start.7) | collective-permute-done | bytes 262176 | tf_op jit(solution)/shard_map/ppermute | solution.py:206
  59.8 0.2 pad_maximum_fusion.refs_9_
  60.0 0.2 collective-permute-start.16
  60.2 0.7 copy-done.11
  60.8 0.7 collective-permute-start.10
  61.5 1.4 %collective-permute-start.8 = (bf16[8,32,512]{2,1,0:T(8,128)(2,1)S(1)}, bf16[8,32,512]{2,1,0:T(8,128)(2,1)S(1)}, u32[]{:S(2)}, u32[]{:S(2)}) collective-permute-start(bf16[8,32,512]{2,1,0:T(8,128)(2,1)S(1)} %copy-done.11), channel_id=1, source_target_pairs={{0,2},{1,3},{2,4},{3,5},{4,6},{5,7},{6,0},{7,1},{8,10},{9,11},{10,... | collective-permute-start | bytes 786440 | tf_op jit(solution)/shard_map/ppermute | solution.py:209
  62.9 1.9 %collective-permute-start.12 = (bf16[8,32,512]{2,1,0:T(8,128)(2,1)S(1)}, bf16[8,32,512]{2,1,0:T(8,128)(2,1)S(1)}, u32[]{:S(2)}, u32[]{:S(2)}) collective-permute-start(bf16[8,32,512]{2,1,0:T(8,128)(2,1)S(1)} %copy-done.10), channel_id=1, source_target_pairs={{0,6},{1,7},{2,0},{3,1},{4,2},{5,3},{6,4},{7,5},{8,14},{9,15},{10,... | collective-permute-start | bytes 786440 | tf_op jit(solution)/shard_map/ppermute | solution.py:208
  64.7 0.2 collective-permute-start.9
  64.9 5.1 %collective-permute-done.10.refs_7_ = bf16[8,32,512]{2,1,0:T(8,128)(2,1)S(1)} collective-permute-done((bf16[8,32,512]{2,1,0:T(8,128)(2,1)S(1)}, bf16[8,32,512]{2,1,0:T(8,128)(2,1)S(1)}, u32[]{:S(2)}, u32[]{:S(2)}) %collective-permute-start.10) | collective-permute-done | bytes 262176 | tf_op jit(solution)/shard_map/ppermute | solution.py:207
  70.0 1.9 %collective-permute-start.11 = (bf16[8,32,512]{2,1,0:T(8,128)(2,1)S(1)}, bf16[8,32,512]{2,1,0:T(8,128)(2,1)S(1)}, u32[]{:S(2)}, u32[]{:S(2)}) collective-permute-start(bf16[8,32,512]{2,1,0:T(8,128)(2,1)S(1)} %collective-permute-done.10.refs_7_), channel_id=1, source_target_pairs={{0,6},{1,7},{2,0},{3,1},{4,2},{5,3},{6,4},{7,5},{8,14},{9,15},{10,... | collective-permute-start | bytes 786440 | tf_op jit(solution)/shard_map/ppermute | solution.py:211
  71.9 0.6 pad_add_fusion.info
  72.4 0.0 collective-permute-done.8.refs_3_
  72.4 3.2 %collective-permute-done.12.refs_6_ = bf16[8,32,512]{2,1,0:T(8,128)(2,1)S(1)} collective-permute-done((bf16[8,32,512]{2,1,0:T(8,128)(2,1)S(1)}, bf16[8,32,512]{2,1,0:T(8,128)(2,1)S(1)}, u32[]{:S(2)}, u32[]{:S(2)}) %collective-permute-start.12) | collective-permute-done | bytes 262176 | tf_op jit(solution)/shard_map/ppermute | solution.py:208
  75.6 0.4 collective-permute-done.9.refs_4_
  76.0 4.4 %collective-permute-done.11.refs_5_ = bf16[8,32,512]{2,1,0:T(8,128)(2,1)S(1)} collective-permute-done((bf16[8,32,512]{2,1,0:T(8,128)(2,1)S(1)}, bf16[8,32,512]{2,1,0:T(8,128)(2,1)S(1)}, u32[]{:S(2)}, u32[]{:S(2)}) %collective-permute-start.11) | collective-permute-done | bytes 262176 | tf_op jit(solution)/shard_map/ppermute | solution.py:211
  80.4 0.6 copy-done.17
  81.1 1.2 %copy-done.1 = bf16[3,256,1024]{2,1,0:T(8,128)(2,1)} copy-done((bf16[3,256,1024]{2,1,0:T(8,128)(2,1)}, bf16[3,256,1024]{2,1,0:T(8,128)(2,1)S(1)}, u32[]{:S(2)}) %copy-start.1) | copy-done | bytes 1572888
  82.2 7.2 %shard_map.57 = bf16[8,64,1024]{2,1,0:T(8,128)(2,1)} custom-call(s32[2]{0:T(128)} %pad_add_fusion.info, bf16[8,32,512]{2,1,0:T(8,128)(2,1)} %get-tuple-element.14.refs_0_, bf16[8,32,512]{2,1,0:T(8,128)(2,1)} %get-tuple-element.15.refs_1_, bf16[8,32,512]{2,1,0:T(8,128)(2,1)} %copy-done.12, bf16[8,32,512]{2,1,0:T(8,128)(2,1)} %copy-done.14, ...), custom_call_target="tpu_custom_call" | custom-call | tf_op jit(solution)/shard_map/pallas_call | solution.py:131
  89.5 21.1 %all_to_all.5.r = bf16[8,64,1024]{2,1,0:T(8,128)(2,1)} all-to-all(bf16[8,64,1024]{2,1,0:T(8,128)(2,1)} %shard_map.57), channel_id=1, replica_groups=mesh['ctx'=32,'head'=8] {'head'}, dimensions={0} | all-to-all | bytes 2097152 | tf_op jit(solution)/shard_map/all_to_all | solution.py:217
  110.6 2.1 %shard_map.58 = bf16[64,4096]{1,0:T(8,128)(2,1)} custom-call(bf16[8,64,1024]{2,1,0:T(8,128)(2,1)} %all_to_all.5.r), custom_call_target="tpu_custom_call" | custom-call | tf_op jit(solution)/shard_map/pallas_call | solution.py:218
  (31 shorter events, 0.1 us)
Async XLA Ops:
  1.0 25.4 %copy-start.2 = (bf16[2,512,128]{2,1,0:T(8,128)(2,1)}, bf16[2,512,128]{2,1,0:T(8,128)(2,1)S(1)}, u32[]{:S(2)}) copy-start(bf16[2,512,128]{2,1,0:T(8,128)(2,1)S(1)} %pad_maximum_fusion.1.own) | copy-start | bytes 786436
  1.0 9.9 %collective-permute-start.3 = (bf16[2,512,128]{2,1,0:T(8,128)(2,1)S(1)}, bf16[2,512,128]{2,1,0:T(8,128)(2,1)S(1)}, u32[]{:S(2)}, u32[]{:S(2)}) collective-permute-start(bf16[2,512,128]{2,1,0:T(8,128)(2,1)S(1)} %pad_maximum_fusion.1.own), channel_id=1, source_target_pairs={{0,32},{8,40},{16,48},{24,56},{32,64},{40,72},{48,80},{56,88},{64,... | collective-permute-start | bytes 786440 | tf_op jit(solution)/shard_map/ppermute | solution.py:165
  3.9 20.9 %collective-permute-start.1 = (bf16[2,512,128]{2,1,0:T(8,128)(2,1)S(1)}, bf16[2,512,128]{2,1,0:T(8,128)(2,1)S(1)}, u32[]{:S(2)}, u32[]{:S(2)}) collective-permute-start(bf16[2,512,128]{2,1,0:T(8,128)(2,1)S(1)} %pad_maximum_fusion.1.own), channel_id=1, source_target_pairs={{0,16},{8,24},{16,64},{24,72},{32,48},{40,56},{48,96},{56,104},{64... | collective-permute-start | bytes 786440 | tf_op jit(solution)/shard_map/ppermute | solution.py:167
  10.9 17.1 %copy-start.3 = (bf16[2,512,128]{2,1,0:T(8,128)(2,1)}, bf16[2,512,128]{2,1,0:T(8,128)(2,1)S(1)}, u32[]{:S(2)}) copy-start(bf16[2,512,128]{2,1,0:T(8,128)(2,1)S(1)} %collective-permute-done.3.refs_2_) | copy-start | bytes 786436
  11.0 17.2 %collective-permute-start.5 = (bf16[2,512,128]{2,1,0:T(8,128)(2,1)S(1)}, bf16[2,512,128]{2,1,0:T(8,128)(2,1)S(1)}, u32[]{:S(2)}, u32[]{:S(2)}) collective-permute-start(bf16[2,512,128]{2,1,0:T(8,128)(2,1)S(1)} %collective-permute-done.3.refs_2_), channel_id=1, source_target_pairs={{0,16},{8,24},{16,0},{24,8},{32,48},{40,56},{48,32},{56,40},{64,80... | collective-permute-start | bytes 786440 | tf_op jit(solution)/shard_map/ppermute | solution.py:192
  17.7 10.9 %collective-permute-start = (bf16[2,512,128]{2,1,0:T(8,128)(2,1)S(1)}, bf16[2,512,128]{2,1,0:T(8,128)(2,1)S(1)}, u32[]{:S(2)}, u32[]{:S(2)}) collective-permute-start(bf16[2,512,128]{2,1,0:T(8,128)(2,1)S(1)} %pad_maximum_fusion.1.own), channel_id=1, source_target_pairs={{0,8},{8,0},{16,24},{24,16},{32,40},{40,32},{48,56},{56,48},{64,72... | collective-permute-start | bytes 786440 | tf_op jit(solution)/shard_map/ppermute | solution.py:168
  24.9 1.6 %copy-start.4 = (bf16[2,512,128]{2,1,0:T(8,128)(2,1)}, bf16[2,512,128]{2,1,0:T(8,128)(2,1)S(1)}, u32[]{:S(2)}) copy-start(bf16[2,512,128]{2,1,0:T(8,128)(2,1)S(1)} %collective-permute-done.1.refs_0_) | copy-start | bytes 786436
  24.9 6.4 %collective-permute-start.2 = (bf16[2,512,128]{2,1,0:T(8,128)(2,1)S(1)}, bf16[2,512,128]{2,1,0:T(8,128)(2,1)S(1)}, u32[]{:S(2)}, u32[]{:S(2)}) collective-permute-start(bf16[2,512,128]{2,1,0:T(8,128)(2,1)S(1)} %collective-permute-done.1.refs_0_), channel_id=1, source_target_pairs={{0,8},{8,0},{16,24},{24,16},{32,40},{40,32},{48,56},{56,48},{64,72... | collective-permute-start | bytes 786440 | tf_op jit(solution)/shard_map/ppermute | solution.py:193
  26.5 18.6 %collective-permute-start.13 = (bf16[256,1024]{1,0:T(8,128)(2,1)S(1)}, bf16[256,1024]{1,0:T(8,128)(2,1)S(1)}, u32[]{:S(2)}, u32[]{:S(2)}) collective-permute-start(bf16[256,1024]{1,0:T(8,128)(2,1)S(1)} %get-tuple-element.21), channel_id=1, source_target_pairs={{0,2},{1,3},{2,4},{3,5},{4,6},{5,7},{6,0},{7,1},{8,10},{9,11},{10,... | collective-permute-start | bytes 1572872 | tf_op jit(solution)/shard_map/ppermute | solution.py:173
  28.0 9.2 %collective-permute-start.4 = (bf16[2,512,128]{2,1,0:T(8,128)(2,1)S(1)}, bf16[2,512,128]{2,1,0:T(8,128)(2,1)S(1)}, u32[]{:S(2)}, u32[]{:S(2)}) collective-permute-start(bf16[2,512,128]{2,1,0:T(8,128)(2,1)S(1)} %collective-permute-done.3.refs_2_), channel_id=1, source_target_pairs={{0,8},{8,0},{16,24},{24,16},{32,40},{40,32},{48,56},{56,48},{64,72... | collective-permute-start | bytes 786440 | tf_op jit(solution)/shard_map/ppermute | solution.py:194
  28.2 9.1 %copy-start.5 = (bf16[2,512,128]{2,1,0:T(8,128)(2,1)}, bf16[2,512,128]{2,1,0:T(8,128)(2,1)S(1)}, u32[]{:S(2)}) copy-start(bf16[2,512,128]{2,1,0:T(8,128)(2,1)S(1)} %collective-permute-done.5.refs_4_) | copy-start | bytes 786436
  28.2 9.0 %collective-permute-start.6 = (bf16[2,512,128]{2,1,0:T(8,128)(2,1)S(1)}, bf16[2,512,128]{2,1,0:T(8,128)(2,1)S(1)}, u32[]{:S(2)}, u32[]{:S(2)}) collective-permute-start(bf16[2,512,128]{2,1,0:T(8,128)(2,1)S(1)} %collective-permute-done.5.refs_4_), channel_id=1, source_target_pairs={{0,8},{8,0},{16,24},{24,16},{32,40},{40,32},{48,56},{56,48},{64,72... | collective-permute-start | bytes 786440 | tf_op jit(solution)/shard_map/ppermute | solution.py:195
  28.6 4.2 %copy-start.9 = (bf16[2,512,128]{2,1,0:T(8,128)(2,1)}, bf16[2,512,128]{2,1,0:T(8,128)(2,1)S(1)}, u32[]{:S(2)}) copy-start(bf16[2,512,128]{2,1,0:T(8,128)(2,1)S(1)} %collective-permute-done.partner) | copy-start | bytes 786436
  28.6 26.3 %collective-permute-start.14 = (bf16[256,1024]{1,0:T(8,128)(2,1)S(1)}, bf16[256,1024]{1,0:T(8,128)(2,1)S(1)}, u32[]{:S(2)}, u32[]{:S(2)}) collective-permute-start(bf16[256,1024]{1,0:T(8,128)(2,1)S(1)} %get-tuple-element.20), channel_id=1, source_target_pairs={{0,4},{1,5},{2,6},{3,7},{4,0},{5,1},{6,2},{7,3},{8,12},{9,13},{10,... | collective-permute-start | bytes 1572872 | tf_op jit(solution)/shard_map/ppermute | solution.py:173
  31.3 6.0 %copy-start.6 = (bf16[2,512,128]{2,1,0:T(8,128)(2,1)}, bf16[2,512,128]{2,1,0:T(8,128)(2,1)S(1)}, u32[]{:S(2)}) copy-start(bf16[2,512,128]{2,1,0:T(8,128)(2,1)S(1)} %collective-permute-done.2.refs_1_) | copy-start | bytes 786436
  31.3 23.5 %collective-permute-start.15 = (bf16[256,1024]{1,0:T(8,128)(2,1)S(1)}, bf16[256,1024]{1,0:T(8,128)(2,1)S(1)}, u32[]{:S(2)}, u32[]{:S(2)}) collective-permute-start(bf16[256,1024]{1,0:T(8,128)(2,1)S(1)} %get-tuple-element.19), channel_id=1, source_target_pairs={{0,6},{1,7},{2,0},{3,1},{4,2},{5,3},{6,4},{7,5},{8,14},{9,15},{10,... | collective-permute-start | bytes 1572872 | tf_op jit(solution)/shard_map/ppermute | solution.py:173
  37.2 0.7 copy-start.7
  37.2 0.8 copy-start.8
  44.4 15.4 %collective-permute-start.7 = (bf16[8,32,512]{2,1,0:T(8,128)(2,1)}, bf16[8,32,512]{2,1,0:T(8,128)(2,1)S(1)}, u32[]{:S(2)}, u32[]{:S(2)}) collective-permute-start(bf16[8,32,512]{2,1,0:T(8,128)(2,1)} %get-tuple-element.14.refs_0_), channel_id=1, source_target_pairs={{0,2},{1,3},{2,4},{3,5},{4,6},{5,7},{6,0},{7,1},{8,10},{9,11},{10,... | collective-permute-start | bytes 786440 | tf_op jit(solution)/shard_map/ppermute | solution.py:206
  59.8 4.9 %copy-start.12 = (bf16[8,32,512]{2,1,0:T(8,128)(2,1)}, bf16[8,32,512]{2,1,0:T(8,128)(2,1)S(1)}, u32[]{:S(2)}) copy-start(bf16[8,32,512]{2,1,0:T(8,128)(2,1)S(1)} %collective-permute-done.7.refs_2_) | copy-start | bytes 786436
  59.8 1.0 copy-start.11
  59.8 3.1 %copy-start.10 = (bf16[8,32,512]{2,1,0:T(8,128)(2,1)S(1)}, bf16[8,32,512]{2,1,0:T(8,128)(2,1)}, u32[]{:S(2)}) copy-start(bf16[8,32,512]{2,1,0:T(8,128)(2,1)} %get-tuple-element.14.refs_0_) | copy-start | bytes 786436
  60.0 20.4 %copy-start = (bf16[3,256,1024]{2,1,0:T(8,128)(2,1)}, bf16[3,256,1024]{2,1,0:T(8,128)(2,1)S(1)}, u32[]{:S(2)}) copy-start(bf16[3,256,1024]{2,1,0:T(8,128)(2,1)S(1)} %pad_maximum_fusion.refs_9_) | copy-start | bytes 4718596
  60.0 20.4 %collective-permute-start.16 = (bf16[3,256,1024]{2,1,0:T(8,128)(2,1)S(1)}, bf16[3,256,1024]{2,1,0:T(8,128)(2,1)S(1)}, u32[]{:S(2)}, u32[]{:S(2)}) collective-permute-start(bf16[3,256,1024]{2,1,0:T(8,128)(2,1)S(1)} %pad_maximum_fusion.refs_9_), channel_id=1, source_target_pairs={{0,8},{8,0},{16,24},{24,16},{32,40},{40,32},{48,56},{56,48},{64,72... | collective-permute-start | bytes 4718600 | tf_op jit(solution)/shard_map/ppermute | solution.py:213
  60.8 9.2 %collective-permute-start.10 = (bf16[8,32,512]{2,1,0:T(8,128)(2,1)S(1)}, bf16[8,32,512]{2,1,0:T(8,128)(2,1)S(1)}, u32[]{:S(2)}, u32[]{:S(2)}) collective-permute-start(bf16[8,32,512]{2,1,0:T(8,128)(2,1)S(1)} %copy-done.11), channel_id=1, source_target_pairs={{0,6},{1,7},{2,0},{3,1},{4,2},{5,3},{6,4},{7,5},{8,14},{9,15},{10,... | collective-permute-start | bytes 786440 | tf_op jit(solution)/shard_map/ppermute | solution.py:207
  61.5 11.0 %collective-permute-start.8 = (bf16[8,32,512]{2,1,0:T(8,128)(2,1)S(1)}, bf16[8,32,512]{2,1,0:T(8,128)(2,1)S(1)}, u32[]{:S(2)}, u32[]{:S(2)}) collective-permute-start(bf16[8,32,512]{2,1,0:T(8,128)(2,1)S(1)} %copy-done.11), channel_id=1, source_target_pairs={{0,2},{1,3},{2,4},{3,5},{4,6},{5,7},{6,0},{7,1},{8,10},{9,11},{10,... | collective-permute-start | bytes 786440 | tf_op jit(solution)/shard_map/ppermute | solution.py:209
  62.9 12.8 %collective-permute-start.12 = (bf16[8,32,512]{2,1,0:T(8,128)(2,1)S(1)}, bf16[8,32,512]{2,1,0:T(8,128)(2,1)S(1)}, u32[]{:S(2)}, u32[]{:S(2)}) collective-permute-start(bf16[8,32,512]{2,1,0:T(8,128)(2,1)S(1)} %copy-done.10), channel_id=1, source_target_pairs={{0,6},{1,7},{2,0},{3,1},{4,2},{5,3},{6,4},{7,5},{8,14},{9,15},{10,... | collective-permute-start | bytes 786440 | tf_op jit(solution)/shard_map/ppermute | solution.py:208
  64.7 11.3 %collective-permute-start.9 = (bf16[8,32,512]{2,1,0:T(8,128)(2,1)S(1)}, bf16[8,32,512]{2,1,0:T(8,128)(2,1)S(1)}, u32[]{:S(2)}, u32[]{:S(2)}) collective-permute-start(bf16[8,32,512]{2,1,0:T(8,128)(2,1)S(1)} %collective-permute-done.7.refs_2_), channel_id=1, source_target_pairs={{0,2},{1,3},{2,4},{3,5},{4,6},{5,7},{6,0},{7,1},{8,10},{9,11},{10,... | collective-permute-start | bytes 786440 | tf_op jit(solution)/shard_map/ppermute | solution.py:210
  70.0 10.4 %copy-start.13 = (bf16[8,32,512]{2,1,0:T(8,128)(2,1)}, bf16[8,32,512]{2,1,0:T(8,128)(2,1)S(1)}, u32[]{:S(2)}) copy-start(bf16[8,32,512]{2,1,0:T(8,128)(2,1)S(1)} %collective-permute-done.10.refs_7_) | copy-start | bytes 786436
  70.0 10.4 %collective-permute-start.11 = (bf16[8,32,512]{2,1,0:T(8,128)(2,1)S(1)}, bf16[8,32,512]{2,1,0:T(8,128)(2,1)S(1)}, u32[]{:S(2)}, u32[]{:S(2)}) collective-permute-start(bf16[8,32,512]{2,1,0:T(8,128)(2,1)S(1)} %collective-permute-done.10.refs_7_), channel_id=1, source_target_pairs={{0,6},{1,7},{2,0},{3,1},{4,2},{5,3},{6,4},{7,5},{8,14},{9,15},{10,... | collective-permute-start | bytes 786440 | tf_op jit(solution)/shard_map/ppermute | solution.py:211
  72.4 8.0 %copy-start.14 = (bf16[8,32,512]{2,1,0:T(8,128)(2,1)}, bf16[8,32,512]{2,1,0:T(8,128)(2,1)S(1)}, u32[]{:S(2)}) copy-start(bf16[8,32,512]{2,1,0:T(8,128)(2,1)S(1)} %collective-permute-done.8.refs_3_) | copy-start | bytes 786436
  75.6 4.8 %copy-start.15 = (bf16[8,32,512]{2,1,0:T(8,128)(2,1)}, bf16[8,32,512]{2,1,0:T(8,128)(2,1)S(1)}, u32[]{:S(2)}) copy-start(bf16[8,32,512]{2,1,0:T(8,128)(2,1)S(1)} %collective-permute-done.12.refs_6_) | copy-start | bytes 786436
  76.0 4.4 %copy-start.16 = (bf16[8,32,512]{2,1,0:T(8,128)(2,1)}, bf16[8,32,512]{2,1,0:T(8,128)(2,1)S(1)}, u32[]{:S(2)}) copy-start(bf16[8,32,512]{2,1,0:T(8,128)(2,1)S(1)} %collective-permute-done.9.refs_4_) | copy-start | bytes 786436
  80.4 0.7 copy-start.17
  81.1 1.2 %copy-start.1 = (bf16[3,256,1024]{2,1,0:T(8,128)(2,1)}, bf16[3,256,1024]{2,1,0:T(8,128)(2,1)S(1)}, u32[]{:S(2)}) copy-start(bf16[3,256,1024]{2,1,0:T(8,128)(2,1)S(1)} %collective-permute-done.16.refs_10_) | copy-start | bytes 4718596

commit v3 on v2

v3 whole, which is shorter than its diff:
```python
import jax
import jax.numpy as jnp
from jax import lax
from jax.experimental import pallas as pl
from jax.experimental.pallas import tpu as pltpu
from jax.sharding import PartitionSpec as P


HD = 128
GROUP = 4
NHEAD = 8
OUT_STEPS = 4
NEG = -1.0e30
SCALE2 = HD ** -0.5 * 1.4426950408889634
F32 = jnp.float32
BF16 = jnp.bfloat16


VMEM = pl.BlockSpec(memory_space=pltpu.VMEM)
SMEM = pl.BlockSpec(memory_space=pltpu.SMEM)
PARAMS = pltpu.CompilerParams(vmem_limit_bytes=56 << 20)


def visit(q_ref, k, v, ok, m_sc, acc_sc, first):
    rows = q_ref.shape[0]
    v = jnp.concatenate([v, jnp.ones_like(v)], axis=1)
    scores = [
        lax.dot_general(
            q_ref[:, g * HD:(g + 1) * HD], k, (((1,), (1,)), ((), ())), preferred_element_type=F32
        )
        for g in range(GROUP)
    ]
    for g, s in enumerate(scores):
        if ok is not None:
            s = jnp.where(ok, s, NEG)
        top = jnp.max(s, axis=1, keepdims=True)
        if first:
            m_new = jnp.broadcast_to(top, (rows, HD))
        else:
            m_old = m_sc[g]
            m_new = jnp.maximum(m_old, top)
        base = m_new * SCALE2
        p = jnp.exp2(s * SCALE2 - jnp.tile(base, (1, s.shape[1] // HD)))
        pv = jnp.dot(p.astype(BF16), v, preferred_element_type=F32)
        if first:
            acc_sc[g] = pv
        else:
            factor = jnp.exp2(m_old * SCALE2 - base)
            acc_sc[g] = acc_sc[g] * jnp.tile(factor, (1, 2)) + pv
        m_sc[g] = m_new


def own_kernel(q_ref, doc_ref, own, partner, m_ref, acc_ref):
    rows = q_ref.shape[0]
    ctx = lax.axis_index("ctx")
    r = lax.broadcasted_iota(jnp.int32, (rows, rows), 0)
    c = lax.broadcasted_iota(jnp.int32, (rows, rows), 1)
    groups, lanes = doc_ref.shape
    doc = jnp.concatenate([
        jnp.broadcast_to(doc_ref[i:i + 1], (lanes, lanes)).T for i in range(groups)
    ]) - ctx * rows
    doc = jnp.tile(doc, (1, rows // lanes))
    visit(q_ref, own[0], own[1], (c >= doc) & (c <= r), m_ref, acc_ref, True)

    @pl.when(lax.rem(ctx, 2) == 1)
    def _():
        visit(q_ref, partner[0], partner[1], c - rows >= doc, m_ref, acc_ref, False)


def rest_kernel(doc, q_ref, m_in, acc_in, *refs):
    blocks, (w_hbm, o_hbm, m_sc, acc_sc, w_sc, a_sc, o_sc, w_sem, o_sem) = refs[:6], refs[6:]
    load = pltpu.make_async_copy(w_hbm, w_sc, w_sem)
    load.start()
    m_sc[...] = m_in[...]
    acc_sc[...] = acc_in[...]
    cell = lax.div(lax.axis_index("ctx"), 2)
    odd = lax.rem(cell, 2)
    size = 2 * q_ref.shape[0]
    for i, other in enumerate((cell - 3 + 2 * odd, cell - 2, cell - 1 - 2 * odd)):
        a, b = blocks[2 * i:2 * i + 2]

        @pl.when((other >= 0) & (other * size >= doc[0]))
        def _(a=a, b=b):
            k = jnp.concatenate([a[0], b[0]], axis=0)
            v = jnp.concatenate([a[1], b[1]], axis=0)
            visit(q_ref, k, v, None, m_sc, acc_sc, False)

    for g in range(GROUP):
        acc = acc_sc[g]
        a_sc[:, g * HD:(g + 1) * HD] = (acc[:, :HD] / acc[:, HD:]).astype(BF16)
    load.wait()
    step = o_sc.shape[2] // OUT_STEPS
    stores = []
    for n in range(OUT_STEPS):
        cols = slice(n * step, (n + 1) * step)
        part = jnp.dot(a_sc[...], w_sc[:, cols], preferred_element_type=F32).astype(BF16)
        o_sc[:, :, cols] = part.reshape(NHEAD, -1, step)
        stores.append(pltpu.make_async_copy(o_sc.at[:, :, cols], o_hbm.at[:, :, cols], o_sem.at[n]))
        stores[-1].start()
    for store in stores:
        store.wait()


def finish_kernel(r, o_ref):
    total = r[0].astype(F32)
    for h in range(1, NHEAD):
        total = total + r[h].astype(F32)
    o_ref[...] = total.astype(BF16)


def on_device(queries, keys, values, doc_start, out_weight):
    rows = queries.shape[0]
    n_ctx = lax.axis_size("ctx")
    swap = [(c, c ^ 1) for c in range(n_ctx)]
    own = jnp.stack([keys, values])

    near = lax.ppermute(own, "ctx", [(c, c + 4) for c in range(n_ctx - 4)])
    jump = [(c, c + (6 if c // 2 % 2 else 2)) for c in range(n_ctx)]
    far = lax.ppermute(own, "ctx", [(c, t) for c, t in jump if t < n_ctx])
    partner = lax.ppermute(own, "ctx", swap)

    state = (
        jax.ShapeDtypeStruct((GROUP, rows, HD), F32),
        jax.ShapeDtypeStruct((GROUP, rows, 2 * HD), F32),
    )
    m, acc = pl.pallas_call(
        own_kernel,
        out_shape=state,
        in_specs=[VMEM] * 4,
        out_specs=[VMEM] * 2,
        compiler_params=PARAMS,
    )(queries, doc_start.reshape(-1, HD), own, partner)

    cross = lax.ppermute(near, "ctx", [(c, c ^ 2) for c in range(n_ctx)])
    far_o = lax.ppermute(far, "ctx", swap)
    near_o = lax.ppermute(near, "ctx", swap)
    cross_o = lax.ppermute(cross, "ctx", swap)
    width = out_weight.shape[1]
    partial = (NHEAD, rows // NHEAD, width)
    anywhere = pl.BlockSpec(memory_space=pl.ANY)
    mixed = pl.pallas_call(
        rest_kernel,
        out_shape=jax.ShapeDtypeStruct(partial, BF16),
        in_specs=[SMEM] + [VMEM] * 9 + [anywhere],
        out_specs=anywhere,
        scratch_shapes=[pltpu.VMEM(t.shape, t.dtype) for t in state] + [
            pltpu.VMEM(out_weight.shape, BF16),
            pltpu.VMEM((rows, GROUP * HD), BF16),
            pltpu.VMEM(partial, BF16),
            pltpu.SemaphoreType.DMA,
            pltpu.SemaphoreType.DMA((OUT_STEPS,)),
        ],
        compiler_params=PARAMS,
    )(doc_start, queries, m, acc, far, far_o, near, near_o, cross, cross_o, out_weight)
    received = lax.all_to_all(mixed, "head", 0, 0)
    step = width // OUT_STEPS
    return pl.pallas_call(
        finish_kernel,
        grid=(OUT_STEPS,),
        out_shape=jax.ShapeDtypeStruct(partial[1:], BF16),
        in_specs=[pl.BlockSpec(partial[:2] + (step,), lambda n: (0, 0, n))],
        out_specs=pl.BlockSpec((partial[1], step), lambda n: (0, n)),
    )(received)


def solution(mesh):
    return jax.shard_map(
        on_device,
        mesh=mesh,
        in_specs=(P("ctx", "head"), P("ctx", "head"), P("ctx", "head"), P("ctx"), P("head", None)),
        out_specs=P(("ctx", "head"), None),
        check_vma=False,
    )
```

time: 113 us -> 107 us (0.947)
  the two profiles are of different devices: /device:TPU:160 before, /device:TPU:193 now
where the time goes in v3:
time: 107 us
  blocking collectives  56.2 us (53%)
  Pallas kernels  24.7 us (23%)
  starting transfers between devices  20 us (19%)
  waiting for transfers between devices  3.23 us (3%)
  local copies, waits for them, and re-layouts  1.53 us (1%)
    all_to_all x1, blocking collectives, on_device(): received = lax.all_to_all(mixed, 'head', 0, 0)  56.2 us
    pallas_call x1, Pallas kernels, on_device(): pl.pallas_call(rest_kernel, out_shape=jax.ShapeDtypeStruct(partial, BF16)...  14.3 us
    ppermute x1, starting transfers between devices, on_device(): partner = lax.ppermute(own, 'ctx', swap)  8.56 us
    pallas_call x1, Pallas kernels, on_device(): pl.pallas_call(own_kernel, out_shape=state, in_specs=[VMEM] * 4, out_spec...  6.32 us
    pallas_call x1, Pallas kernels, on_device(): pl.pallas_call(finish_kernel, grid=(OUT_STEPS,), out_shape=jax.ShapeDtype...  4.11 us
    ppermute x1, starting transfers between devices, on_device(): cross_o = lax.ppermute(cross, 'ctx', swap)  3.83 us
    ppermute x1, waiting for transfers between devices, on_device(): near = lax.ppermute(own, 'ctx', [(c, c + 4) for c in range(n_ctx - 4)])  3.22 us
    ppermute x1, starting transfers between devices, on_device(): far = lax.ppermute(own, 'ctx', [(c, t) for c, t in jump if t < n_ctx])  3.2 us
  transfers between devices with their start and end apart: 7, of which 1 were waited for; matrix products, arithmetic and copies ran while one was open for 0% of the time, Pallas kernels for 6%

profile of v3, /device:TPU:193, one launch (start us, length us, event | category | flops | bytes accessed | tf_op | source)
XLA Modules:
  0.0 106.8 jit_solution(3075215400963843842)
XLA Ops:
  0.0 1.0 pad_maximum_fusion.own
  1.0 0.0 copy-start
  1.0 2.6 %collective-permute-start.3 = (bf16[2,512,128]{2,1,0:T(8,128)(2,1)S(1)}, bf16[2,512,128]{2,1,0:T(8,128)(2,1)S(1)}, u32[]{:S(2)}, u32[]{:S(2)}) collective-permute-start(bf16[2,512,128]{2,1,0:T(8,128)(2,1)S(1)} %pad_maximum_fusion.own), channel_id=1, source_target_pairs={{0,32},{8,40},{16,48},{24,56},{32,64},{40,72},{48,80},{56,88},{64,... | collective-permute-start | bytes 786440 | tf_op jit(solution)/shard_map/ppermute | solution.py:117
  3.7 3.2 %collective-permute-start.1 = (bf16[2,512,128]{2,1,0:T(8,128)(2,1)S(1)}, bf16[2,512,128]{2,1,0:T(8,128)(2,1)S(1)}, u32[]{:S(2)}, u32[]{:S(2)}) collective-permute-start(bf16[2,512,128]{2,1,0:T(8,128)(2,1)S(1)} %pad_maximum_fusion.own), channel_id=1, source_target_pairs={{0,16},{8,24},{16,64},{24,72},{32,48},{40,56},{48,96},{56,104},{64... | collective-permute-start | bytes 786440 | tf_op jit(solution)/shard_map/ppermute | solution.py:119
  6.9 3.2 %collective-permute-done.3.refs_2_ = bf16[2,512,128]{2,1,0:T(8,128)(2,1)S(1)} collective-permute-done((bf16[2,512,128]{2,1,0:T(8,128)(2,1)S(1)}, bf16[2,512,128]{2,1,0:T(8,128)(2,1)S(1)}, u32[]{:S(2)}, u32[]{:S(2)}) %collective-permute-start.3) | collective-permute-done | bytes 262176 | tf_op jit(solution)/shard_map/ppermute | solution.py:117
  10.1 0.0 copy-start.1
  10.1 1.3 %collective-permute-start.5 = (bf16[2,512,128]{2,1,0:T(8,128)(2,1)S(1)}, bf16[2,512,128]{2,1,0:T(8,128)(2,1)S(1)}, u32[]{:S(2)}, u32[]{:S(2)}) collective-permute-start(bf16[2,512,128]{2,1,0:T(8,128)(2,1)S(1)} %collective-permute-done.3.refs_2_), channel_id=1, source_target_pairs={{0,16},{8,24},{16,0},{24,8},{32,48},{40,56},{48,32},{56,40},{64,80... | collective-permute-start | bytes 786440 | tf_op jit(solution)/shard_map/ppermute | solution.py:134
  11.4 8.6 %collective-permute-start = (bf16[2,512,128]{2,1,0:T(8,128)(2,1)S(1)}, bf16[2,512,128]{2,1,0:T(8,128)(2,1)S(1)}, u32[]{:S(2)}, u32[]{:S(2)}) collective-permute-start(bf16[2,512,128]{2,1,0:T(8,128)(2,1)S(1)} %pad_maximum_fusion.own), channel_id=1, source_target_pairs={{0,8},{8,0},{16,24},{24,16},{32,40},{40,32},{48,56},{56,48},{64,72... | collective-permute-start | bytes 786440 | tf_op jit(solution)/shard_map/ppermute | solution.py:120
  20.0 0.0 collective-permute-start.4
  20.0 0.0 collective-permute-done.1.refs_0_
  20.0 0.0 copy-start.2
  20.0 0.5 collective-permute-start.2
  20.5 0.0 collective-permute-done.5.refs_4_
  20.5 0.0 copy-start.3
  20.5 3.8 %collective-permute-start.6 = (bf16[2,512,128]{2,1,0:T(8,128)(2,1)S(1)}, bf16[2,512,128]{2,1,0:T(8,128)(2,1)S(1)}, u32[]{:S(2)}, u32[]{:S(2)}) collective-permute-start(bf16[2,512,128]{2,1,0:T(8,128)(2,1)S(1)} %collective-permute-done.5.refs_4_), channel_id=1, source_target_pairs={{0,8},{8,0},{16,24},{24,16},{32,40},{40,32},{48,56},{56,48},{64,72... | collective-permute-start | bytes 786440 | tf_op jit(solution)/shard_map/ppermute | solution.py:137
  24.3 0.0 collective-permute-done.partner
  24.3 0.0 copy-start.7
  24.3 0.0 copy-done
  24.3 0.7 copy-done.7
  25.0 6.3 %shard_map.55 = (f32[4,512,128]{2,1,0:T(8,128)}, f32[4,512,256]{2,1,0:T(8,128)}) custom-call(bf16[512,512]{1,0:T(8,128)(2,1)} %q_ref.3, s32[4,128]{1,0:T(4,128)} %bitcast.5, bf16[2,512,128]{2,1,0:T(8,128)(2,1)} %copy-done, bf16[2,512,128]{2,1,0:T(8,128)(2,1)} %copy-done.7), custom_call_target="tpu_custom_call" | custom-call | tf_op jit(solution)/shard_map/pallas_call | solution.py:126
  31.3 0.0 collective-permute-done.4.refs_3_
  31.3 0.0 copy-start.4
  31.3 0.0 collective-permute-done.2.refs_1_
  31.3 0.0 copy-start.5
  31.3 0.0 collective-permute-done.6.refs_5_
  31.4 0.0 copy-start.6
  31.4 0.0 copy-done.1
  31.4 0.0 copy-done.2
  31.4 0.0 copy-done.3
  31.4 0.6 copy-done.4
  32.0 0.1 copy-done.5
  32.1 0.1 copy-done.6
  32.2 14.3 %shard_map.56 = bf16[8,64,4096]{2,1,0:T(8,128)(2,1)} custom-call(s32[512]{0:T(512)} %doc.1, bf16[512,512]{1,0:T(8,128)(2,1)} %q_ref.3, f32[4,512,128]{2,1,0:T(8,128)} %get-tuple-element.7.m_in, f32[4,512,256]{2,1,0:T(8,128)} %get-tuple-element.8.acc_in, bf16[2,512,128]{2,1,0:T(8,128)(2,1)} %copy-done.2, bf16[2,512,128]{2,1,0:T(8,128)(2,1)} %copy-done.5, ...), custom_call_target="tpu_custom_call" | custom-call | tf_op jit(solution)/shard_map/pallas_call | solution.py:141
  46.5 56.2 %all_to_all.5.r = bf16[8,64,4096]{2,1,0:T(8,128)(2,1)} all-to-all(bf16[8,64,4096]{2,1,0:T(8,128)(2,1)} %shard_map.56), channel_id=1, replica_groups=mesh['ctx'=32,'head'=8] {'head'}, dimensions={0} | all-to-all | bytes 8388608 | tf_op jit(solution)/shard_map/all_to_all | solution.py:155
  102.7 4.1 %shard_map.57 = bf16[64,4096]{1,0:T(8,128)(2,1)} custom-call(bf16[8,64,4096]{2,1,0:T(8,128)(2,1)} %all_to_all.5.r), custom_call_target="tpu_custom_call" | custom-call | tf_op jit(solution)/shard_map/pallas_call | solution.py:157
Async XLA Ops:
  1.0 23.3 %copy-start = (bf16[2,512,128]{2,1,0:T(8,128)(2,1)}, bf16[2,512,128]{2,1,0:T(8,128)(2,1)S(1)}, u32[]{:S(2)}) copy-start(bf16[2,512,128]{2,1,0:T(8,128)(2,1)S(1)} %pad_maximum_fusion.own) | copy-start | bytes 786436
  1.0 9.1 %collective-permute-start.3 = (bf16[2,512,128]{2,1,0:T(8,128)(2,1)S(1)}, bf16[2,512,128]{2,1,0:T(8,128)(2,1)S(1)}, u32[]{:S(2)}, u32[]{:S(2)}) collective-permute-start(bf16[2,512,128]{2,1,0:T(8,128)(2,1)S(1)} %pad_maximum_fusion.own), channel_id=1, source_target_pairs={{0,32},{8,40},{16,48},{24,56},{32,64},{40,72},{48,80},{56,88},{64,... | collective-permute-start | bytes 786440 | tf_op jit(solution)/shard_map/ppermute | solution.py:117
  3.7 16.3 %collective-permute-start.1 = (bf16[2,512,128]{2,1,0:T(8,128)(2,1)S(1)}, bf16[2,512,128]{2,1,0:T(8,128)(2,1)S(1)}, u32[]{:S(2)}, u32[]{:S(2)}) collective-permute-start(bf16[2,512,128]{2,1,0:T(8,128)(2,1)S(1)} %pad_maximum_fusion.own), channel_id=1, source_target_pairs={{0,16},{8,24},{16,64},{24,72},{32,48},{40,56},{48,96},{56,104},{64... | collective-permute-start | bytes 786440 | tf_op jit(solution)/shard_map/ppermute | solution.py:119
  10.1 21.3 %copy-start.1 = (bf16[2,512,128]{2,1,0:T(8,128)(2,1)}, bf16[2,512,128]{2,1,0:T(8,128)(2,1)S(1)}, u32[]{:S(2)}) copy-start(bf16[2,512,128]{2,1,0:T(8,128)(2,1)S(1)} %collective-permute-done.3.refs_2_) | copy-start | bytes 786436
  10.1 10.4 %collective-permute-start.5 = (bf16[2,512,128]{2,1,0:T(8,128)(2,1)S(1)}, bf16[2,512,128]{2,1,0:T(8,128)(2,1)S(1)}, u32[]{:S(2)}, u32[]{:S(2)}) collective-permute-start(bf16[2,512,128]{2,1,0:T(8,128)(2,1)S(1)} %collective-permute-done.3.refs_2_), channel_id=1, source_target_pairs={{0,16},{8,24},{16,0},{24,8},{32,48},{40,56},{48,32},{56,40},{64,80... | collective-permute-start | bytes 786440 | tf_op jit(solution)/shard_map/ppermute | solution.py:134
  11.4 12.9 %collective-permute-start = (bf16[2,512,128]{2,1,0:T(8,128)(2,1)S(1)}, bf16[2,512,128]{2,1,0:T(8,128)(2,1)S(1)}, u32[]{:S(2)}, u32[]{:S(2)}) collective-permute-start(bf16[2,512,128]{2,1,0:T(8,128)(2,1)S(1)} %pad_maximum_fusion.own), channel_id=1, source_target_pairs={{0,8},{8,0},{16,24},{24,16},{32,40},{40,32},{48,56},{56,48},{64,72... | collective-permute-start | bytes 786440 | tf_op jit(solution)/shard_map/ppermute | solution.py:120
  20.0 11.4 %collective-permute-start.4 = (bf16[2,512,128]{2,1,0:T(8,128)(2,1)S(1)}, bf16[2,512,128]{2,1,0:T(8,128)(2,1)S(1)}, u32[]{:S(2)}, u32[]{:S(2)}) collective-permute-start(bf16[2,512,128]{2,1,0:T(8,128)(2,1)S(1)} %collective-permute-done.3.refs_2_), channel_id=1, source_target_pairs={{0,8},{8,0},{16,24},{24,16},{32,40},{40,32},{48,56},{56,48},{64,72... | collective-permute-start | bytes 786440 | tf_op jit(solution)/shard_map/ppermute | solution.py:136
  20.0 11.4 %copy-start.2 = (bf16[2,512,128]{2,1,0:T(8,128)(2,1)}, bf16[2,512,128]{2,1,0:T(8,128)(2,1)S(1)}, u32[]{:S(2)}) copy-start(bf16[2,512,128]{2,1,0:T(8,128)(2,1)S(1)} %collective-permute-done.1.refs_0_) | copy-start | bytes 786436
  20.0 11.4 %collective-permute-start.2 = (bf16[2,512,128]{2,1,0:T(8,128)(2,1)S(1)}, bf16[2,512,128]{2,1,0:T(8,128)(2,1)S(1)}, u32[]{:S(2)}, u32[]{:S(2)}) collective-permute-start(bf16[2,512,128]{2,1,0:T(8,128)(2,1)S(1)} %collective-permute-done.1.refs_0_), channel_id=1, source_target_pairs={{0,8},{8,0},{16,24},{24,16},{32,40},{40,32},{48,56},{56,48},{64,72... | collective-permute-start | bytes 786440 | tf_op jit(solution)/shard_map/ppermute | solution.py:135
  20.5 10.9 %copy-start.3 = (bf16[2,512,128]{2,1,0:T(8,128)(2,1)}, bf16[2,512,128]{2,1,0:T(8,128)(2,1)S(1)}, u32[]{:S(2)}) copy-start(bf16[2,512,128]{2,1,0:T(8,128)(2,1)S(1)} %collective-permute-done.5.refs_4_) | copy-start | bytes 786436
  20.5 10.9 %collective-permute-start.6 = (bf16[2,512,128]{2,1,0:T(8,128)(2,1)S(1)}, bf16[2,512,128]{2,1,0:T(8,128)(2,1)S(1)}, u32[]{:S(2)}, u32[]{:S(2)}) collective-permute-start(bf16[2,512,128]{2,1,0:T(8,128)(2,1)S(1)} %collective-permute-done.5.refs_4_), channel_id=1, source_target_pairs={{0,8},{8,0},{16,24},{24,16},{32,40},{40,32},{48,56},{56,48},{64,72... | collective-permute-start | bytes 786440 | tf_op jit(solution)/shard_map/ppermute | solution.py:137
  24.3 0.7 copy-start.7
  31.3 0.7 copy-start.4
  31.3 0.8 copy-start.5
  31.4 0.8 copy-start.6

commit v4 on v2

--- a/solution.py
+++ b/solution.py
@@ -72,7 +72,7 @@
 
 
 def rest_kernel(doc, q_ref, m_in, acc_in, *refs):
-    blocks, (o0, o1, m_sc, acc_sc) = refs[:6], refs[6:]
+    blocks, (o_ref, m_sc, acc_sc) = refs[:6], refs[6:]
     m_sc[...] = m_in[...]
     acc_sc[...] = acc_in[...]
     cell = lax.div(lax.axis_index("ctx"), 2)
@@ -89,68 +89,51 @@
 
     for g in range(GROUP):
         acc = acc_sc[g]
-        out = (acc[:, :HD] / acc[:, HD:]).astype(BF16)
-        out = out.reshape(NHEAD, 2, -1, HD)
-        o0[:, :, g * HD:(g + 1) * HD] = out[:, 0]
-        o1[:, :, g * HD:(g + 1) * HD] = out[:, 1]
+        o_ref[:, g * HD:(g + 1) * HD] = (acc[:, :HD] / acc[:, HD:]).astype(BF16)
 
 
 def project_kernel(info, *refs):
-    left, (w_own, w_mine, w_other, o_ref, a_sc) = refs[:2 * NX], refs[2 * NX:]
+    left, (w_own, w_mine, w_other, o_ref, a_sc) = refs[:NX], refs[NX:]
     depth = w_mine.shape[1]
-    core = info[1]
+    core, part = info[1], info[2]
 
     @pl.when(pl.program_id(0) == 0)
     def _():
-        for d in range(NX):
-            for k in range(2):
-                a = left[2 * d + k]
-                for j, half in enumerate((core, 1 - core) if d else (0, 1)):
-                    part = a[:, :, pl.ds(pl.multiple_of(half * depth, depth), depth)]
-                    part = part.reshape(-1, depth)
-                    rows = part.shape[0]
-                    a_sc[k * rows:(k + 1) * rows, (2 * d + j) * depth:(2 * d + j + 1) * depth] = part
+        for d, a in enumerate(left):
+            for j, half in enumerate((core, 1 - core) if d else (0, 1)):
+                cols = pl.ds(pl.multiple_of(half * depth, depth), depth)
+                a_sc[:, (2 * d + j) * depth:(2 * d + j + 1) * depth] = a[:, part, :, cols].reshape(-1, depth)
 
     total = jnp.dot(a_sc[:, :2 * depth], w_own[...], preferred_element_type=F32)
     for d in range(1, NX):
         for j, w in enumerate((w_mine, w_other)):
             cols = slice((2 * d + j) * depth, (2 * d + j + 1) * depth)
             total = total + jnp.dot(a_sc[:, cols], w[d - 1], preferred_element_type=F32)
-    rows = total.shape[0] // 2
-    for k in range(2):
-        part = total[k * rows:(k + 1) * rows].astype(BF16).reshape(NHEAD, -1, total.shape[1])
-        o_ref[:, k * part.shape[1]:(k + 1) * part.shape[1]] = part
-
-
-def project(info, attended, weight, w_mine, w_other):
-    rows = attended[0].shape[1] * 2
+    o_ref[...] = total.reshape(o_ref.shape).astype(o_ref.dtype)
+
+
+def project(info, attended, weight, w_mine, w_other, dtype):
+    rows = attended[0].shape[2]
     width = w_mine.shape[2]
     steps = 4
     step = width // steps
     mine = pl.BlockSpec((NX - 1, w_mine.shape[1], step), lambda n, info: (0, 0, n))
     return pl.pallas_call(
         project_kernel,
-        out_shape=jax.ShapeDtypeStruct((NHEAD, rows, width), BF16),
+        out_shape=jax.ShapeDtypeStruct((NX, rows, width), dtype),
         grid_spec=pltpu.PrefetchScalarGridSpec(
             num_scalar_prefetch=1,
             grid=(steps,),
-            in_specs=[VMEM] * (2 * NX) + [
+            in_specs=[VMEM] * NX + [
                 pl.BlockSpec((weight.shape[0], step), lambda n, info: (0, info[0] * steps + n)),
                 mine,
                 mine,
             ],
-            out_specs=pl.BlockSpec((NHEAD, rows, step), lambda n, info: (0, 0, n)),
-            scratch_shapes=[pltpu.VMEM((NHEAD * rows, NX * weight.shape[0]), BF16)],
+            out_specs=pl.BlockSpec((NX, rows, step), lambda n, info: (0, 0, n)),
+            scratch_shapes=[pltpu.VMEM((NX * rows, NX * weight.shape[0]), BF16)],
         ),
         compiler_params=PARAMS,
     )(info, *attended, weight, w_mine, w_other)
-
-
-def finish_kernel(r, o_ref):
-    width = r.shape[2]
-    for x in range(NX):
-        both = r[2 * x].astype(F32) + r[2 * x + 1].astype(F32)
-        o_ref[:, x * width:(x + 1) * width] = both.astype(BF16)
 
 
 def on_device(queries, keys, values, doc_start, out_weight):
@@ -158,7 +141,7 @@
     ctx = lax.axis_index("ctx")
     head = lax.axis_index("head")
     n_ctx = lax.axis_size("ctx")
-    core, x = ctx % 2, head // 2
+    core, x, part = ctx % 2, head // 2, head % 2
     swap = [(c, c ^ 1) for c in range(n_ctx)]
     own = jnp.stack([keys, values])
 
@@ -193,34 +176,28 @@
     far_o = lax.ppermute(far, "ctx", swap)
     near_o = lax.ppermute(near, "ctx", swap)
     cross_o = lax.ppermute(cross, "ctx", swap)
-    half = jax.ShapeDtypeStruct((NHEAD, rows // NHEAD // 2, GROUP * HD), BF16)
-    a0, a1 = pl.pallas_call(
+    mine = pl.pallas_call(
         rest_kernel,
-        out_shape=[half] * 2,
+        out_shape=jax.ShapeDtypeStruct((rows, GROUP * HD), BF16),
         in_specs=[SMEM] + [VMEM] * 9,
-        out_specs=[VMEM] * 2,
+        out_specs=VMEM,
         scratch_shapes=[pltpu.VMEM(t.shape, t.dtype) for t in state],
         compiler_params=PARAMS,
     )(doc_start, queries, m, acc, far, far_o, near, near_o, cross, cross_o)
 
-    up0 = lax.ppermute(a0, "head", x_ring(1))
-    down1 = lax.ppermute(a1, "head", x_ring(3))
-    down0 = lax.ppermute(a0, "head", x_ring(3))
-    up1 = lax.ppermute(a1, "head", x_ring(1))
-    across0 = lax.ppermute(up0, "head", x_ring(1))
-    across1 = lax.ppermute(down1, "head", x_ring(3))
-    w_mine = jnp.stack(lax.optimization_barrier((*w_mine, up0))[:-1])
+    gathered = [mine] + [lax.ppermute(mine, "head", x_ring(d)) for d in range(1, NX)]
+    attended = [a.reshape(NX, 2, rows // NHEAD, -1) for a in gathered]
+    w_mine = jnp.stack(lax.optimization_barrier((*w_mine, mine))[:-1])
     w_other = lax.ppermute(w_mine, "ctx", swap)
-    attended = (a0, a1, up0, up1, across0, across1, down0, down1)
-    info = jnp.stack([x, core]).astype(jnp.int32)
-    partial = project(info, attended, out_weight, w_mine, w_other)
-    received = lax.all_to_all(partial, "head", 0, 0)
-    return pl.pallas_call(
-        finish_kernel,
-        out_shape=jax.ShapeDtypeStruct((rows // NHEAD, NX * width), BF16),
-        in_specs=[VMEM],
-        out_specs=VMEM,
-    )(received)
+    info = jnp.stack([x, core, 1 - part, x, core, part]).astype(jnp.int32)
+    weights = (out_weight, w_mine, w_other)
+    give = project(info[:3], attended, *weights, BF16)
+    got = lax.ppermute(give, "head", [(h, h ^ 1) for h in range(NHEAD)])
+    keep = project(info[3:], attended, *weights, F32)
+    mixed = (keep + got.astype(F32)).astype(BF16)
+    groups = [[x * 2 + y for x in range(NX)] for y in range(2)]
+    received = lax.all_to_all(mixed, "head", 0, 0, axis_index_groups=groups)
+    return received.transpose(1, 0, 2).reshape(rows // NHEAD, NX * width)
 
 
 def solution(mesh):

time: 113 us -> 118 us (1.044)
  the two profiles are of different devices: /device:TPU:160 before, /device:TPU:112 now
where the time goes in v4:
time: 118 us
  waiting for transfers between devices  47.2 us (40%)
  starting transfers between devices  28.4 us (24%)
  Pallas kernels  21 us (18%)
  blocking collectives  13.1 us (11%)
  local copies, waits for them, and re-layouts  4.24 us (4%)
  other arithmetic  3.78 us (3%)
    ppermute x3, waiting for transfers between devices, on_device(): lax.ppermute(mine, 'head', x_ring(d))  21.7 us
    all_to_all x1, blocking collectives, on_device(): received = lax.all_to_all(mixed, 'head', 0, 0, axis_index_groups=groups)  13.1 us
    pallas_call x2, Pallas kernels, project(): pl.pallas_call(project_kernel, out_shape=jax.ShapeDtypeStruct((NX, rows,...  12.7 us
    ppermute x3, waiting for transfers between devices, on_device(): lax.ppermute(w, 'head', x_ring(d))  10.7 us
    ppermute x1, starting transfers between devices, on_device(): cross = lax.ppermute(near, 'ctx', [(c, c ^ 2) for c in range(n_ctx)])  8.09 us
    ppermute x1, waiting for transfers between devices, on_device(): got = lax.ppermute(give, 'head', [(h, h ^ 1) for h in range(NHEAD)])  7.58 us
    ppermute x1, waiting for transfers between devices, on_device(): far = lax.ppermute(own, 'ctx', [(c, t) for c, t in jump if t < n_ctx])  7.1 us
    ppermute x3, starting transfers between devices, on_device(): lax.ppermute(w, 'head', x_ring(d))  5.66 us
  transfers between devices with their start and end apart: 15, of which 6 were waited for; matrix products, arithmetic and copies ran while one was open for 2% of the time, Pallas kernels for 12%

profile of v4, /device:TPU:112, one launch (start us, length us, event | category | flops | bytes accessed | tf_op | source)
XLA Modules:
  0.0 117.9 jit_solution(12809186172344562494)
XLA Ops:
  0.0 1.0 pad_maximum_fusion.1.own
  1.0 0.0 copy-start.2
  1.0 3.2 %collective-permute-start.1 = (bf16[2,512,128]{2,1,0:T(8,128)(2,1)S(1)}, bf16[2,512,128]{2,1,0:T(8,128)(2,1)S(1)}, u32[]{:S(2)}, u32[]{:S(2)}) collective-permute-start(bf16[2,512,128]{2,1,0:T(8,128)(2,1)S(1)} %pad_maximum_fusion.1.own), channel_id=1, source_target_pairs={{0,16},{8,24},{16,64},{24,72},{32,48},{40,56},{48,96},{56,104},{64... | collective-permute-start | bytes 786440 | tf_op jit(solution)/shard_map/ppermute | solution.py:150
  4.2 5.0 %collective-permute-start.3 = (bf16[2,512,128]{2,1,0:T(8,128)(2,1)S(1)}, bf16[2,512,128]{2,1,0:T(8,128)(2,1)S(1)}, u32[]{:S(2)}, u32[]{:S(2)}) collective-permute-start(bf16[2,512,128]{2,1,0:T(8,128)(2,1)S(1)} %pad_maximum_fusion.1.own), channel_id=1, source_target_pairs={{0,32},{8,40},{16,48},{24,56},{32,64},{40,72},{48,80},{56,88},{64,... | collective-permute-start | bytes 786440 | tf_op jit(solution)/shard_map/ppermute | solution.py:148
  9.3 0.1 collective-permute-start
  9.4 1.5 %fusion = (bf16[256,1024]{1,0:T(8,128)(2,1)S(1)}, bf16[256,1024]{1,0:T(8,128)(2,1)S(1)}, bf16[256,1024]{1,0:T(8,128)(2,1)S(1)}) fusion(bf16[512,4096]{1,0:T(8,128)(2,1)} %refs_4_.3, s32[]{:T(128)S(6)} %select_n.44, s32[]{:T(128)S(6)} %select_n.50, s32[]{:T(128)S(6)} %select_n.48, s32[]{:T(128)S(6)} %select_n.46), kind=kLoop, calls=%fused_computation.6 | loop fusion | bytes 3145744 | tf_op jit(solution)/shard_map/dynamic_slice | solution.py:158
  10.9 7.1 %collective-permute-done.1.refs_0_ = bf16[2,512,128]{2,1,0:T(8,128)(2,1)S(1)} collective-permute-done((bf16[2,512,128]{2,1,0:T(8,128)(2,1)S(1)}, bf16[2,512,128]{2,1,0:T(8,128)(2,1)S(1)}, u32[]{:S(2)}, u32[]{:S(2)}) %collective-permute-start.1) | collective-permute-done | bytes 262176 | tf_op jit(solution)/shard_map/ppermute | solution.py:150
  18.1 0.0 collective-permute-start.2
  18.1 0.0 collective-permute-done.3.refs_2_
  18.1 0.0 copy-start.5
  18.1 8.1 %collective-permute-start.5 = (bf16[2,512,128]{2,1,0:T(8,128)(2,1)S(1)}, bf16[2,512,128]{2,1,0:T(8,128)(2,1)S(1)}, u32[]{:S(2)}, u32[]{:S(2)}) collective-permute-start(bf16[2,512,128]{2,1,0:T(8,128)(2,1)S(1)} %collective-permute-done.3.refs_2_), channel_id=1, source_target_pairs={{0,16},{8,24},{16,0},{24,8},{32,48},{40,56},{48,32},{56,40},{64,80... | collective-permute-start | bytes 786440 | tf_op jit(solution)/shard_map/ppermute | solution.py:175
  26.2 1.5 %collective-permute-start.10 = (bf16[256,1024]{1,0:T(8,128)(2,1)S(1)}, bf16[256,1024]{1,0:T(8,128)(2,1)S(1)}, u32[]{:S(2)}, u32[]{:S(2)}) collective-permute-start(bf16[256,1024]{1,0:T(8,128)(2,1)S(1)} %get-tuple-element.17), channel_id=1, source_target_pairs={{0,2},{1,3},{2,4},{3,5},{4,6},{5,7},{6,0},{7,1},{8,10},{9,11},{10,... | collective-permute-start | bytes 1572872 | tf_op jit(solution)/shard_map/ppermute | solution.py:156
  27.6 2.7 %collective-permute-start.11 = (bf16[256,1024]{1,0:T(8,128)(2,1)S(1)}, bf16[256,1024]{1,0:T(8,128)(2,1)S(1)}, u32[]{:S(2)}, u32[]{:S(2)}) collective-permute-start(bf16[256,1024]{1,0:T(8,128)(2,1)S(1)} %get-tuple-element.16), channel_id=1, source_target_pairs={{0,4},{1,5},{2,6},{3,7},{4,0},{5,1},{6,2},{7,3},{8,12},{9,13},{10,... | collective-permute-start | bytes 1572872 | tf_op jit(solution)/shard_map/ppermute | solution.py:156
  30.4 0.0 collective-permute-done.partner
  30.4 1.4 %collective-permute-start.12 = (bf16[256,1024]{1,0:T(8,128)(2,1)S(1)}, bf16[256,1024]{1,0:T(8,128)(2,1)S(1)}, u32[]{:S(2)}, u32[]{:S(2)}) collective-permute-start(bf16[256,1024]{1,0:T(8,128)(2,1)S(1)} %get-tuple-element.15), channel_id=1, source_target_pairs={{0,6},{1,7},{2,0},{3,1},{4,2},{5,3},{6,4},{7,5},{8,14},{9,15},{10,... | collective-permute-start | bytes 1572872 | tf_op jit(solution)/shard_map/ppermute | solution.py:156
  31.8 0.0 collective-permute-done.2.refs_1_
  31.8 0.0 collective-permute-start.4
  31.8 0.0 collective-permute-done.5.refs_4_
  31.9 0.5 collective-permute-start.6
  32.3 0.0 copy-done.3
  32.3 4.5 %shard_map.55 = (f32[4,512,128]{2,1,0:T(8,128)}, f32[4,512,256]{2,1,0:T(8,128)}) custom-call(bf16[512,512]{1,0:T(8,128)(2,1)} %q_ref.3, s32[4,128]{1,0:T(4,128)} %bitcast.23, bf16[2,512,128]{2,1,0:T(8,128)(2,1)} %copy-done.2, bf16[2,512,128]{2,1,0:T(8,128)(2,1)} %copy-done.3), custom_call_target="tpu_custom_call" | custom-call | tf_op jit(solution)/shard_map/pallas_call | solution.py:167
  36.8 0.0 collective-permute-done.4.refs_3_
  36.8 0.0 collective-permute-done.6.refs_5_
  36.9 0.7 copy-done.8
  37.5 0.1 copy-done.9
  37.6 3.8 %shard_map.56 = bf16[512,512]{1,0:T(8,128)(2,1)} custom-call(s32[512]{0:T(512)} %doc.1, bf16[512,512]{1,0:T(8,128)(2,1)} %q_ref.3, f32[4,512,128]{2,1,0:T(8,128)} %get-tuple-element.10.m_in, f32[4,512,256]{2,1,0:T(8,128)} %get-tuple-element.11.acc_in, bf16[2,512,128]{2,1,0:T(8,128)(2,1)} %copy-done.4, bf16[2,512,128]{2,1,0:T(8,128)(2,1)} %copy-done.6, ...), custom_call_target="tpu_custom_call" | custom-call | tf_op jit(solution)/shard_map/pallas_call | solution.py:179
  41.4 0.0 collective-permute-done.10
  41.4 10.7 %collective-permute-done.11 = bf16[256,1024]{1,0:T(8,128)(2,1)S(1)} collective-permute-done((bf16[256,1024]{1,0:T(8,128)(2,1)S(1)}, bf16[256,1024]{1,0:T(8,128)(2,1)S(1)}, u32[]{:S(2)}, u32[]{:S(2)}) %collective-permute-start.11) | collective-permute-done | bytes 524320 | tf_op jit(solution)/shard_map/ppermute | solution.py:156
  52.2 0.0 collective-permute-done.12
  52.2 0.2 pad_maximum_fusion.refs_5_
  52.3 0.1 collective-permute-start.13
  52.4 1.4 %collective-permute-start.7 = (bf16[512,512]{1,0:T(8,128)(2,1)}, bf16[512,512]{1,0:T(8,128)(2,1)}, u32[]{:S(2)}, u32[]{:S(2)}) collective-permute-start(bf16[512,512]{1,0:T(8,128)(2,1)} %shard_map.56), channel_id=1, source_target_pairs={{0,2},{1,3},{2,4},{3,5},{4,6},{5,7},{6,0},{7,1},{8,10},{9,11},{10,... | collective-permute-start | bytes 1572872 | tf_op jit(solution)/shard_map/ppermute | solution.py:188
  53.9 2.4 %collective-permute-start.8 = (bf16[512,512]{1,0:T(8,128)(2,1)}, bf16[512,512]{1,0:T(8,128)(2,1)}, u32[]{:S(2)}, u32[]{:S(2)}) collective-permute-start(bf16[512,512]{1,0:T(8,128)(2,1)} %shard_map.56), channel_id=1, source_target_pairs={{0,4},{1,5},{2,6},{3,7},{4,0},{5,1},{6,2},{7,3},{8,12},{9,13},{10,... | collective-permute-start | bytes 1572872 | tf_op jit(solution)/shard_map/ppermute | solution.py:188
  56.2 1.6 %collective-permute-start.9 = (bf16[512,512]{1,0:T(8,128)(2,1)}, bf16[512,512]{1,0:T(8,128)(2,1)}, u32[]{:S(2)}, u32[]{:S(2)}) collective-permute-start(bf16[512,512]{1,0:T(8,128)(2,1)} %shard_map.56), channel_id=1, source_target_pairs={{0,6},{1,7},{2,0},{3,1},{4,2},{5,3},{6,4},{7,5},{8,14},{9,15},{10,... | collective-permute-start | bytes 1572872 | tf_op jit(solution)/shard_map/ppermute | solution.py:188
  57.8 0.6 pad_add_fusion.2.info
  58.4 9.9 %collective-permute-done.7 = bf16[512,512]{1,0:T(8,128)(2,1)} collective-permute-done((bf16[512,512]{1,0:T(8,128)(2,1)}, bf16[512,512]{1,0:T(8,128)(2,1)}, u32[]{:S(2)}, u32[]{:S(2)}) %collective-permute-start.7) | collective-permute-done | bytes 524320 | tf_op jit(solution)/shard_map/ppermute | solution.py:188
  68.4 11.7 %collective-permute-done.8 = bf16[512,512]{1,0:T(8,128)(2,1)} collective-permute-done((bf16[512,512]{1,0:T(8,128)(2,1)}, bf16[512,512]{1,0:T(8,128)(2,1)}, u32[]{:S(2)}, u32[]{:S(2)}) %collective-permute-start.8) | collective-permute-done | bytes 524320 | tf_op jit(solution)/shard_map/ppermute | solution.py:188
  80.0 0.1 collective-permute-done.9
  80.2 0.0 collective-permute-done.13.refs_6_
  80.2 1.1 copy-done.1
  81.3 6.3 %shard_map.58 = bf16[4,64,1024]{2,1,0:T(8,128)(2,1)} custom-call(s32[3]{0:T(128)} %pad_add_fusion.2.info, bf16[4,2,64,512]{3,2,1,0:T(8,128)(2,1)} %bitcast.6.refs_0_, bf16[4,2,64,512]{3,2,1,0:T(8,128)(2,1)} %bitcast.7.refs_1_, bf16[4,2,64,512]{3,2,1,0:T(8,128)(2,1)} %bitcast.8.refs_2_, bf16[4,2,64,512]{3,2,1,0:T(8,128)(2,1)} %bitcast.9.refs_3_, ...), custom_call_target="tpu_custom_call" | custom-call | tf_op jit(solution)/shard_map/pallas_call | solution.py:121
  87.6 0.3 collective-permute-start.14
  88.0 0.7 pad_add_fusion.info
  88.6 6.4 %shard_map.57 = f32[4,64,1024]{2,1,0:T(8,128)} custom-call(s32[3]{0:T(128)} %pad_add_fusion.info, bf16[4,2,64,512]{3,2,1,0:T(8,128)(2,1)} %bitcast.6.refs_0_, bf16[4,2,64,512]{3,2,1,0:T(8,128)(2,1)} %bitcast.7.refs_1_, bf16[4,2,64,512]{3,2,1,0:T(8,128)(2,1)} %bitcast.8.refs_2_, bf16[4,2,64,512]{3,2,1,0:T(8,128)(2,1)} %bitcast.9.refs_3_, ...), custom_call_target="tpu_custom_call" | custom-call | tf_op jit(solution)/shard_map/pallas_call | solution.py:121
  95.0 7.6 %collective-permute-done.14 = bf16[4,64,1024]{2,1,0:T(8,128)(2,1)S(1)} collective-permute-done((bf16[4,64,1024]{2,1,0:T(8,128)(2,1)}, bf16[4,64,1024]{2,1,0:T(8,128)(2,1)S(1)}, u32[]{:S(2)}, u32[]{:S(2)}) %collective-permute-start.14) | collective-permute-done | bytes 524320 | tf_op jit(solution)/shard_map/ppermute | solution.py:195
  102.6 1.4 %add_convert_fusion = bf16[4,64,1024]{2,1,0:T(8,128)(2,1)S(1)} fusion(f32[4,64,1024]{2,1,0:T(8,128)} %shard_map.57, bf16[4,64,1024]{2,1,0:T(8,128)(2,1)S(1)} %collective-permute-done.14), kind=kLoop, calls=%fused_computation.1 | loop fusion | flops 786432 | bytes 2097152 | tf_op jit(solution)/shard_map/convert_element_type | solution.py:197
  104.0 13.1 %all_to_all.5 = bf16[4,64,1024]{2,1,0:T(8,128)(2,1)S(1)} all-to-all(bf16[4,64,1024]{2,1,0:T(8,128)(2,1)S(1)} %add_convert_fusion), channel_id=1, replica_groups={{0,2,4,6},{1,3,5,7},{8,10,12,14},{9,11,13,15},{16,18,20,22},{17,19,21,2..., dimensions={0} | all-to-all | bytes 1048576 | tf_op jit(solution)/shard_map/all_to_all | solution.py:199
  117.0 0.8 copy.7
  (14 shorter events, 0.0 us)
Async XLA Ops:
  1.0 9.9 %copy-start.2 = (bf16[2,512,128]{2,1,0:T(8,128)(2,1)}, bf16[2,512,128]{2,1,0:T(8,128)(2,1)S(1)}, u32[]{:S(2)}) copy-start(bf16[2,512,128]{2,1,0:T(8,128)(2,1)S(1)} %pad_maximum_fusion.1.own) | copy-start | bytes 786436
  1.0 17.0 %collective-permute-start.1 = (bf16[2,512,128]{2,1,0:T(8,128)(2,1)S(1)}, bf16[2,512,128]{2,1,0:T(8,128)(2,1)S(1)}, u32[]{:S(2)}, u32[]{:S(2)}) collective-permute-start(bf16[2,512,128]{2,1,0:T(8,128)(2,1)S(1)} %pad_maximum_fusion.1.own), channel_id=1, source_target_pairs={{0,16},{8,24},{16,64},{24,72},{32,48},{40,56},{48,96},{56,104},{64... | collective-permute-start | bytes 786440 | tf_op jit(solution)/shard_map/ppermute | solution.py:150
  4.2 13.8 %collective-permute-start.3 = (bf16[2,512,128]{2,1,0:T(8,128)(2,1)S(1)}, bf16[2,512,128]{2,1,0:T(8,128)(2,1)S(1)}, u32[]{:S(2)}, u32[]{:S(2)}) collective-permute-start(bf16[2,512,128]{2,1,0:T(8,128)(2,1)S(1)} %pad_maximum_fusion.1.own), channel_id=1, source_target_pairs={{0,32},{8,40},{16,48},{24,56},{32,64},{40,72},{48,80},{56,88},{64,... | collective-permute-start | bytes 786440 | tf_op jit(solution)/shard_map/ppermute | solution.py:148
  9.3 21.1 %collective-permute-start = (bf16[2,512,128]{2,1,0:T(8,128)(2,1)S(1)}, bf16[2,512,128]{2,1,0:T(8,128)(2,1)S(1)}, u32[]{:S(2)}, u32[]{:S(2)}) collective-permute-start(bf16[2,512,128]{2,1,0:T(8,128)(2,1)S(1)} %pad_maximum_fusion.1.own), channel_id=1, source_target_pairs={{0,8},{8,0},{16,24},{24,16},{32,40},{40,32},{48,56},{56,48},{64,72... | collective-permute-start | bytes 786440 | tf_op jit(solution)/shard_map/ppermute | solution.py:151
  18.0 18.8 %copy-start.4 = (bf16[2,512,128]{2,1,0:T(8,128)(2,1)}, bf16[2,512,128]{2,1,0:T(8,128)(2,1)S(1)}, u32[]{:S(2)}) copy-start(bf16[2,512,128]{2,1,0:T(8,128)(2,1)S(1)} %collective-permute-done.1.refs_0_) | copy-start | bytes 786436
  18.1 13.8 %collective-permute-start.2 = (bf16[2,512,128]{2,1,0:T(8,128)(2,1)S(1)}, bf16[2,512,128]{2,1,0:T(8,128)(2,1)S(1)}, u32[]{:S(2)}, u32[]{:S(2)}) collective-permute-start(bf16[2,512,128]{2,1,0:T(8,128)(2,1)S(1)} %collective-permute-done.1.refs_0_), channel_id=1, source_target_pairs={{0,8},{8,0},{16,24},{24,16},{32,40},{40,32},{48,56},{56,48},{64,72... | collective-permute-start | bytes 786440 | tf_op jit(solution)/shard_map/ppermute | solution.py:176
  18.1 18.8 %copy-start.5 = (bf16[2,512,128]{2,1,0:T(8,128)(2,1)}, bf16[2,512,128]{2,1,0:T(8,128)(2,1)S(1)}, u32[]{:S(2)}) copy-start(bf16[2,512,128]{2,1,0:T(8,128)(2,1)S(1)} %collective-permute-done.3.refs_2_) | copy-start | bytes 786436
  18.1 13.8 %collective-permute-start.5 = (bf16[2,512,128]{2,1,0:T(8,128)(2,1)S(1)}, bf16[2,512,128]{2,1,0:T(8,128)(2,1)S(1)}, u32[]{:S(2)}, u32[]{:S(2)}) collective-permute-start(bf16[2,512,128]{2,1,0:T(8,128)(2,1)S(1)} %collective-permute-done.3.refs_2_), channel_id=1, source_target_pairs={{0,16},{8,24},{16,0},{24,8},{32,48},{40,56},{48,32},{56,40},{64,80... | collective-permute-start | bytes 786440 | tf_op jit(solution)/shard_map/ppermute | solution.py:175
  26.2 15.3 %collective-permute-start.10 = (bf16[256,1024]{1,0:T(8,128)(2,1)S(1)}, bf16[256,1024]{1,0:T(8,128)(2,1)S(1)}, u32[]{:S(2)}, u32[]{:S(2)}) collective-permute-start(bf16[256,1024]{1,0:T(8,128)(2,1)S(1)} %get-tuple-element.17), channel_id=1, source_target_pairs={{0,2},{1,3},{2,4},{3,5},{4,6},{5,7},{6,0},{7,1},{8,10},{9,11},{10,... | collective-permute-start | bytes 1572872 | tf_op jit(solution)/shard_map/ppermute | solution.py:156
  27.6 24.5 %collective-permute-start.11 = (bf16[256,1024]{1,0:T(8,128)(2,1)S(1)}, bf16[256,1024]{1,0:T(8,128)(2,1)S(1)}, u32[]{:S(2)}, u32[]{:S(2)}) collective-permute-start(bf16[256,1024]{1,0:T(8,128)(2,1)S(1)} %get-tuple-element.16), channel_id=1, source_target_pairs={{0,4},{1,5},{2,6},{3,7},{4,0},{5,1},{6,2},{7,3},{8,12},{9,13},{10,... | collective-permute-start | bytes 1572872 | tf_op jit(solution)/shard_map/ppermute | solution.py:156
  30.4 2.0 %copy-start.3 = (bf16[2,512,128]{2,1,0:T(8,128)(2,1)}, bf16[2,512,128]{2,1,0:T(8,128)(2,1)S(1)}, u32[]{:S(2)}) copy-start(bf16[2,512,128]{2,1,0:T(8,128)(2,1)S(1)} %collective-permute-done.partner) | copy-start | bytes 786436
  30.4 21.8 %collective-permute-start.12 = (bf16[256,1024]{1,0:T(8,128)(2,1)S(1)}, bf16[256,1024]{1,0:T(8,128)(2,1)S(1)}, u32[]{:S(2)}, u32[]{:S(2)}) collective-permute-start(bf16[256,1024]{1,0:T(8,128)(2,1)S(1)} %get-tuple-element.15), channel_id=1, source_target_pairs={{0,6},{1,7},{2,0},{3,1},{4,2},{5,3},{6,4},{7,5},{8,14},{9,15},{10,... | collective-permute-start | bytes 1572872 | tf_op jit(solution)/shard_map/ppermute | solution.py:156
  31.8 5.0 %copy-start.6 = (bf16[2,512,128]{2,1,0:T(8,128)(2,1)}, bf16[2,512,128]{2,1,0:T(8,128)(2,1)S(1)}, u32[]{:S(2)}) copy-start(bf16[2,512,128]{2,1,0:T(8,128)(2,1)S(1)} %collective-permute-done.2.refs_1_) | copy-start | bytes 786436
  31.8 5.0 %collective-permute-start.4 = (bf16[2,512,128]{2,1,0:T(8,128)(2,1)S(1)}, bf16[2,512,128]{2,1,0:T(8,128)(2,1)S(1)}, u32[]{:S(2)}, u32[]{:S(2)}) collective-permute-start(bf16[2,512,128]{2,1,0:T(8,128)(2,1)S(1)} %collective-permute-done.3.refs_2_), channel_id=1, source_target_pairs={{0,8},{8,0},{16,24},{24,16},{32,40},{40,32},{48,56},{56,48},{64,72... | collective-permute-start | bytes 786440 | tf_op jit(solution)/shard_map/ppermute | solution.py:177
  31.8 5.0 %copy-start.7 = (bf16[2,512,128]{2,1,0:T(8,128)(2,1)}, bf16[2,512,128]{2,1,0:T(8,128)(2,1)S(1)}, u32[]{:S(2)}) copy-start(bf16[2,512,128]{2,1,0:T(8,128)(2,1)S(1)} %collective-permute-done.5.refs_4_) | copy-start | bytes 786436
  31.9 5.0 %collective-permute-start.6 = (bf16[2,512,128]{2,1,0:T(8,128)(2,1)S(1)}, bf16[2,512,128]{2,1,0:T(8,128)(2,1)S(1)}, u32[]{:S(2)}, u32[]{:S(2)}) collective-permute-start(bf16[2,512,128]{2,1,0:T(8,128)(2,1)S(1)} %collective-permute-done.5.refs_4_), channel_id=1, source_target_pairs={{0,8},{8,0},{16,24},{24,16},{32,40},{40,32},{48,56},{56,48},{64,72... | collective-permute-start | bytes 786440 | tf_op jit(solution)/shard_map/ppermute | solution.py:178
  36.8 0.7 copy-start.8
  36.8 0.8 copy-start.9
  52.3 27.8 %copy-start = (bf16[3,256,1024]{2,1,0:T(8,128)(2,1)}, bf16[3,256,1024]{2,1,0:T(8,128)(2,1)S(1)}, u32[]{:S(2)}) copy-start(bf16[3,256,1024]{2,1,0:T(8,128)(2,1)S(1)} %pad_maximum_fusion.refs_5_) | copy-start | bytes 4718596
  52.3 27.8 %collective-permute-start.13 = (bf16[3,256,1024]{2,1,0:T(8,128)(2,1)S(1)}, bf16[3,256,1024]{2,1,0:T(8,128)(2,1)S(1)}, u32[]{:S(2)}, u32[]{:S(2)}) collective-permute-start(bf16[3,256,1024]{2,1,0:T(8,128)(2,1)S(1)} %pad_maximum_fusion.refs_5_), channel_id=1, source_target_pairs={{0,8},{8,0},{16,24},{24,16},{32,40},{40,32},{48,56},{56,48},{64,72... | collective-permute-start | bytes 4718600 | tf_op jit(solution)/shard_map/ppermute | solution.py:191
  52.4 15.9 %collective-permute-start.7 = (bf16[512,512]{1,0:T(8,128)(2,1)}, bf16[512,512]{1,0:T(8,128)(2,1)}, u32[]{:S(2)}, u32[]{:S(2)}) collective-permute-start(bf16[512,512]{1,0:T(8,128)(2,1)} %shard_map.56), channel_id=1, source_target_pairs={{0,2},{1,3},{2,4},{3,5},{4,6},{5,7},{6,0},{7,1},{8,10},{9,11},{10,... | collective-permute-start | bytes 1572872 | tf_op jit(solution)/shard_map/ppermute | solution.py:188
  53.9 26.2 %collective-permute-start.8 = (bf16[512,512]{1,0:T(8,128)(2,1)}, bf16[512,512]{1,0:T(8,128)(2,1)}, u32[]{:S(2)}, u32[]{:S(2)}) collective-permute-start(bf16[512,512]{1,0:T(8,128)(2,1)} %shard_map.56), channel_id=1, source_target_pairs={{0,4},{1,5},{2,6},{3,7},{4,0},{5,1},{6,2},{7,3},{8,12},{9,13},{10,... | collective-permute-start | bytes 1572872 | tf_op jit(solution)/shard_map/ppermute | solution.py:188
  56.2 23.9 %collective-permute-start.9 = (bf16[512,512]{1,0:T(8,128)(2,1)}, bf16[512,512]{1,0:T(8,128)(2,1)}, u32[]{:S(2)}, u32[]{:S(2)}) collective-permute-start(bf16[512,512]{1,0:T(8,128)(2,1)} %shard_map.56), channel_id=1, source_target_pairs={{0,6},{1,7},{2,0},{3,1},{4,2},{5,3},{6,4},{7,5},{8,14},{9,15},{10,... | collective-permute-start | bytes 1572872 | tf_op jit(solution)/shard_map/ppermute | solution.py:188
  80.2 1.1 copy-start.1
  87.6 15.0 %collective-permute-start.14 = (bf16[4,64,1024]{2,1,0:T(8,128)(2,1)}, bf16[4,64,1024]{2,1,0:T(8,128)(2,1)S(1)}, u32[]{:S(2)}, u32[]{:S(2)}) collective-permute-start(bf16[4,64,1024]{2,1,0:T(8,128)(2,1)} %shard_map.58), channel_id=1, source_target_pairs={{0,1},{1,0},{2,3},{3,2},{4,5},{5,4},{6,7},{7,6},{8,9},{9,8},{10,11... | collective-permute-start | bytes 1572872 | tf_op jit(solution)/shard_map/ppermute | solution.py:195

commit v5 on v3

--- a/solution.py
+++ b/solution.py
@@ -9,7 +9,7 @@
 HD = 128
 GROUP = 4
 NHEAD = 8
-OUT_STEPS = 4
+NX = 4
 NEG = -1.0e30
 SCALE2 = HD ** -0.5 * 1.4426950408889634
 F32 = jnp.float32
@@ -68,14 +68,16 @@
 
 
 def rest_kernel(doc, q_ref, m_in, acc_in, *refs):
-    blocks, (w_hbm, o_hbm, m_sc, acc_sc, w_sc, a_sc, o_sc, w_sem, o_sem) = refs[:6], refs[6:]
+    blocks, refs = refs[:6], refs[6:]
+    w_hbm, p_send, p_keep, q_send, q_keep, q_sc, m_sc, acc_sc, w_sc, a_sc, w_sem = refs
     load = pltpu.make_async_copy(w_hbm, w_sc, w_sem)
     load.start()
-    m_sc[...] = m_in[...]
-    acc_sc[...] = acc_in[...]
+    q_sc[...] = q_ref[...].reshape(q_sc.shape)
+    m_sc[...] = m_in[...].reshape(m_sc.shape)
+    acc_sc[...] = acc_in[...].reshape(acc_sc.shape)
     cell = lax.div(lax.axis_index("ctx"), 2)
     odd = lax.rem(cell, 2)
-    size = 2 * q_ref.shape[0]
+    size = blocks[0].shape[1] * 2
     for i, other in enumerate((cell - 3 + 2 * odd, cell - 2, cell - 1 - 2 * odd)):
         a, b = blocks[2 * i:2 * i + 2]
 
@@ -83,29 +85,49 @@
         def _(a=a, b=b):
             k = jnp.concatenate([a[0], b[0]], axis=0)
             v = jnp.concatenate([a[1], b[1]], axis=0)
-            visit(q_ref, k, v, None, m_sc, acc_sc, False)
+            visit(q_sc, k, v, None, m_sc, acc_sc, False)
 
     for g in range(GROUP):
         acc = acc_sc[g]
-        a_sc[:, g * HD:(g + 1) * HD] = (acc[:, :HD] / acc[:, HD:]).astype(BF16)
+        out = (acc[:, :HD] / acc[:, HD:]).astype(BF16)
+        a_sc[:, :, g * HD:(g + 1) * HD] = out.reshape(NX, -1, HD)
     load.wait()
-    step = o_sc.shape[2] // OUT_STEPS
-    stores = []
-    for n in range(OUT_STEPS):
-        cols = slice(n * step, (n + 1) * step)
-        part = jnp.dot(a_sc[...], w_sc[:, cols], preferred_element_type=F32).astype(BF16)
-        o_sc[:, :, cols] = part.reshape(NHEAD, -1, step)
-        stores.append(pltpu.make_async_copy(o_sc.at[:, :, cols], o_hbm.at[:, :, cols], o_sem.at[n]))
-        stores[-1].start()
-    for store in stores:
-        store.wait()
-
-
-def finish_kernel(r, o_ref):
-    total = r[0].astype(F32)
-    for h in range(1, NHEAD):
-        total = total + r[h].astype(F32)
-    o_ref[...] = total.astype(BF16)
+    x = lax.div(lax.axis_index("head"), 2)
+    near, far = lax.bitwise_xor(x, 1), 3 - x
+    half = w_sc.shape[1] // 2
+    step = half // 2
+    for base, order, send, keep in (
+        (0, (near, 3 - near, x, far), p_send, p_keep),
+        (half, (far, lax.bitwise_xor(far, 1), x, near), q_send, q_keep),
+    ):
+        left = jnp.concatenate([a_sc[i] for i in order])
+        for n in range(0, half, step):
+            part = jnp.dot(left, w_sc[:, base + n:base + n + step], preferred_element_type=F32)
+            part = part.astype(BF16).reshape(2, 2, -1, step)
+            send[:, :, n:n + step] = part[0]
+            keep[:, :, n:n + step] = part[1]
+
+
+def halve_kernel(p_got, p_keep, q_got, q_keep, p_send, p_next, q_send, q_next):
+    for got, keep, send, rest in ((p_got, p_keep, p_send, p_next), (q_got, q_keep, q_send, q_next)):
+        rest[...] = (got[0].astype(F32) + keep[0].astype(F32)).astype(BF16)
+        send[...] = (got[1].astype(F32) + keep[1].astype(F32)).astype(BF16)
+
+
+def part_kernel(p_got, p_keep, q_got, q_keep, send, rest):
+    part = lax.rem(lax.axis_index("head"), 2)
+    rows, half = send.shape[0], p_got.shape[1]
+    mine = pl.ds(pl.multiple_of(part * rows, rows), rows)
+    give = pl.ds(pl.multiple_of((1 - part) * rows, rows), rows)
+    for n, got, keep in ((0, p_got, p_keep), (half, q_got, q_keep)):
+        rest[:, n:n + half] = got[mine, :].astype(F32) + keep[mine, :].astype(F32)
+        send[:, n:n + half] = (got[give, :].astype(F32) + keep[give, :].astype(F32)).astype(BF16)
+
+
+def finish_kernel(r0, g0, r1, g1, o_ref):
+    rows = r0.shape[0]
+    for k, (r, g) in enumerate(((r0, g0), (r1, g1))):
+        o_ref[k * rows:(k + 1) * rows, :] = (r[...] + g[...].astype(F32)).astype(BF16)
 
 
 def on_device(queries, keys, values, doc_start, out_weight):
@@ -136,31 +158,58 @@
     near_o = lax.ppermute(near, "ctx", swap)
     cross_o = lax.ppermute(cross, "ctx", swap)
     width = out_weight.shape[1]
-    partial = (NHEAD, rows // NHEAD, width)
-    anywhere = pl.BlockSpec(memory_space=pl.ANY)
-    mixed = pl.pallas_call(
-        rest_kernel,
-        out_shape=jax.ShapeDtypeStruct(partial, BF16),
-        in_specs=[SMEM] + [VMEM] * 9 + [anywhere],
-        out_specs=anywhere,
-        scratch_shapes=[pltpu.VMEM(t.shape, t.dtype) for t in state] + [
-            pltpu.VMEM(out_weight.shape, BF16),
-            pltpu.VMEM((rows, GROUP * HD), BF16),
-            pltpu.VMEM(partial, BF16),
-            pltpu.SemaphoreType.DMA,
-            pltpu.SemaphoreType.DMA((OUT_STEPS,)),
-        ],
-        compiler_params=PARAMS,
-    )(doc_start, queries, m, acc, far, far_o, near, near_o, cross, cross_o, out_weight)
-    received = lax.all_to_all(mixed, "head", 0, 0)
-    step = width // OUT_STEPS
+    half = width // 2
+    block = rows // NHEAD // 2
+    shaped = (queries, m, acc)
+    shaped = [t.reshape(t.shape[:-2] + (NHEAD, 2, block, t.shape[-1])) for t in shaped]
+    to_near = [(h, h ^ 2) for h in range(NHEAD)]
+    to_far = [(h, (3 - h // 2) * 2 + h % 2) for h in range(NHEAD)]
+    to_part = [(h, h ^ 1) for h in range(NHEAD)]
+    vmem = lambda *shapes: [pltpu.VMEM(t, d) for t, d in shapes]
+    quad = jax.ShapeDtypeStruct((2, 2 * block, half), BF16)
+    pair = jax.ShapeDtypeStruct((2 * block, half), BF16)
+
+    def chunk(k):
+        specs = [
+            pl.BlockSpec(t.shape[:-3] + (1,) + t.shape[-2:], lambda i, n=t.ndim: (0,) * (n - 3) + (k, 0, 0))
+            for t in shaped
+        ]
+        p_send, p_keep, q_send, q_keep = pl.pallas_call(
+            rest_kernel,
+            grid=(1,),
+            out_shape=[quad] * 4,
+            in_specs=[SMEM] + specs + [VMEM] * 6 + [pl.BlockSpec(memory_space=pl.ANY)],
+            out_specs=[VMEM] * 4,
+            scratch_shapes=vmem(
+                ((rows // 2, GROUP * HD), BF16),
+                ((GROUP, rows // 2, HD), F32),
+                ((GROUP, rows // 2, 2 * HD), F32),
+                (out_weight.shape, BF16),
+                ((NX, 2 * block, GROUP * HD), BF16),
+            ) + [pltpu.SemaphoreType.DMA],
+            compiler_params=PARAMS,
+        )(doc_start, *shaped, far, far_o, near, near_o, cross, cross_o, out_weight)
+        p_got = lax.ppermute(p_send, "head", to_near)
+        q_got = lax.ppermute(q_send, "head", to_far)
+        p_send, p_keep, q_send, q_keep = pl.pallas_call(
+            halve_kernel, out_shape=[pair] * 4, in_specs=[VMEM] * 4, out_specs=[VMEM] * 4
+        )(p_got, p_keep, q_got, q_keep)
+        p_got = lax.ppermute(p_send, "head", to_far)
+        q_got = lax.ppermute(q_send, "head", to_near)
+        send, rest = pl.pallas_call(
+            part_kernel,
+            out_shape=[jax.ShapeDtypeStruct((block, width), t) for t in (BF16, F32)],
+            in_specs=[VMEM] * 4,
+            out_specs=[VMEM] * 2,
+        )(p_got, p_keep, q_got, q_keep)
+        return rest, lax.ppermute(send, "head", to_part)
+
     return pl.pallas_call(
         finish_kernel,
-        grid=(OUT_STEPS,),
-        out_shape=jax.ShapeDtypeStruct(partial[1:], BF16),
-        in_specs=[pl.BlockSpec(partial[:2] + (step,), lambda n: (0, 0, n))],
-        out_specs=pl.BlockSpec((partial[1], step), lambda n: (0, n)),
-    )(received)
+        out_shape=jax.ShapeDtypeStruct((2 * block, width), BF16),
+        in_specs=[VMEM] * 4,
+        out_specs=VMEM,
+    )(*chunk(0), *chunk(1))
 
 
 def solution(mesh):

time: 107 us -> 98.9 us (0.924)
  the two profiles are of different devices: /device:TPU:193 before, /device:TPU:97 now
where the time goes in v5:
time: 98.9 us; the launch traced here: 98.5 us
  starting transfers between devices  31.8 us (32%)
  Pallas kernels  30.7 us (31%)
  waiting for transfers between devices  29.5 us (30%)
  local copies, waits for them, and re-layouts  5.41 us (5%)
  other arithmetic  0.99 us (1%)
    pallas_call x2, Pallas kernels, chunk(): pl.pallas_call(rest_kernel, grid=(1,), out_shape=[quad] * 4, in_specs=[SM...  12.6 us
    ppermute x2, waiting for transfers between devices, chunk(): return (rest, lax.ppermute(send, 'head', to_part))  6.93 us
    ppermute x2, waiting for transfers between devices, chunk(): p_got = lax.ppermute(p_send, 'head', to_near)  6.39 us
    pallas_call x1, Pallas kernels, on_device(): pl.pallas_call(own_kernel, out_shape=state, in_specs=[VMEM] * 4, out_spec...  6.33 us
    ppermute x1, starting transfers between devices, on_device(): cross = lax.ppermute(near, 'ctx', [(c, c ^ 2) for c in range(n_ctx)])  5.95 us
    ppermute x2, waiting for transfers between devices, chunk(): q_got = lax.ppermute(q_send, 'head', to_far)  5.83 us
    unnamed x36, local copies, waits for them, and re-layouts  5.41 us
    pallas_call x2, Pallas kernels, chunk(): pl.pallas_call(halve_kernel, out_shape=[pair] * 4, in_specs=[VMEM] * 4, o...  5.14 us
  transfers between devices with their start and end apart: 17, of which 9 were waited for; matrix products, arithmetic and copies ran while one was open for 0% of the time, Pallas kernels for 22%

profile of v5, /device:TPU:97, one launch (start us, length us, event | category | flops | bytes accessed | tf_op | source)
XLA Modules:
  0.0 98.5 jit_solution(2457044035110866823)
XLA Ops:
  0.0 1.0 %pad_maximum_fusion.own = bf16[2,512,128]{2,1,0:T(8,128)(2,1)S(1)} fusion(bf16[1,512,128]{2,1,0:T(8,128)(2,1)} %bitcast.12, bf16[1,512,128]{2,1,0:T(8,128)(2,1)} %bitcast.13), kind=kLoop, calls=%fused_computation | loop fusion | flops 131072 | bytes 524288 | tf_op jit(solution)/shard_map/stack | solution.py:137
  1.0 0.0 copy-start.6
  1.0 4.8 %collective-permute-start.3 = (bf16[2,512,128]{2,1,0:T(8,128)(2,1)S(1)}, bf16[2,512,128]{2,1,0:T(8,128)(2,1)S(1)}, u32[]{:S(2)}, u32[]{:S(2)}) collective-permute-start(bf16[2,512,128]{2,1,0:T(8,128)(2,1)S(1)} %pad_maximum_fusion.own), channel_id=1, source_target_pairs={{0,32},{8,40},{16,48},{24,56},{32,64},{40,72},{48,80},{56,88},{64,... | collective-permute-start | bytes 786440 | tf_op jit(solution)/shard_map/ppermute | solution.py:139
  5.8 3.2 %collective-permute-start.1 = (bf16[2,512,128]{2,1,0:T(8,128)(2,1)S(1)}, bf16[2,512,128]{2,1,0:T(8,128)(2,1)S(1)}, u32[]{:S(2)}, u32[]{:S(2)}) collective-permute-start(bf16[2,512,128]{2,1,0:T(8,128)(2,1)S(1)} %pad_maximum_fusion.own), channel_id=1, source_target_pairs={{0,16},{8,24},{16,64},{24,72},{32,48},{40,56},{48,96},{56,104},{64... | collective-permute-start | bytes 786440 | tf_op jit(solution)/shard_map/ppermute | solution.py:141
  9.0 1.8 %collective-permute-done.3.refs_2_ = bf16[2,512,128]{2,1,0:T(8,128)(2,1)S(1)} collective-permute-done((bf16[2,512,128]{2,1,0:T(8,128)(2,1)S(1)}, bf16[2,512,128]{2,1,0:T(8,128)(2,1)S(1)}, u32[]{:S(2)}, u32[]{:S(2)}) %collective-permute-start.3) | collective-permute-done | bytes 262176 | tf_op jit(solution)/shard_map/ppermute | solution.py:139
  10.7 6.0 %collective-permute-start.5 = (bf16[2,512,128]{2,1,0:T(8,128)(2,1)S(1)}, bf16[2,512,128]{2,1,0:T(8,128)(2,1)S(1)}, u32[]{:S(2)}, u32[]{:S(2)}) collective-permute-start(bf16[2,512,128]{2,1,0:T(8,128)(2,1)S(1)} %collective-permute-done.3.refs_2_), channel_id=1, source_target_pairs={{0,16},{8,24},{16,0},{24,8},{32,48},{40,56},{48,32},{56,40},{64,80... | collective-permute-start | bytes 786440 | tf_op jit(solution)/shard_map/ppermute | solution.py:156
  16.7 3.4 %collective-permute-start = (bf16[2,512,128]{2,1,0:T(8,128)(2,1)S(1)}, bf16[2,512,128]{2,1,0:T(8,128)(2,1)S(1)}, u32[]{:S(2)}, u32[]{:S(2)}) collective-permute-start(bf16[2,512,128]{2,1,0:T(8,128)(2,1)S(1)} %pad_maximum_fusion.own), channel_id=1, source_target_pairs={{0,8},{8,0},{16,24},{24,16},{32,40},{40,32},{48,56},{56,48},{64,72... | collective-permute-start | bytes 786440 | tf_op jit(solution)/shard_map/ppermute | solution.py:142
  20.1 0.0 collective-permute-start.4
  20.1 2.6 %collective-permute-done.1.refs_0_ = bf16[2,512,128]{2,1,0:T(8,128)(2,1)S(1)} collective-permute-done((bf16[2,512,128]{2,1,0:T(8,128)(2,1)S(1)}, bf16[2,512,128]{2,1,0:T(8,128)(2,1)S(1)}, u32[]{:S(2)}, u32[]{:S(2)}) %collective-permute-start.1) | collective-permute-done | bytes 262176 | tf_op jit(solution)/shard_map/ppermute | solution.py:141
  22.7 1.0 collective-permute-start.2
  23.6 5.0 %collective-permute-done.5.refs_4_ = bf16[2,512,128]{2,1,0:T(8,128)(2,1)S(1)} collective-permute-done((bf16[2,512,128]{2,1,0:T(8,128)(2,1)S(1)}, bf16[2,512,128]{2,1,0:T(8,128)(2,1)S(1)}, u32[]{:S(2)}, u32[]{:S(2)}) %collective-permute-start.5) | collective-permute-done | bytes 262176 | tf_op jit(solution)/shard_map/ppermute | solution.py:156
  28.6 0.5 collective-permute-start.6
  29.1 0.0 collective-permute-done.partner
  29.1 0.7 copy-done.15
  29.8 6.3 %shard_map.55 = (f32[4,512,128]{2,1,0:T(8,128)}, f32[4,512,256]{2,1,0:T(8,128)}) custom-call(bf16[512,512]{1,0:T(8,128)(2,1)} %q_ref.1, s32[4,128]{1,0:T(4,128)} %bitcast.14, bf16[2,512,128]{2,1,0:T(8,128)(2,1)} %copy-done.6, bf16[2,512,128]{2,1,0:T(8,128)(2,1)} %copy-done.15), custom_call_target="tpu_custom_call" | custom-call | tf_op jit(solution)/shard_map/pallas_call | solution.py:148
  36.2 0.0 collective-permute-done.2.refs_1_
  36.2 0.0 collective-permute-done.6.refs_5_
  36.2 0.7 copy-done.3
  36.9 0.1 copy-done.4
  37.0 0.1 copy-done.5
  37.1 6.3 %shard_map.59 = (bf16[2,64,2048]{2,1,0:T(8,128)(2,1)}, bf16[2,64,2048]{2,1,0:T(8,128)(2,1)}, bf16[2,64,2048]{2,1,0:T(8,128)(2,1)}, bf16[2,64,2048]{2,1,0:T(8,128)(2,1)}) custom-call(s32[512]{0:T(512)} %doc.3, bf16[8,2,32,512]{3,2,1,0:T(8,128)(2,1)} %bitcast.8, f32[4,8,2,32,128]{4,3,2,1,0:T(8,128)} %bitcast.10, f32[4,8,2,32,256]{4,3,2,1,0:T(8,128)} %bitcast.6, ...), custom_call_target="tpu_custom_call" | custom-call | tf_op jit(solution)/shard_map/pallas_call | solution.py:177
  43.4 1.5 %collective-permute-start.12 = (bf16[2,64,2048]{2,1,0:T(8,128)(2,1)}, bf16[2,64,2048]{2,1,0:T(8,128)(2,1)S(1)}, u32[]{:S(2)}, u32[]{:S(2)}) collective-permute-start(bf16[2,64,2048]{2,1,0:T(8,128)(2,1)} %get-tuple-element.39), channel_id=1, source_target_pairs={{0,2},{1,3},{2,0},{3,1},{4,6},{5,7},{6,4},{7,5},{8,10},{9,11},{10,... | collective-permute-start | bytes 1572872 | tf_op jit(solution)/shard_map/ppermute | solution.py:192
  44.9 1.8 %collective-permute-start.13 = (bf16[2,64,2048]{2,1,0:T(8,128)(2,1)}, bf16[2,64,2048]{2,1,0:T(8,128)(2,1)S(1)}, u32[]{:S(2)}, u32[]{:S(2)}) collective-permute-start(bf16[2,64,2048]{2,1,0:T(8,128)(2,1)} %get-tuple-element.41), channel_id=1, source_target_pairs={{0,6},{1,7},{2,4},{3,5},{4,2},{5,3},{6,0},{7,1},{8,14},{9,15},{10,... | collective-permute-start | bytes 1572872 | tf_op jit(solution)/shard_map/ppermute | solution.py:193
  46.7 6.3 %shard_map.56 = (bf16[2,64,2048]{2,1,0:T(8,128)(2,1)}, bf16[2,64,2048]{2,1,0:T(8,128)(2,1)}, bf16[2,64,2048]{2,1,0:T(8,128)(2,1)}, bf16[2,64,2048]{2,1,0:T(8,128)(2,1)}) custom-call(s32[512]{0:T(512)} %doc.3, bf16[8,2,32,512]{3,2,1,0:T(8,128)(2,1)} %bitcast.9, f32[4,8,2,32,128]{4,3,2,1,0:T(8,128)} %bitcast.11, f32[4,8,2,32,256]{4,3,2,1,0:T(8,128)} %bitcast.7, ...), custom_call_target="tpu_custom_call" | custom-call | tf_op jit(solution)/shard_map/pallas_call | solution.py:177
  53.1 0.4 collective-permute-start.7
  53.5 0.6 collective-permute-start.8
  54.1 3.6 %collective-permute-done.12.p_got = bf16[2,64,2048]{2,1,0:T(8,128)(2,1)S(1)} collective-permute-done((bf16[2,64,2048]{2,1,0:T(8,128)(2,1)}, bf16[2,64,2048]{2,1,0:T(8,128)(2,1)S(1)}, u32[]{:S(2)}, u32[]{:S(2)}) %collective-permute-start.12) | collective-permute-done | bytes 524320 | tf_op jit(solution)/shard_map/ppermute | solution.py:192
  57.7 2.5 %collective-permute-done.13.q_got = bf16[2,64,2048]{2,1,0:T(8,128)(2,1)S(1)} collective-permute-done((bf16[2,64,2048]{2,1,0:T(8,128)(2,1)}, bf16[2,64,2048]{2,1,0:T(8,128)(2,1)S(1)}, u32[]{:S(2)}, u32[]{:S(2)}) %collective-permute-start.13) | collective-permute-done | bytes 524320 | tf_op jit(solution)/shard_map/ppermute | solution.py:193
  60.3 0.8 copy-done.10
  61.1 2.6 %shard_map.60 = (bf16[64,2048]{1,0:T(8,128)(2,1)}, bf16[64,2048]{1,0:T(8,128)(2,1)}, bf16[64,2048]{1,0:T(8,128)(2,1)}, bf16[64,2048]{1,0:T(8,128)(2,1)}) custom-call(bf16[2,64,2048]{2,1,0:T(8,128)(2,1)} %copy-done.9, bf16[2,64,2048]{2,1,0:T(8,128)(2,1)} %get-tuple-element.40.p_keep, bf16[2,64,2048]{2,1,0:T(8,128)(2,1)} %copy-done.10, ...), custom_call_target="tpu_custom_call" | custom-call | tf_op jit(solution)/shard_map/pallas_call | solution.py:194
  63.7 1.8 %collective-permute-start.14 = (bf16[64,2048]{1,0:T(8,128)(2,1)}, bf16[64,2048]{1,0:T(8,128)(2,1)S(1)}, u32[]{:S(2)}, u32[]{:S(2)}) collective-permute-start(bf16[64,2048]{1,0:T(8,128)(2,1)} %get-tuple-element.43), channel_id=1, source_target_pairs={{0,6},{1,7},{2,4},{3,5},{4,2},{5,3},{6,0},{7,1},{8,14},{9,15},{10,... | collective-permute-start | bytes 786440 | tf_op jit(solution)/shard_map/ppermute | solution.py:197
  65.5 0.0 collective-permute-start.15
  65.5 2.7 %collective-permute-done.7.p_got = bf16[2,64,2048]{2,1,0:T(8,128)(2,1)S(1)} collective-permute-done((bf16[2,64,2048]{2,1,0:T(8,128)(2,1)}, bf16[2,64,2048]{2,1,0:T(8,128)(2,1)S(1)}, u32[]{:S(2)}, u32[]{:S(2)}) %collective-permute-start.7) | collective-permute-done | bytes 524320 | tf_op jit(solution)/shard_map/ppermute | solution.py:192
  68.2 3.3 %collective-permute-done.8.q_got = bf16[2,64,2048]{2,1,0:T(8,128)(2,1)S(1)} collective-permute-done((bf16[2,64,2048]{2,1,0:T(8,128)(2,1)}, bf16[2,64,2048]{2,1,0:T(8,128)(2,1)S(1)}, u32[]{:S(2)}, u32[]{:S(2)}) %collective-permute-start.8) | collective-permute-done | bytes 524320 | tf_op jit(solution)/shard_map/ppermute | solution.py:193
  71.5 0.8 copy-done.8
  72.3 2.6 %shard_map.57 = (bf16[64,2048]{1,0:T(8,128)(2,1)}, bf16[64,2048]{1,0:T(8,128)(2,1)}, bf16[64,2048]{1,0:T(8,128)(2,1)}, bf16[64,2048]{1,0:T(8,128)(2,1)}) custom-call(bf16[2,64,2048]{2,1,0:T(8,128)(2,1)} %copy-done.7, bf16[2,64,2048]{2,1,0:T(8,128)(2,1)} %get-tuple-element.30.p_keep, bf16[2,64,2048]{2,1,0:T(8,128)(2,1)} %copy-done.8, ...), custom_call_target="tpu_custom_call" | custom-call | tf_op jit(solution)/shard_map/pallas_call | solution.py:194
  74.9 1.8 %collective-permute-start.9 = (bf16[64,2048]{1,0:T(8,128)(2,1)}, bf16[64,2048]{1,0:T(8,128)(2,1)S(1)}, u32[]{:S(2)}, u32[]{:S(2)}) collective-permute-start(bf16[64,2048]{1,0:T(8,128)(2,1)} %get-tuple-element.33), channel_id=1, source_target_pairs={{0,6},{1,7},{2,4},{3,5},{4,2},{5,3},{6,0},{7,1},{8,14},{9,15},{10,... | collective-permute-start | bytes 786440 | tf_op jit(solution)/shard_map/ppermute | solution.py:197
  76.7 0.7 copy-done.11
  77.4 0.1 copy-done.12
  77.5 2.2 %shard_map.61 = (bf16[32,4096]{1,0:T(8,128)(2,1)}, f32[32,4096]{1,0:T(8,128)}) custom-call(bf16[64,2048]{1,0:T(8,128)(2,1)} %copy-done.11, bf16[64,2048]{1,0:T(8,128)(2,1)} %get-tuple-element.44.p_keep, bf16[64,2048]{1,0:T(8,128)(2,1)} %copy-done.12, bf16[64,2048]{1,0:T(8,128)(2,1)} %get-tuple-element.46.q_keep), custom_call_target="tpu_custom_call" | custom-call | tf_op jit(solution)/shard_map/pallas_call | solution.py:199
  79.7 2.6 %collective-permute-start.16 = (bf16[32,4096]{1,0:T(8,128)(2,1)}, bf16[32,4096]{1,0:T(8,128)(2,1)S(1)}, u32[]{:S(2)}, u32[]{:S(2)}) collective-permute-start(bf16[32,4096]{1,0:T(8,128)(2,1)} %get-tuple-element.48), channel_id=1, source_target_pairs={{0,1},{1,0},{2,3},{3,2},{4,5},{5,4},{6,7},{7,6},{8,9},{9,8},{10,11... | collective-permute-start | bytes 786440 | tf_op jit(solution)/shard_map/ppermute | solution.py:205
  82.3 1.0 %collective-permute-done.9.p_got = bf16[64,2048]{1,0:T(8,128)(2,1)S(1)} collective-permute-done((bf16[64,2048]{1,0:T(8,128)(2,1)}, bf16[64,2048]{1,0:T(8,128)(2,1)S(1)}, u32[]{:S(2)}, u32[]{:S(2)}) %collective-permute-start.9) | collective-permute-done | bytes 262176 | tf_op jit(solution)/shard_map/ppermute | solution.py:197
  83.3 0.7 copy-done.14
  84.0 2.2 %shard_map.58 = (bf16[32,4096]{1,0:T(8,128)(2,1)}, f32[32,4096]{1,0:T(8,128)}) custom-call(bf16[64,2048]{1,0:T(8,128)(2,1)} %copy-done.14, bf16[64,2048]{1,0:T(8,128)(2,1)} %get-tuple-element.34.p_keep, bf16[64,2048]{1,0:T(8,128)(2,1)} %copy-done.13, bf16[64,2048]{1,0:T(8,128)(2,1)} %get-tuple-element.36.q_keep), custom_call_target="tpu_custom_call" | custom-call | tf_op jit(solution)/shard_map/pallas_call | solution.py:199
  86.2 2.4 %collective-permute-start.11 = (bf16[32,4096]{1,0:T(8,128)(2,1)}, bf16[32,4096]{1,0:T(8,128)(2,1)S(1)}, u32[]{:S(2)}, u32[]{:S(2)}) collective-permute-start(bf16[32,4096]{1,0:T(8,128)(2,1)} %get-tuple-element.38), channel_id=1, source_target_pairs={{0,1},{1,0},{2,3},{3,2},{4,5},{5,4},{6,7},{7,6},{8,9},{9,8},{10,11... | collective-permute-start | bytes 786440 | tf_op jit(solution)/shard_map/ppermute | solution.py:205
  88.6 6.9 %collective-permute-done.11.g0 = bf16[32,4096]{1,0:T(8,128)(2,1)S(1)} collective-permute-done((bf16[32,4096]{1,0:T(8,128)(2,1)}, bf16[32,4096]{1,0:T(8,128)(2,1)S(1)}, u32[]{:S(2)}, u32[]{:S(2)}) %collective-permute-start.11) | collective-permute-done | bytes 262176 | tf_op jit(solution)/shard_map/ppermute | solution.py:205
  95.6 0.7 copy-done.17
  96.2 2.2 %shard_map.62 = bf16[64,4096]{1,0:T(8,128)(2,1)} custom-call(f32[32,4096]{1,0:T(8,128)} %get-tuple-element.37.r0, bf16[32,4096]{1,0:T(8,128)(2,1)} %copy-done.17, f32[32,4096]{1,0:T(8,128)} %get-tuple-element.47.r1, bf16[32,4096]{1,0:T(8,128)(2,1)} %copy-done.16), custom_call_target="tpu_custom_call" | custom-call | tf_op jit(solution)/shard_map/pallas_call | solution.py:207
  (31 shorter events, 0.1 us)
Async XLA Ops:
  1.0 28.1 %copy-start.6 = (bf16[2,512,128]{2,1,0:T(8,128)(2,1)}, bf16[2,512,128]{2,1,0:T(8,128)(2,1)S(1)}, u32[]{:S(2)}) copy-start(bf16[2,512,128]{2,1,0:T(8,128)(2,1)S(1)} %pad_maximum_fusion.own) | copy-start | bytes 786436
  1.0 9.7 %collective-permute-start.3 = (bf16[2,512,128]{2,1,0:T(8,128)(2,1)S(1)}, bf16[2,512,128]{2,1,0:T(8,128)(2,1)S(1)}, u32[]{:S(2)}, u32[]{:S(2)}) collective-permute-start(bf16[2,512,128]{2,1,0:T(8,128)(2,1)S(1)} %pad_maximum_fusion.own), channel_id=1, source_target_pairs={{0,32},{8,40},{16,48},{24,56},{32,64},{40,72},{48,80},{56,88},{64,... | collective-permute-start | bytes 786440 | tf_op jit(solution)/shard_map/ppermute | solution.py:139
  5.8 16.9 %collective-permute-start.1 = (bf16[2,512,128]{2,1,0:T(8,128)(2,1)S(1)}, bf16[2,512,128]{2,1,0:T(8,128)(2,1)S(1)}, u32[]{:S(2)}, u32[]{:S(2)}) collective-permute-start(bf16[2,512,128]{2,1,0:T(8,128)(2,1)S(1)} %pad_maximum_fusion.own), channel_id=1, source_target_pairs={{0,16},{8,24},{16,64},{24,72},{32,48},{40,56},{48,96},{56,104},{64... | collective-permute-start | bytes 786440 | tf_op jit(solution)/shard_map/ppermute | solution.py:141
  10.7 25.5 %copy-start = (bf16[2,512,128]{2,1,0:T(8,128)(2,1)}, bf16[2,512,128]{2,1,0:T(8,128)(2,1)S(1)}, u32[]{:S(2)}) copy-start(bf16[2,512,128]{2,1,0:T(8,128)(2,1)S(1)} %collective-permute-done.3.refs_2_) | copy-start | bytes 786436
  10.7 17.9 %collective-permute-start.5 = (bf16[2,512,128]{2,1,0:T(8,128)(2,1)S(1)}, bf16[2,512,128]{2,1,0:T(8,128)(2,1)S(1)}, u32[]{:S(2)}, u32[]{:S(2)}) collective-permute-start(bf16[2,512,128]{2,1,0:T(8,128)(2,1)S(1)} %collective-permute-done.3.refs_2_), channel_id=1, source_target_pairs={{0,16},{8,24},{16,0},{24,8},{32,48},{40,56},{48,32},{56,40},{64,80... | collective-permute-start | bytes 786440 | tf_op jit(solution)/shard_map/ppermute | solution.py:156
  16.7 12.4 %collective-permute-start = (bf16[2,512,128]{2,1,0:T(8,128)(2,1)S(1)}, bf16[2,512,128]{2,1,0:T(8,128)(2,1)S(1)}, u32[]{:S(2)}, u32[]{:S(2)}) collective-permute-start(bf16[2,512,128]{2,1,0:T(8,128)(2,1)S(1)} %pad_maximum_fusion.own), channel_id=1, source_target_pairs={{0,8},{8,0},{16,24},{24,16},{32,40},{40,32},{48,56},{56,48},{64,72... | collective-permute-start | bytes 786440 | tf_op jit(solution)/shard_map/ppermute | solution.py:142
  20.1 16.1 %collective-permute-start.4 = (bf16[2,512,128]{2,1,0:T(8,128)(2,1)S(1)}, bf16[2,512,128]{2,1,0:T(8,128)(2,1)S(1)}, u32[]{:S(2)}, u32[]{:S(2)}) collective-permute-start(bf16[2,512,128]{2,1,0:T(8,128)(2,1)S(1)} %collective-permute-done.3.refs_2_), channel_id=1, source_target_pairs={{0,8},{8,0},{16,24},{24,16},{32,40},{40,32},{48,56},{56,48},{64,72... | collective-permute-start | bytes 786440 | tf_op jit(solution)/shard_map/ppermute | solution.py:158
  22.7 13.5 %copy-start.1 = (bf16[2,512,128]{2,1,0:T(8,128)(2,1)}, bf16[2,512,128]{2,1,0:T(8,128)(2,1)S(1)}, u32[]{:S(2)}) copy-start(bf16[2,512,128]{2,1,0:T(8,128)(2,1)S(1)} %collective-permute-done.1.refs_0_) | copy-start | bytes 786436
  22.7 13.5 %collective-permute-start.2 = (bf16[2,512,128]{2,1,0:T(8,128)(2,1)S(1)}, bf16[2,512,128]{2,1,0:T(8,128)(2,1)S(1)}, u32[]{:S(2)}, u32[]{:S(2)}) collective-permute-start(bf16[2,512,128]{2,1,0:T(8,128)(2,1)S(1)} %collective-permute-done.1.refs_0_), channel_id=1, source_target_pairs={{0,8},{8,0},{16,24},{24,16},{32,40},{40,32},{48,56},{56,48},{64,72... | collective-permute-start | bytes 786440 | tf_op jit(solution)/shard_map/ppermute | solution.py:157
  28.6 7.6 %copy-start.2 = (bf16[2,512,128]{2,1,0:T(8,128)(2,1)}, bf16[2,512,128]{2,1,0:T(8,128)(2,1)S(1)}, u32[]{:S(2)}) copy-start(bf16[2,512,128]{2,1,0:T(8,128)(2,1)S(1)} %collective-permute-done.5.refs_4_) | copy-start | bytes 786436
  28.6 7.6 %collective-permute-start.6 = (bf16[2,512,128]{2,1,0:T(8,128)(2,1)S(1)}, bf16[2,512,128]{2,1,0:T(8,128)(2,1)S(1)}, u32[]{:S(2)}, u32[]{:S(2)}) collective-permute-start(bf16[2,512,128]{2,1,0:T(8,128)(2,1)S(1)} %collective-permute-done.5.refs_4_), channel_id=1, source_target_pairs={{0,8},{8,0},{16,24},{24,16},{32,40},{40,32},{48,56},{56,48},{64,72... | collective-permute-start | bytes 786440 | tf_op jit(solution)/shard_map/ppermute | solution.py:159
  29.1 0.7 copy-start.15
  36.2 0.7 copy-start.3
  36.2 0.9 copy-start.4
  36.2 0.9 copy-start.5
  43.4 14.3 %collective-permute-start.12 = (bf16[2,64,2048]{2,1,0:T(8,128)(2,1)}, bf16[2,64,2048]{2,1,0:T(8,128)(2,1)S(1)}, u32[]{:S(2)}, u32[]{:S(2)}) collective-permute-start(bf16[2,64,2048]{2,1,0:T(8,128)(2,1)} %get-tuple-element.39), channel_id=1, source_target_pairs={{0,2},{1,3},{2,0},{3,1},{4,6},{5,7},{6,4},{7,5},{8,10},{9,11},{10,... | collective-permute-start | bytes 1572872 | tf_op jit(solution)/shard_map/ppermute | solution.py:192
  44.9 15.4 %collective-permute-start.13 = (bf16[2,64,2048]{2,1,0:T(8,128)(2,1)}, bf16[2,64,2048]{2,1,0:T(8,128)(2,1)S(1)}, u32[]{:S(2)}, u32[]{:S(2)}) collective-permute-start(bf16[2,64,2048]{2,1,0:T(8,128)(2,1)} %get-tuple-element.41), channel_id=1, source_target_pairs={{0,6},{1,7},{2,4},{3,5},{4,2},{5,3},{6,0},{7,1},{8,14},{9,15},{10,... | collective-permute-start | bytes 1572872 | tf_op jit(solution)/shard_map/ppermute | solution.py:193
  53.1 15.2 %collective-permute-start.7 = (bf16[2,64,2048]{2,1,0:T(8,128)(2,1)}, bf16[2,64,2048]{2,1,0:T(8,128)(2,1)S(1)}, u32[]{:S(2)}, u32[]{:S(2)}) collective-permute-start(bf16[2,64,2048]{2,1,0:T(8,128)(2,1)} %get-tuple-element.29), channel_id=1, source_target_pairs={{0,2},{1,3},{2,0},{3,1},{4,6},{5,7},{6,4},{7,5},{8,10},{9,11},{10,... | collective-permute-start | bytes 1572872 | tf_op jit(solution)/shard_map/ppermute | solution.py:192
  53.5 18.1 %collective-permute-start.8 = (bf16[2,64,2048]{2,1,0:T(8,128)(2,1)}, bf16[2,64,2048]{2,1,0:T(8,128)(2,1)S(1)}, u32[]{:S(2)}, u32[]{:S(2)}) collective-permute-start(bf16[2,64,2048]{2,1,0:T(8,128)(2,1)} %get-tuple-element.31), channel_id=1, source_target_pairs={{0,6},{1,7},{2,4},{3,5},{4,2},{5,3},{6,0},{7,1},{8,14},{9,15},{10,... | collective-permute-start | bytes 1572872 | tf_op jit(solution)/shard_map/ppermute | solution.py:193
  57.7 2.5 %copy-start.9 = (bf16[2,64,2048]{2,1,0:T(8,128)(2,1)}, bf16[2,64,2048]{2,1,0:T(8,128)(2,1)S(1)}, u32[]{:S(2)}) copy-start(bf16[2,64,2048]{2,1,0:T(8,128)(2,1)S(1)} %collective-permute-done.12.p_got) | copy-start | bytes 1572868
  60.3 0.8 copy-start.10
  63.7 13.0 %collective-permute-start.14 = (bf16[64,2048]{1,0:T(8,128)(2,1)}, bf16[64,2048]{1,0:T(8,128)(2,1)S(1)}, u32[]{:S(2)}, u32[]{:S(2)}) collective-permute-start(bf16[64,2048]{1,0:T(8,128)(2,1)} %get-tuple-element.43), channel_id=1, source_target_pairs={{0,6},{1,7},{2,4},{3,5},{4,2},{5,3},{6,0},{7,1},{8,14},{9,15},{10,... | collective-permute-start | bytes 786440 | tf_op jit(solution)/shard_map/ppermute | solution.py:197
  65.5 11.2 %collective-permute-start.15 = (bf16[64,2048]{1,0:T(8,128)(2,1)}, bf16[64,2048]{1,0:T(8,128)(2,1)S(1)}, u32[]{:S(2)}, u32[]{:S(2)}) collective-permute-start(bf16[64,2048]{1,0:T(8,128)(2,1)} %get-tuple-element.45), channel_id=1, source_target_pairs={{0,2},{1,3},{2,0},{3,1},{4,6},{5,7},{6,4},{7,5},{8,10},{9,11},{10,... | collective-permute-start | bytes 786440 | tf_op jit(solution)/shard_map/ppermute | solution.py:198
  68.2 3.3 %copy-start.7 = (bf16[2,64,2048]{2,1,0:T(8,128)(2,1)}, bf16[2,64,2048]{2,1,0:T(8,128)(2,1)S(1)}, u32[]{:S(2)}) copy-start(bf16[2,64,2048]{2,1,0:T(8,128)(2,1)S(1)} %collective-permute-done.7.p_got) | copy-start | bytes 1572868
  71.5 0.8 copy-start.8
  74.9 7.4 %collective-permute-start.10 = (bf16[64,2048]{1,0:T(8,128)(2,1)}, bf16[64,2048]{1,0:T(8,128)(2,1)S(1)}, u32[]{:S(2)}, u32[]{:S(2)}) collective-permute-start(bf16[64,2048]{1,0:T(8,128)(2,1)} %get-tuple-element.35), channel_id=1, source_target_pairs={{0,2},{1,3},{2,0},{3,1},{4,6},{5,7},{6,4},{7,5},{8,10},{9,11},{10,... | collective-permute-start | bytes 786440 | tf_op jit(solution)/shard_map/ppermute | solution.py:198
  74.9 8.5 %collective-permute-start.9 = (bf16[64,2048]{1,0:T(8,128)(2,1)}, bf16[64,2048]{1,0:T(8,128)(2,1)S(1)}, u32[]{:S(2)}, u32[]{:S(2)}) collective-permute-start(bf16[64,2048]{1,0:T(8,128)(2,1)} %get-tuple-element.33), channel_id=1, source_target_pairs={{0,6},{1,7},{2,4},{3,5},{4,2},{5,3},{6,0},{7,1},{8,14},{9,15},{10,... | collective-permute-start | bytes 786440 | tf_op jit(solution)/shard_map/ppermute | solution.py:197
  76.7 0.7 copy-start.11
  76.7 0.8 copy-start.12
  79.7 9.0 %collective-permute-start.16 = (bf16[32,4096]{1,0:T(8,128)(2,1)}, bf16[32,4096]{1,0:T(8,128)(2,1)S(1)}, u32[]{:S(2)}, u32[]{:S(2)}) collective-permute-start(bf16[32,4096]{1,0:T(8,128)(2,1)} %get-tuple-element.48), channel_id=1, source_target_pairs={{0,1},{1,0},{2,3},{3,2},{4,5},{5,4},{6,7},{7,6},{8,9},{9,8},{10,11... | collective-permute-start | bytes 786440 | tf_op jit(solution)/shard_map/ppermute | solution.py:205
  82.3 1.0 %copy-start.13 = (bf16[64,2048]{1,0:T(8,128)(2,1)}, bf16[64,2048]{1,0:T(8,128)(2,1)S(1)}, u32[]{:S(2)}) copy-start(bf16[64,2048]{1,0:T(8,128)(2,1)S(1)} %collective-permute-done.10.q_got) | copy-start | bytes 786436
  83.3 0.7 copy-start.14
  86.2 9.3 %collective-permute-start.11 = (bf16[32,4096]{1,0:T(8,128)(2,1)}, bf16[32,4096]{1,0:T(8,128)(2,1)S(1)}, u32[]{:S(2)}, u32[]{:S(2)}) collective-permute-start(bf16[32,4096]{1,0:T(8,128)(2,1)} %get-tuple-element.38), channel_id=1, source_target_pairs={{0,1},{1,0},{2,3},{3,2},{4,5},{5,4},{6,7},{7,6},{8,9},{9,8},{10,11... | collective-permute-start | bytes 786440 | tf_op jit(solution)/shard_map/ppermute | solution.py:205
  88.6 6.9 %copy-start.16 = (bf16[32,4096]{1,0:T(8,128)(2,1)}, bf16[32,4096]{1,0:T(8,128)(2,1)S(1)}, u32[]{:S(2)}) copy-start(bf16[32,4096]{1,0:T(8,128)(2,1)S(1)} %collective-permute-done.16.g1) | copy-start | bytes 786436
  95.6 0.7 copy-start.17

commit v6 on v5

--- a/solution.py
+++ b/solution.py
@@ -69,8 +69,8 @@
 
 def rest_kernel(doc, q_ref, m_in, acc_in, *refs):
     blocks, refs = refs[:6], refs[6:]
-    w_hbm, p_send, p_keep, q_send, q_keep, q_sc, m_sc, acc_sc, w_sc, a_sc, w_sem = refs
-    load = pltpu.make_async_copy(w_hbm, w_sc, w_sem)
+    w_hbm, p_send, p_keep, q_send, q_keep, q_sc, m_sc, acc_sc, w_ref, a_sc, w_sem = refs
+    load = pltpu.make_async_copy(w_hbm, w_ref, w_sem)
     load.start()
     q_sc[...] = q_ref[...].reshape(q_sc.shape)
     m_sc[...] = m_in[...].reshape(m_sc.shape)
@@ -94,7 +94,7 @@
     load.wait()
     x = lax.div(lax.axis_index("head"), 2)
     near, far = lax.bitwise_xor(x, 1), 3 - x
-    half = w_sc.shape[1] // 2
+    half = w_ref.shape[1] // 2
     step = half // 2
     for base, order, send, keep in (
         (0, (near, 3 - near, x, far), p_send, p_keep),
@@ -102,32 +102,17 @@
     ):
         left = jnp.concatenate([a_sc[i] for i in order])
         for n in range(0, half, step):
-            part = jnp.dot(left, w_sc[:, base + n:base + n + step], preferred_element_type=F32)
+            part = jnp.dot(left, w_ref[:, base + n:base + n + step], preferred_element_type=F32)
             part = part.astype(BF16).reshape(2, 2, -1, step)
             send[:, :, n:n + step] = part[0]
             keep[:, :, n:n + step] = part[1]
 
 
-def halve_kernel(p_got, p_keep, q_got, q_keep, p_send, p_next, q_send, q_next):
-    for got, keep, send, rest in ((p_got, p_keep, p_send, p_next), (q_got, q_keep, q_send, q_next)):
-        rest[...] = (got[0].astype(F32) + keep[0].astype(F32)).astype(BF16)
-        send[...] = (got[1].astype(F32) + keep[1].astype(F32)).astype(BF16)
-
-
-def part_kernel(p_got, p_keep, q_got, q_keep, send, rest):
-    part = lax.rem(lax.axis_index("head"), 2)
-    rows, half = send.shape[0], p_got.shape[1]
-    mine = pl.ds(pl.multiple_of(part * rows, rows), rows)
-    give = pl.ds(pl.multiple_of((1 - part) * rows, rows), rows)
-    for n, got, keep in ((0, p_got, p_keep), (half, q_got, q_keep)):
-        rest[:, n:n + half] = got[mine, :].astype(F32) + keep[mine, :].astype(F32)
-        send[:, n:n + half] = (got[give, :].astype(F32) + keep[give, :].astype(F32)).astype(BF16)
-
-
-def finish_kernel(r0, g0, r1, g1, o_ref):
-    rows = r0.shape[0]
-    for k, (r, g) in enumerate(((r0, g0), (r1, g1))):
-        o_ref[k * rows:(k + 1) * rows, :] = (r[...] + g[...].astype(F32)).astype(BF16)
+def add(*terms):
+    total = terms[0].astype(F32)
+    for term in terms[1:]:
+        total = total + term.astype(F32)
+    return total
 
 
 def on_device(queries, keys, values, doc_start, out_weight):
@@ -157,8 +142,8 @@
     far_o = lax.ppermute(far, "ctx", swap)
     near_o = lax.ppermute(near, "ctx", swap)
     cross_o = lax.ppermute(cross, "ctx", swap)
-    width = out_weight.shape[1]
-    half = width // 2
+    part = lax.axis_index("head") % 2
+    half = out_weight.shape[1] // 2
     block = rows // NHEAD // 2
     shaped = (queries, m, acc)
     shaped = [t.reshape(t.shape[:-2] + (NHEAD, 2, block, t.shape[-1])) for t in shaped]
@@ -167,7 +152,6 @@
     to_part = [(h, h ^ 1) for h in range(NHEAD)]
     vmem = lambda *shapes: [pltpu.VMEM(t, d) for t, d in shapes]
     quad = jax.ShapeDtypeStruct((2, 2 * block, half), BF16)
-    pair = jax.ShapeDtypeStruct((2 * block, half), BF16)
 
     def chunk(k):
         specs = [
@@ -191,25 +175,22 @@
         )(doc_start, *shaped, far, far_o, near, near_o, cross, cross_o, out_weight)
         p_got = lax.ppermute(p_send, "head", to_near)
         q_got = lax.ppermute(q_send, "head", to_far)
-        p_send, p_keep, q_send, q_keep = pl.pallas_call(
-            halve_kernel, out_shape=[pair] * 4, in_specs=[VMEM] * 4, out_specs=[VMEM] * 4
-        )(p_got, p_keep, q_got, q_keep)
-        p_got = lax.ppermute(p_send, "head", to_far)
-        q_got = lax.ppermute(q_send, "head", to_near)
-        send, rest = pl.pallas_call(
-            part_kernel,
-            out_shape=[jax.ShapeDtypeStruct((block, width), t) for t in (BF16, F32)],
-            in_specs=[VMEM] * 4,
-            out_specs=[VMEM] * 2,
-        )(p_got, p_keep, q_got, q_keep)
-        return rest, lax.ppermute(send, "head", to_part)
-
-    return pl.pallas_call(
-        finish_kernel,
-        out_shape=jax.ShapeDtypeStruct((2 * block, width), BF16),
-        in_specs=[VMEM] * 4,
-        out_specs=VMEM,
-    )(*chunk(0), *chunk(1))
+        p_next = add(p_got[1], p_keep[1]).astype(BF16)
+        q_next = add(q_got[1], q_keep[1]).astype(BF16)
+        p_last = lax.ppermute(p_next, "head", to_far)
+        q_last = lax.ppermute(q_next, "head", to_near)
+
+        def total(y):
+            terms = ((p_got, p_keep, p_last), (q_got, q_keep, q_last))
+            return jnp.concatenate([
+                add(*(lax.dynamic_slice_in_dim(t.reshape(-1, half), y * block, block, 0) for t in side))
+                for side in terms
+            ], axis=1)
+
+        got = lax.ppermute(total(1 - part).astype(BF16), "head", to_part)
+        return (total(part) + got.astype(F32)).astype(BF16)
+
+    return jnp.concatenate([chunk(0), chunk(1)])
 
 
 def solution(mesh):

time: 98.9 us -> 92.6 us (0.936)
  Pallas kernels: 30.7 us -> 19.1 us
  local copies, waits for them, and re-layouts: 5.41 us -> 1.59 us
  other arithmetic: 0.99 us -> 4.56 us
  waiting for transfers between devices: 29.5 us -> 32.6 us
  starting transfers between devices: 31.8 us -> 34.2 us
    pallas_call x5 -> x0, Pallas kernels: 11.7 us -> none  [the longest x2 5.14 us: chunk(): pl.pallas_call(halve_kernel, out_shape=[pair] * 4, in_specs=[VMEM] * 4, o...]
    ppermute x2, waiting for transfers between devices: 5.83 us -> 0.01 us  [chunk(): q_got = lax.ppermute(q_send, 'head', to_far)]
    ppermute x2, waiting for transfers between devices: 6.39 us -> 11.6 us  [chunk(): p_got = lax.ppermute(p_send, 'head', to_near)]
    unnamed x36 -> x24, local copies, waits for them, and re-layouts: 5.41 us -> 1.59 us
    ppermute x6, waiting for transfers between devices: 7.97 us -> 11.7 us  [the longest x2 6.82 us: chunk(): got = lax.ppermute(total(1 - part).astype(BF16), 'head', to_part)]
    ppermute x6, starting transfers between devices: 8.64 us -> 11.1 us  [the longest x2 5.6 us: chunk(): p_last = lax.ppermute(p_next, 'head', to_far)]
    convert_element_type x0 -> x6, other arithmetic: none -> 2.29 us  [the longest x2 1.08 us: chunk(): q_next = add(q_got[1], q_keep[1]).astype(BF16)]
  transfers between devices with their start and end apart: 17 -> 17, of which waited for: 9 -> 9; matrix products, arithmetic and copies ran while one was open for 0% -> 3% of each run, Pallas kernels for 22% -> 14%
where the time goes in v6:
time: 92.6 us; the launch traced here: 92.3 us
  starting transfers between devices  34.2 us (37%)
  waiting for transfers between devices  32.6 us (35%)
  Pallas kernels  19.1 us (21%)
  other arithmetic  4.56 us (5%)
  local copies, waits for them, and re-layouts  1.59 us (2%)
    pallas_call x2, Pallas kernels, chunk(): pl.pallas_call(rest_kernel, grid=(1,), out_shape=[quad] * 4, in_specs=[SM...  12.7 us
    ppermute x2, waiting for transfers between devices, chunk(): p_got = lax.ppermute(p_send, 'head', to_near)  11.6 us
    ppermute x2, waiting for transfers between devices, chunk(): got = lax.ppermute(total(1 - part).astype(BF16), 'head', to_part)  6.82 us
    pallas_call x1, Pallas kernels, on_device(): pl.pallas_call(own_kernel, out_shape=state, in_specs=[VMEM] * 4, out_spec...  6.32 us
    ppermute x1, starting transfers between devices, on_device(): cross = lax.ppermute(near, 'ctx', [(c, c ^ 2) for c in range(n_ctx)])  5.95 us
    ppermute x2, starting transfers between devices, chunk(): p_last = lax.ppermute(p_next, 'head', to_far)  5.6 us
    ppermute x2, starting transfers between devices, chunk(): got = lax.ppermute(total(1 - part).astype(BF16), 'head', to_part)  5.31 us
    ppermute x1, waiting for transfers between devices, on_device(): cross = lax.ppermute(near, 'ctx', [(c, c ^ 2) for c in range(n_ctx)])  4.98 us
  transfers between devices with their start and end apart: 17, of which 9 were waited for; matrix products, arithmetic and copies ran while one was open for 3% of the time, Pallas kernels for 14%

profile of v6, /device:TPU:97, one launch (start us, length us, event | category | flops | bytes accessed | tf_op | source)
XLA Modules:
  0.0 92.3 jit_solution(7038353247745127697)
XLA Ops:
  0.0 1.0 %pad_maximum_fusion.1.own = bf16[2,512,128]{2,1,0:T(8,128)(2,1)S(1)} fusion(bf16[1,512,128]{2,1,0:T(8,128)(2,1)} %bitcast.36, bf16[1,512,128]{2,1,0:T(8,128)(2,1)} %bitcast.37), kind=kLoop, calls=%fused_computation.13 | loop fusion | flops 131072 | bytes 524288 | tf_op jit(solution)/shard_map/stack | solution.py:122
  1.0 0.0 copy-start.6
  1.0 4.8 %collective-permute-start.3 = (bf16[2,512,128]{2,1,0:T(8,128)(2,1)S(1)}, bf16[2,512,128]{2,1,0:T(8,128)(2,1)S(1)}, u32[]{:S(2)}, u32[]{:S(2)}) collective-permute-start(bf16[2,512,128]{2,1,0:T(8,128)(2,1)S(1)} %pad_maximum_fusion.1.own), channel_id=1, source_target_pairs={{0,32},{8,40},{16,48},{24,56},{32,64},{40,72},{48,80},{56,88},{64,... | collective-permute-start | bytes 786440 | tf_op jit(solution)/shard_map/ppermute | solution.py:124
  5.8 3.2 %collective-permute-start.1 = (bf16[2,512,128]{2,1,0:T(8,128)(2,1)S(1)}, bf16[2,512,128]{2,1,0:T(8,128)(2,1)S(1)}, u32[]{:S(2)}, u32[]{:S(2)}) collective-permute-start(bf16[2,512,128]{2,1,0:T(8,128)(2,1)S(1)} %pad_maximum_fusion.1.own), channel_id=1, source_target_pairs={{0,16},{8,24},{16,64},{24,72},{32,48},{40,56},{48,96},{56,104},{64... | collective-permute-start | bytes 786440 | tf_op jit(solution)/shard_map/ppermute | solution.py:126
  9.0 1.8 %collective-permute-done.3.refs_2_ = bf16[2,512,128]{2,1,0:T(8,128)(2,1)S(1)} collective-permute-done((bf16[2,512,128]{2,1,0:T(8,128)(2,1)S(1)}, bf16[2,512,128]{2,1,0:T(8,128)(2,1)S(1)}, u32[]{:S(2)}, u32[]{:S(2)}) %collective-permute-start.3) | collective-permute-done | bytes 262176 | tf_op jit(solution)/shard_map/ppermute | solution.py:124
  10.7 6.0 %collective-permute-start.5 = (bf16[2,512,128]{2,1,0:T(8,128)(2,1)S(1)}, bf16[2,512,128]{2,1,0:T(8,128)(2,1)S(1)}, u32[]{:S(2)}, u32[]{:S(2)}) collective-permute-start(bf16[2,512,128]{2,1,0:T(8,128)(2,1)S(1)} %collective-permute-done.3.refs_2_), channel_id=1, source_target_pairs={{0,16},{8,24},{16,0},{24,8},{32,48},{40,56},{48,32},{56,40},{64,80... | collective-permute-start | bytes 786440 | tf_op jit(solution)/shard_map/ppermute | solution.py:141
  16.7 3.4 %collective-permute-start = (bf16[2,512,128]{2,1,0:T(8,128)(2,1)S(1)}, bf16[2,512,128]{2,1,0:T(8,128)(2,1)S(1)}, u32[]{:S(2)}, u32[]{:S(2)}) collective-permute-start(bf16[2,512,128]{2,1,0:T(8,128)(2,1)S(1)} %pad_maximum_fusion.1.own), channel_id=1, source_target_pairs={{0,8},{8,0},{16,24},{24,16},{32,40},{40,32},{48,56},{56,48},{64,72... | collective-permute-start | bytes 786440 | tf_op jit(solution)/shard_map/ppermute | solution.py:127
  20.1 0.0 collective-permute-start.4
  20.1 2.6 %collective-permute-done.1.refs_0_ = bf16[2,512,128]{2,1,0:T(8,128)(2,1)S(1)} collective-permute-done((bf16[2,512,128]{2,1,0:T(8,128)(2,1)S(1)}, bf16[2,512,128]{2,1,0:T(8,128)(2,1)S(1)}, u32[]{:S(2)}, u32[]{:S(2)}) %collective-permute-start.1) | collective-permute-done | bytes 262176 | tf_op jit(solution)/shard_map/ppermute | solution.py:126
  22.7 1.0 %collective-permute-start.2 = (bf16[2,512,128]{2,1,0:T(8,128)(2,1)S(1)}, bf16[2,512,128]{2,1,0:T(8,128)(2,1)S(1)}, u32[]{:S(2)}, u32[]{:S(2)}) collective-permute-start(bf16[2,512,128]{2,1,0:T(8,128)(2,1)S(1)} %collective-permute-done.1.refs_0_), channel_id=1, source_target_pairs={{0,8},{8,0},{16,24},{24,16},{32,40},{40,32},{48,56},{56,48},{64,72... | collective-permute-start | bytes 786440 | tf_op jit(solution)/shard_map/ppermute | solution.py:142
  23.6 5.0 %collective-permute-done.5.refs_4_ = bf16[2,512,128]{2,1,0:T(8,128)(2,1)S(1)} collective-permute-done((bf16[2,512,128]{2,1,0:T(8,128)(2,1)S(1)}, bf16[2,512,128]{2,1,0:T(8,128)(2,1)S(1)}, u32[]{:S(2)}, u32[]{:S(2)}) %collective-permute-start.5) | collective-permute-done | bytes 262176 | tf_op jit(solution)/shard_map/ppermute | solution.py:141
  28.6 0.5 collective-permute-start.6
  29.1 0.0 collective-permute-done.partner
  29.1 0.7 copy-done.11
  29.8 6.3 %shard_map.55 = (f32[4,512,128]{2,1,0:T(8,128)}, f32[4,512,256]{2,1,0:T(8,128)}) custom-call(bf16[512,512]{1,0:T(8,128)(2,1)} %q_ref.1, s32[4,128]{1,0:T(4,128)} %bitcast.38, bf16[2,512,128]{2,1,0:T(8,128)(2,1)} %copy-done.6, bf16[2,512,128]{2,1,0:T(8,128)(2,1)} %copy-done.11), custom_call_target="tpu_custom_call" | custom-call | tf_op jit(solution)/shard_map/pallas_call | solution.py:133
  36.1 0.0 collective-permute-done.4.refs_3_
  36.2 0.7 copy-done.3
  36.9 0.1 copy-done.4
  37.0 0.1 copy-done.5
  37.1 6.3 %shard_map.56 = (bf16[2,64,2048]{2,1,0:T(8,128)(2,1)}, bf16[2,64,2048]{2,1,0:T(8,128)(2,1)}, bf16[2,64,2048]{2,1,0:T(8,128)(2,1)}, bf16[2,64,2048]{2,1,0:T(8,128)(2,1)}) custom-call(s32[512]{0:T(512)} %doc.3, bf16[8,2,32,512]{3,2,1,0:T(8,128)(2,1)} %bitcast.24, f32[4,8,2,32,128]{4,3,2,1,0:T(8,128)} %bitcast.26, f32[4,8,2,32,256]{4,3,2,1,0:T(8,128)} %bitcast.22, ...), custom_call_target="tpu_custom_call" | custom-call | tf_op jit(solution)/shard_map/pallas_call | solution.py:161
  43.4 1.5 %collective-permute-start.7 = (bf16[2,64,2048]{2,1,0:T(8,128)(2,1)}, bf16[2,64,2048]{2,1,0:T(8,128)(2,1)S(1)}, u32[]{:S(2)}, u32[]{:S(2)}) collective-permute-start(bf16[2,64,2048]{2,1,0:T(8,128)(2,1)} %get-tuple-element.17), channel_id=1, source_target_pairs={{0,2},{1,3},{2,0},{3,1},{4,6},{5,7},{6,4},{7,5},{8,10},{9,11},{10,... | collective-permute-start | bytes 1572872 | tf_op jit(solution)/shard_map/ppermute | solution.py:176
  44.9 1.8 %collective-permute-start.9 = (bf16[2,64,2048]{2,1,0:T(8,128)(2,1)}, bf16[2,64,2048]{2,1,0:T(8,128)(2,1)S(1)}, u32[]{:S(2)}, u32[]{:S(2)}) collective-permute-start(bf16[2,64,2048]{2,1,0:T(8,128)(2,1)} %get-tuple-element.19), channel_id=1, source_target_pairs={{0,6},{1,7},{2,4},{3,5},{4,2},{5,3},{6,0},{7,1},{8,14},{9,15},{10,... | collective-permute-start | bytes 1572872 | tf_op jit(solution)/shard_map/ppermute | solution.py:177
  46.7 6.4 %shard_map.57 = (bf16[2,64,2048]{2,1,0:T(8,128)(2,1)}, bf16[2,64,2048]{2,1,0:T(8,128)(2,1)}, bf16[2,64,2048]{2,1,0:T(8,128)(2,1)}, bf16[2,64,2048]{2,1,0:T(8,128)(2,1)}) custom-call(s32[512]{0:T(512)} %doc.3, bf16[8,2,32,512]{3,2,1,0:T(8,128)(2,1)} %bitcast.25, f32[4,8,2,32,128]{4,3,2,1,0:T(8,128)} %bitcast.27, f32[4,8,2,32,256]{4,3,2,1,0:T(8,128)} %bitcast.23, ...), custom_call_target="tpu_custom_call" | custom-call | tf_op jit(solution)/shard_map/pallas_call | solution.py:161
  53.1 0.4 collective-permute-start.12
  53.5 0.6 collective-permute-start.14
  54.2 3.4 %collective-permute-done.7 = bf16[2,64,2048]{2,1,0:T(8,128)(2,1)S(1)} collective-permute-done((bf16[2,64,2048]{2,1,0:T(8,128)(2,1)}, bf16[2,64,2048]{2,1,0:T(8,128)(2,1)S(1)}, u32[]{:S(2)}, u32[]{:S(2)}) %collective-permute-start.7) | collective-permute-done | bytes 524320 | tf_op jit(solution)/shard_map/ppermute | solution.py:176
  57.6 0.1 fusion.2
  57.7 2.8 %collective-permute-start.8 = (bf16[64,2048]{1,0:T(8,128)(2,1)S(1)}, bf16[64,2048]{1,0:T(8,128)(2,1)S(1)}, u32[]{:S(2)}, u32[]{:S(2)}) collective-permute-start(bf16[64,2048]{1,0:T(8,128)(2,1)S(1)} %fusion.2), channel_id=1, source_target_pairs={{0,6},{1,7},{2,4},{3,5},{4,2},{5,3},{6,0},{7,1},{8,14},{9,15},{10,... | collective-permute-start | bytes 786440 | tf_op jit(solution)/shard_map/ppermute | solution.py:180
  60.5 0.1 fusion.3
  60.5 0.1 collective-permute-start.10
  60.6 8.2 %collective-permute-done.12 = bf16[2,64,2048]{2,1,0:T(8,128)(2,1)S(1)} collective-permute-done((bf16[2,64,2048]{2,1,0:T(8,128)(2,1)}, bf16[2,64,2048]{2,1,0:T(8,128)(2,1)S(1)}, u32[]{:S(2)}, u32[]{:S(2)}) %collective-permute-start.12) | collective-permute-done | bytes 524320 | tf_op jit(solution)/shard_map/ppermute | solution.py:176
  68.8 1.0 %fusion.4 = bf16[64,2048]{1,0:T(8,128)(2,1)S(1)} fusion(bf16[2,64,2048]{2,1,0:T(8,128)(2,1)S(1)} %collective-permute-done.12, bf16[2,64,2048]{2,1,0:T(8,128)(2,1)} %get-tuple-element.22), kind=kLoop, calls=%fused_computation.11 | loop fusion | flops 524288 | bytes 786432 | tf_op jit(solution)/shard_map/convert_element_type | solution.py:178
  69.8 2.8 %collective-permute-start.13 = (bf16[64,2048]{1,0:T(8,128)(2,1)S(1)}, bf16[64,2048]{1,0:T(8,128)(2,1)S(1)}, u32[]{:S(2)}, u32[]{:S(2)}) collective-permute-start(bf16[64,2048]{1,0:T(8,128)(2,1)S(1)} %fusion.4), channel_id=1, source_target_pairs={{0,6},{1,7},{2,4},{3,5},{4,2},{5,3},{6,0},{7,1},{8,14},{9,15},{10,... | collective-permute-start | bytes 786440 | tf_op jit(solution)/shard_map/ppermute | solution.py:180
  72.7 1.0 %fusion.5 = bf16[64,2048]{1,0:T(8,128)(2,1)S(1)} fusion(bf16[2,64,2048]{2,1,0:T(8,128)(2,1)S(1)} %collective-permute-done.14, bf16[2,64,2048]{2,1,0:T(8,128)(2,1)} %get-tuple-element.24), kind=kLoop, calls=%fused_computation.12 | loop fusion | flops 524288 | bytes 786432 | tf_op jit(solution)/shard_map/convert_element_type | solution.py:179
  73.7 0.1 collective-permute-start.15
  73.8 3.3 %collective-permute-done.8 = bf16[64,2048]{1,0:T(8,128)(2,1)S(1)} collective-permute-done((bf16[64,2048]{1,0:T(8,128)(2,1)S(1)}, bf16[64,2048]{1,0:T(8,128)(2,1)S(1)}, u32[]{:S(2)}, u32[]{:S(2)}) %collective-permute-start.8) | collective-permute-done | bytes 262176 | tf_op jit(solution)/shard_map/ppermute | solution.py:180
  77.1 0.1 add_convert_fusion.7
  77.2 0.1 add_convert_fusion.6
  77.4 2.7 %collective-permute-start.11 = (bf16[32,4096]{1,0:T(8,128)(2,1)S(1)}, bf16[32,4096]{1,0:T(8,128)(2,1)S(1)}, u32[]{:S(2)}, u32[]{:S(2)}) collective-permute-start(bf16[32,4096]{1,0:T(8,128)(2,1)S(1)} %pad_maximum_fusion.2), channel_id=1, source_target_pairs={{0,1},{1,0},{2,3},{3,2},{4,5},{5,4},{6,7},{7,6},{8,9},{9,8},{10,11... | collective-permute-start | bytes 786440 | tf_op jit(solution)/shard_map/ppermute | solution.py:190
  80.1 1.6 %collective-permute-done.13 = bf16[64,2048]{1,0:T(8,128)(2,1)S(1)} collective-permute-done((bf16[64,2048]{1,0:T(8,128)(2,1)S(1)}, bf16[64,2048]{1,0:T(8,128)(2,1)S(1)}, u32[]{:S(2)}, u32[]{:S(2)}) %collective-permute-start.13) | collective-permute-done | bytes 262176 | tf_op jit(solution)/shard_map/ppermute | solution.py:180
  81.7 0.1 add_convert_fusion.5
  81.8 0.1 add_convert_fusion.4
  81.9 2.6 %collective-permute-start.16 = (bf16[32,4096]{1,0:T(8,128)(2,1)S(1)}, bf16[32,4096]{1,0:T(8,128)(2,1)S(1)}, u32[]{:S(2)}, u32[]{:S(2)}) collective-permute-start(bf16[32,4096]{1,0:T(8,128)(2,1)S(1)} %pad_maximum_fusion.3), channel_id=1, source_target_pairs={{0,1},{1,0},{2,3},{3,2},{4,5},{5,4},{6,7},{7,6},{8,9},{9,8},{10,11... | collective-permute-start | bytes 786440 | tf_op jit(solution)/shard_map/ppermute | solution.py:190
  84.5 1.2 %collective-permute-done.11 = bf16[32,4096]{1,0:T(8,128)(2,1)S(1)} collective-permute-done((bf16[32,4096]{1,0:T(8,128)(2,1)S(1)}, bf16[32,4096]{1,0:T(8,128)(2,1)S(1)}, u32[]{:S(2)}, u32[]{:S(2)}) %collective-permute-start.11) | collective-permute-done | bytes 262176 | tf_op jit(solution)/shard_map/ppermute | solution.py:190
  85.7 0.1 fusion
  85.8 5.6 %collective-permute-done.16 = bf16[32,4096]{1,0:T(8,128)(2,1)S(1)} collective-permute-done((bf16[32,4096]{1,0:T(8,128)(2,1)S(1)}, bf16[32,4096]{1,0:T(8,128)(2,1)S(1)}, u32[]{:S(2)}, u32[]{:S(2)}) %collective-permute-start.16) | collective-permute-done | bytes 262176 | tf_op jit(solution)/shard_map/ppermute | solution.py:190
  91.4 0.1 fusion.1
  91.5 0.8 pad_maximum_fusion
  (27 shorter events, 0.1 us)
Async XLA Ops:
  1.0 28.1 %copy-start.6 = (bf16[2,512,128]{2,1,0:T(8,128)(2,1)}, bf16[2,512,128]{2,1,0:T(8,128)(2,1)S(1)}, u32[]{:S(2)}) copy-start(bf16[2,512,128]{2,1,0:T(8,128)(2,1)S(1)} %pad_maximum_fusion.1.own) | copy-start | bytes 786436
  1.0 9.7 %collective-permute-start.3 = (bf16[2,512,128]{2,1,0:T(8,128)(2,1)S(1)}, bf16[2,512,128]{2,1,0:T(8,128)(2,1)S(1)}, u32[]{:S(2)}, u32[]{:S(2)}) collective-permute-start(bf16[2,512,128]{2,1,0:T(8,128)(2,1)S(1)} %pad_maximum_fusion.1.own), channel_id=1, source_target_pairs={{0,32},{8,40},{16,48},{24,56},{32,64},{40,72},{48,80},{56,88},{64,... | collective-permute-start | bytes 786440 | tf_op jit(solution)/shard_map/ppermute | solution.py:124
  5.8 16.9 %collective-permute-start.1 = (bf16[2,512,128]{2,1,0:T(8,128)(2,1)S(1)}, bf16[2,512,128]{2,1,0:T(8,128)(2,1)S(1)}, u32[]{:S(2)}, u32[]{:S(2)}) collective-permute-start(bf16[2,512,128]{2,1,0:T(8,128)(2,1)S(1)} %pad_maximum_fusion.1.own), channel_id=1, source_target_pairs={{0,16},{8,24},{16,64},{24,72},{32,48},{40,56},{48,96},{56,104},{64... | collective-permute-start | bytes 786440 | tf_op jit(solution)/shard_map/ppermute | solution.py:126
  10.7 25.4 %copy-start = (bf16[2,512,128]{2,1,0:T(8,128)(2,1)}, bf16[2,512,128]{2,1,0:T(8,128)(2,1)S(1)}, u32[]{:S(2)}) copy-start(bf16[2,512,128]{2,1,0:T(8,128)(2,1)S(1)} %collective-permute-done.3.refs_2_) | copy-start | bytes 786436
  10.7 17.9 %collective-permute-start.5 = (bf16[2,512,128]{2,1,0:T(8,128)(2,1)S(1)}, bf16[2,512,128]{2,1,0:T(8,128)(2,1)S(1)}, u32[]{:S(2)}, u32[]{:S(2)}) collective-permute-start(bf16[2,512,128]{2,1,0:T(8,128)(2,1)S(1)} %collective-permute-done.3.refs_2_), channel_id=1, source_target_pairs={{0,16},{8,24},{16,0},{24,8},{32,48},{40,56},{48,32},{56,40},{64,80... | collective-permute-start | bytes 786440 | tf_op jit(solution)/shard_map/ppermute | solution.py:141
  16.7 12.4 %collective-permute-start = (bf16[2,512,128]{2,1,0:T(8,128)(2,1)S(1)}, bf16[2,512,128]{2,1,0:T(8,128)(2,1)S(1)}, u32[]{:S(2)}, u32[]{:S(2)}) collective-permute-start(bf16[2,512,128]{2,1,0:T(8,128)(2,1)S(1)} %pad_maximum_fusion.1.own), channel_id=1, source_target_pairs={{0,8},{8,0},{16,24},{24,16},{32,40},{40,32},{48,56},{56,48},{64,72... | collective-permute-start | bytes 786440 | tf_op jit(solution)/shard_map/ppermute | solution.py:127
  20.1 16.0 %collective-permute-start.4 = (bf16[2,512,128]{2,1,0:T(8,128)(2,1)S(1)}, bf16[2,512,128]{2,1,0:T(8,128)(2,1)S(1)}, u32[]{:S(2)}, u32[]{:S(2)}) collective-permute-start(bf16[2,512,128]{2,1,0:T(8,128)(2,1)S(1)} %collective-permute-done.3.refs_2_), channel_id=1, source_target_pairs={{0,8},{8,0},{16,24},{24,16},{32,40},{40,32},{48,56},{56,48},{64,72... | collective-permute-start | bytes 786440 | tf_op jit(solution)/shard_map/ppermute | solution.py:143
  22.7 13.5 %copy-start.1 = (bf16[2,512,128]{2,1,0:T(8,128)(2,1)}, bf16[2,512,128]{2,1,0:T(8,128)(2,1)S(1)}, u32[]{:S(2)}) copy-start(bf16[2,512,128]{2,1,0:T(8,128)(2,1)S(1)} %collective-permute-done.1.refs_0_) | copy-start | bytes 786436
  22.7 13.5 %collective-permute-start.2 = (bf16[2,512,128]{2,1,0:T(8,128)(2,1)S(1)}, bf16[2,512,128]{2,1,0:T(8,128)(2,1)S(1)}, u32[]{:S(2)}, u32[]{:S(2)}) collective-permute-start(bf16[2,512,128]{2,1,0:T(8,128)(2,1)S(1)} %collective-permute-done.1.refs_0_), channel_id=1, source_target_pairs={{0,8},{8,0},{16,24},{24,16},{32,40},{40,32},{48,56},{56,48},{64,72... | collective-permute-start | bytes 786440 | tf_op jit(solution)/shard_map/ppermute | solution.py:142
  28.6 7.6 %copy-start.2 = (bf16[2,512,128]{2,1,0:T(8,128)(2,1)}, bf16[2,512,128]{2,1,0:T(8,128)(2,1)S(1)}, u32[]{:S(2)}) copy-start(bf16[2,512,128]{2,1,0:T(8,128)(2,1)S(1)} %collective-permute-done.5.refs_4_) | copy-start | bytes 786436
  28.6 7.6 %collective-permute-start.6 = (bf16[2,512,128]{2,1,0:T(8,128)(2,1)S(1)}, bf16[2,512,128]{2,1,0:T(8,128)(2,1)S(1)}, u32[]{:S(2)}, u32[]{:S(2)}) collective-permute-start(bf16[2,512,128]{2,1,0:T(8,128)(2,1)S(1)} %collective-permute-done.5.refs_4_), channel_id=1, source_target_pairs={{0,8},{8,0},{16,24},{24,16},{32,40},{40,32},{48,56},{56,48},{64,72... | collective-permute-start | bytes 786440 | tf_op jit(solution)/shard_map/ppermute | solution.py:144
  29.1 0.7 copy-start.11
  36.1 0.7 copy-start.3
  36.2 0.8 copy-start.4
  36.2 0.9 copy-start.5
  43.4 14.2 %collective-permute-start.7 = (bf16[2,64,2048]{2,1,0:T(8,128)(2,1)}, bf16[2,64,2048]{2,1,0:T(8,128)(2,1)S(1)}, u32[]{:S(2)}, u32[]{:S(2)}) collective-permute-start(bf16[2,64,2048]{2,1,0:T(8,128)(2,1)} %get-tuple-element.17), channel_id=1, source_target_pairs={{0,2},{1,3},{2,0},{3,1},{4,6},{5,7},{6,4},{7,5},{8,10},{9,11},{10,... | collective-permute-start | bytes 1572872 | tf_op jit(solution)/shard_map/ppermute | solution.py:176
  44.9 15.6 %collective-permute-start.9 = (bf16[2,64,2048]{2,1,0:T(8,128)(2,1)}, bf16[2,64,2048]{2,1,0:T(8,128)(2,1)S(1)}, u32[]{:S(2)}, u32[]{:S(2)}) collective-permute-start(bf16[2,64,2048]{2,1,0:T(8,128)(2,1)} %get-tuple-element.19), channel_id=1, source_target_pairs={{0,6},{1,7},{2,4},{3,5},{4,2},{5,3},{6,0},{7,1},{8,14},{9,15},{10,... | collective-permute-start | bytes 1572872 | tf_op jit(solution)/shard_map/ppermute | solution.py:177
  46.7 10.9 %copy-start.8 = (bf16[2,64,2048]{2,1,0:T(8,128)(2,1)S(1)}, bf16[2,64,2048]{2,1,0:T(8,128)(2,1)}, u32[]{:S(2)}) copy-start(bf16[2,64,2048]{2,1,0:T(8,128)(2,1)} %get-tuple-element.18) | copy-start | bytes 1572868
  46.7 13.8 %copy-start.7 = (bf16[2,64,2048]{2,1,0:T(8,128)(2,1)S(1)}, bf16[2,64,2048]{2,1,0:T(8,128)(2,1)}, u32[]{:S(2)}) copy-start(bf16[2,64,2048]{2,1,0:T(8,128)(2,1)} %get-tuple-element.20) | copy-start | bytes 1572868
  53.1 28.5 %copy-start.10 = (bf16[2,64,2048]{2,1,0:T(8,128)(2,1)S(1)}, bf16[2,64,2048]{2,1,0:T(8,128)(2,1)}, u32[]{:S(2)}) copy-start(bf16[2,64,2048]{2,1,0:T(8,128)(2,1)} %get-tuple-element.22) | copy-start | bytes 1572868
  53.1 28.6 %copy-start.9 = (bf16[2,64,2048]{2,1,0:T(8,128)(2,1)S(1)}, bf16[2,64,2048]{2,1,0:T(8,128)(2,1)}, u32[]{:S(2)}) copy-start(bf16[2,64,2048]{2,1,0:T(8,128)(2,1)} %get-tuple-element.24) | copy-start | bytes 1572868
  53.1 15.7 %collective-permute-start.12 = (bf16[2,64,2048]{2,1,0:T(8,128)(2,1)}, bf16[2,64,2048]{2,1,0:T(8,128)(2,1)S(1)}, u32[]{:S(2)}, u32[]{:S(2)}) collective-permute-start(bf16[2,64,2048]{2,1,0:T(8,128)(2,1)} %get-tuple-element.21), channel_id=1, source_target_pairs={{0,2},{1,3},{2,0},{3,1},{4,6},{5,7},{6,4},{7,5},{8,10},{9,11},{10,... | collective-permute-start | bytes 1572872 | tf_op jit(solution)/shard_map/ppermute | solution.py:176
  53.5 19.1 %collective-permute-start.14 = (bf16[2,64,2048]{2,1,0:T(8,128)(2,1)}, bf16[2,64,2048]{2,1,0:T(8,128)(2,1)S(1)}, u32[]{:S(2)}, u32[]{:S(2)}) collective-permute-start(bf16[2,64,2048]{2,1,0:T(8,128)(2,1)} %get-tuple-element.23), channel_id=1, source_target_pairs={{0,6},{1,7},{2,4},{3,5},{4,2},{5,3},{6,0},{7,1},{8,14},{9,15},{10,... | collective-permute-start | bytes 1572872 | tf_op jit(solution)/shard_map/ppermute | solution.py:177
  57.7 19.4 %collective-permute-start.8 = (bf16[64,2048]{1,0:T(8,128)(2,1)S(1)}, bf16[64,2048]{1,0:T(8,128)(2,1)S(1)}, u32[]{:S(2)}, u32[]{:S(2)}) collective-permute-start(bf16[64,2048]{1,0:T(8,128)(2,1)S(1)} %fusion.2), channel_id=1, source_target_pairs={{0,6},{1,7},{2,4},{3,5},{4,2},{5,3},{6,0},{7,1},{8,14},{9,15},{10,... | collective-permute-start | bytes 786440 | tf_op jit(solution)/shard_map/ppermute | solution.py:180
  60.5 16.7 %collective-permute-start.10 = (bf16[64,2048]{1,0:T(8,128)(2,1)S(1)}, bf16[64,2048]{1,0:T(8,128)(2,1)S(1)}, u32[]{:S(2)}, u32[]{:S(2)}) collective-permute-start(bf16[64,2048]{1,0:T(8,128)(2,1)S(1)} %fusion.3), channel_id=1, source_target_pairs={{0,2},{1,3},{2,0},{3,1},{4,6},{5,7},{6,4},{7,5},{8,10},{9,11},{10,... | collective-permute-start | bytes 786440 | tf_op jit(solution)/shard_map/ppermute | solution.py:181
  69.8 11.8 %collective-permute-start.13 = (bf16[64,2048]{1,0:T(8,128)(2,1)S(1)}, bf16[64,2048]{1,0:T(8,128)(2,1)S(1)}, u32[]{:S(2)}, u32[]{:S(2)}) collective-permute-start(bf16[64,2048]{1,0:T(8,128)(2,1)S(1)} %fusion.4), channel_id=1, source_target_pairs={{0,6},{1,7},{2,4},{3,5},{4,2},{5,3},{6,0},{7,1},{8,14},{9,15},{10,... | collective-permute-start | bytes 786440 | tf_op jit(solution)/shard_map/ppermute | solution.py:180
  73.7 8.1 %collective-permute-start.15 = (bf16[64,2048]{1,0:T(8,128)(2,1)S(1)}, bf16[64,2048]{1,0:T(8,128)(2,1)S(1)}, u32[]{:S(2)}, u32[]{:S(2)}) collective-permute-start(bf16[64,2048]{1,0:T(8,128)(2,1)S(1)} %fusion.5), channel_id=1, source_target_pairs={{0,2},{1,3},{2,0},{3,1},{4,6},{5,7},{6,4},{7,5},{8,10},{9,11},{10,... | collective-permute-start | bytes 786440 | tf_op jit(solution)/shard_map/ppermute | solution.py:181
  77.4 8.3 %collective-permute-start.11 = (bf16[32,4096]{1,0:T(8,128)(2,1)S(1)}, bf16[32,4096]{1,0:T(8,128)(2,1)S(1)}, u32[]{:S(2)}, u32[]{:S(2)}) collective-permute-start(bf16[32,4096]{1,0:T(8,128)(2,1)S(1)} %pad_maximum_fusion.2), channel_id=1, source_target_pairs={{0,1},{1,0},{2,3},{3,2},{4,5},{5,4},{6,7},{7,6},{8,9},{9,8},{10,11... | collective-permute-start | bytes 786440 | tf_op jit(solution)/shard_map/ppermute | solution.py:190
  81.9 9.5 %collective-permute-start.16 = (bf16[32,4096]{1,0:T(8,128)(2,1)S(1)}, bf16[32,4096]{1,0:T(8,128)(2,1)S(1)}, u32[]{:S(2)}, u32[]{:S(2)}) collective-permute-start(bf16[32,4096]{1,0:T(8,128)(2,1)S(1)} %pad_maximum_fusion.3), channel_id=1, source_target_pairs={{0,1},{1,0},{2,3},{3,2},{4,5},{5,4},{6,7},{7,6},{8,9},{9,8},{10,11... | collective-permute-start | bytes 786440 | tf_op jit(solution)/shard_map/ppermute | solution.py:190

commit v7 on v6

--- a/solution.py
+++ b/solution.py
@@ -9,6 +9,7 @@
 HD = 128
 GROUP = 4
 NHEAD = 8
+W_STEPS = 4
 NX = 4
 NEG = -1.0e30
 SCALE2 = HD ** -0.5 * 1.4426950408889634
@@ -69,9 +70,16 @@
 
 def rest_kernel(doc, q_ref, m_in, acc_in, *refs):
     blocks, refs = refs[:6], refs[6:]
-    w_hbm, p_send, p_keep, q_send, q_keep, q_sc, m_sc, acc_sc, w_ref, a_sc, w_sem = refs
-    load = pltpu.make_async_copy(w_hbm, w_ref, w_sem)
-    load.start()
+    w_hbm, p_send, p_keep, q_send, q_keep, q_sc, m_sc, acc_sc, w_ref, a_sc, o_sc, w_sem, o_sem = refs
+    step = w_ref.shape[1] // W_STEPS
+    loads = [
+        pltpu.make_async_copy(
+            w_hbm.at[:, n * step:(n + 1) * step], w_ref.at[:, n * step:(n + 1) * step], w_sem.at[n]
+        )
+        for n in range(W_STEPS)
+    ]
+    for load in loads:
+        load.start()
     q_sc[...] = q_ref[...].reshape(q_sc.shape)
     m_sc[...] = m_in[...].reshape(m_sc.shape)
     acc_sc[...] = acc_in[...].reshape(acc_sc.shape)
@@ -91,21 +99,27 @@
         acc = acc_sc[g]
         out = (acc[:, :HD] / acc[:, HD:]).astype(BF16)
         a_sc[:, :, g * HD:(g + 1) * HD] = out.reshape(NX, -1, HD)
-    load.wait()
     x = lax.div(lax.axis_index("head"), 2)
     near, far = lax.bitwise_xor(x, 1), 3 - x
-    half = w_ref.shape[1] // 2
-    step = half // 2
-    for base, order, send, keep in (
-        (0, (near, 3 - near, x, far), p_send, p_keep),
-        (half, (far, lax.bitwise_xor(far, 1), x, near), q_send, q_keep),
-    ):
-        left = jnp.concatenate([a_sc[i] for i in order])
-        for n in range(0, half, step):
-            part = jnp.dot(left, w_ref[:, base + n:base + n + step], preferred_element_type=F32)
-            part = part.astype(BF16).reshape(2, 2, -1, step)
-            send[:, :, n:n + step] = part[0]
-            keep[:, :, n:n + step] = part[1]
+    sides = (
+        ((near, 3 - near, x, far), p_send, p_keep),
+        ((far, lax.bitwise_xor(far, 1), x, near), q_send, q_keep),
+    )
+    stores = []
+    for i, (order, *outs) in enumerate(sides):
+        left = jnp.concatenate([a_sc[j] for j in order])
+        for n in range(W_STEPS // 2):
+            k = i * (W_STEPS // 2) + n
+            loads[k].wait()
+            part = jnp.dot(left, w_ref[:, k * step:(k + 1) * step], preferred_element_type=F32)
+            o_sc[k] = part.astype(BF16).reshape(o_sc.shape[1:])
+            for j, out in enumerate(outs):
+                stores.append(pltpu.make_async_copy(
+                    o_sc.at[k, j], out.at[:, :, n * step:(n + 1) * step], o_sem.at[2 * k + j]
+                ))
+                stores[-1].start()
+    for store in stores:
+        store.wait()
 
 
 def add(*terms):
@@ -163,14 +177,15 @@
             grid=(1,),
             out_shape=[quad] * 4,
             in_specs=[SMEM] + specs + [VMEM] * 6 + [pl.BlockSpec(memory_space=pl.ANY)],
-            out_specs=[VMEM] * 4,
+            out_specs=[pl.BlockSpec(memory_space=pl.ANY)] * 4,
             scratch_shapes=vmem(
                 ((rows // 2, GROUP * HD), BF16),
                 ((GROUP, rows // 2, HD), F32),
                 ((GROUP, rows // 2, 2 * HD), F32),
                 (out_weight.shape, BF16),
                 ((NX, 2 * block, GROUP * HD), BF16),
-            ) + [pltpu.SemaphoreType.DMA],
+                ((W_STEPS, 2, 2, 2 * block, 2 * half // W_STEPS), BF16),
+            ) + [pltpu.SemaphoreType.DMA((W_STEPS,)), pltpu.SemaphoreType.DMA((2 * W_STEPS,))],
             compiler_params=PARAMS,
         )(doc_start, *shaped, far, far_o, near, near_o, cross, cross_o, out_weight)
         p_got = lax.ppermute(p_send, "head", to_near)

time: 92.6 us -> 92.4 us (level)
  the two profiles are of different devices: /device:TPU:97 before, /device:TPU:193 now
where the time goes in v7:
time: 92.4 us; the launch traced here: 92.1 us
  starting transfers between devices  33 us (36%)
  waiting for transfers between devices  27.6 us (30%)
  Pallas kernels  25.1 us (27%)
  other arithmetic  4.56 us (5%)
  local copies, waits for them, and re-layouts  1.59 us (2%)
    pallas_call x2, Pallas kernels, chunk(): pl.pallas_call(rest_kernel, grid=(1,), out_shape=[quad] * 4, in_specs=[SM...  18.8 us
    ppermute x2, waiting for transfers between devices, chunk(): p_got = lax.ppermute(p_send, 'head', to_near)  10.5 us
    ppermute x1, starting transfers between devices, on_device(): partner = lax.ppermute(own, 'ctx', swap)  8.56 us
    ppermute x2, waiting for transfers between devices, chunk(): got = lax.ppermute(total(1 - part).astype(BF16), 'head', to_part)  7.61 us
    pallas_call x1, Pallas kernels, on_device(): pl.pallas_call(own_kernel, out_shape=state, in_specs=[VMEM] * 4, out_spec...  6.32 us
    ppermute x2, waiting for transfers between devices, chunk(): p_last = lax.ppermute(p_next, 'head', to_far)  6.2 us
    ppermute x2, starting transfers between devices, chunk(): got = lax.ppermute(total(1 - part).astype(BF16), 'head', to_part)  5.26 us
    ppermute x1, starting transfers between devices, on_device(): cross_o = lax.ppermute(cross, 'ctx', swap)  3.83 us
  transfers between devices with their start and end apart: 17, of which 6 were waited for; matrix products, arithmetic and copies ran while one was open for 3% of the time, Pallas kernels for 17%

profile of v7, /device:TPU:193, one launch (start us, length us, event | category | flops | bytes accessed | tf_op | source)
XLA Modules:
  0.0 92.1 jit_solution(4148540252188906439)
XLA Ops:
  0.0 1.0 %pad_maximum_fusion.1.own = bf16[2,512,128]{2,1,0:T(8,128)(2,1)S(1)} fusion(bf16[1,512,128]{2,1,0:T(8,128)(2,1)} %bitcast.36, bf16[1,512,128]{2,1,0:T(8,128)(2,1)} %bitcast.37), kind=kLoop, calls=%fused_computation.13 | loop fusion | flops 131072 | bytes 524288 | tf_op jit(solution)/shard_map/stack | solution.py:136
  1.0 0.0 copy-start.6
  1.0 2.6 %collective-permute-start.3 = (bf16[2,512,128]{2,1,0:T(8,128)(2,1)S(1)}, bf16[2,512,128]{2,1,0:T(8,128)(2,1)S(1)}, u32[]{:S(2)}, u32[]{:S(2)}) collective-permute-start(bf16[2,512,128]{2,1,0:T(8,128)(2,1)S(1)} %pad_maximum_fusion.1.own), channel_id=1, source_target_pairs={{0,32},{8,40},{16,48},{24,56},{32,64},{40,72},{48,80},{56,88},{64,... | collective-permute-start | bytes 786440 | tf_op jit(solution)/shard_map/ppermute | solution.py:138
  3.7 3.2 %collective-permute-start.1 = (bf16[2,512,128]{2,1,0:T(8,128)(2,1)S(1)}, bf16[2,512,128]{2,1,0:T(8,128)(2,1)S(1)}, u32[]{:S(2)}, u32[]{:S(2)}) collective-permute-start(bf16[2,512,128]{2,1,0:T(8,128)(2,1)S(1)} %pad_maximum_fusion.1.own), channel_id=1, source_target_pairs={{0,16},{8,24},{16,64},{24,72},{32,48},{40,56},{48,96},{56,104},{64... | collective-permute-start | bytes 786440 | tf_op jit(solution)/shard_map/ppermute | solution.py:140
  6.9 3.2 %collective-permute-done.3.refs_2_ = bf16[2,512,128]{2,1,0:T(8,128)(2,1)S(1)} collective-permute-done((bf16[2,512,128]{2,1,0:T(8,128)(2,1)S(1)}, bf16[2,512,128]{2,1,0:T(8,128)(2,1)S(1)}, u32[]{:S(2)}, u32[]{:S(2)}) %collective-permute-start.3) | collective-permute-done | bytes 262176 | tf_op jit(solution)/shard_map/ppermute | solution.py:138
  10.1 1.3 %collective-permute-start.5 = (bf16[2,512,128]{2,1,0:T(8,128)(2,1)S(1)}, bf16[2,512,128]{2,1,0:T(8,128)(2,1)S(1)}, u32[]{:S(2)}, u32[]{:S(2)}) collective-permute-start(bf16[2,512,128]{2,1,0:T(8,128)(2,1)S(1)} %collective-permute-done.3.refs_2_), channel_id=1, source_target_pairs={{0,16},{8,24},{16,0},{24,8},{32,48},{40,56},{48,32},{56,40},{64,80... | collective-permute-start | bytes 786440 | tf_op jit(solution)/shard_map/ppermute | solution.py:155
  11.4 8.6 %collective-permute-start = (bf16[2,512,128]{2,1,0:T(8,128)(2,1)S(1)}, bf16[2,512,128]{2,1,0:T(8,128)(2,1)S(1)}, u32[]{:S(2)}, u32[]{:S(2)}) collective-permute-start(bf16[2,512,128]{2,1,0:T(8,128)(2,1)S(1)} %pad_maximum_fusion.1.own), channel_id=1, source_target_pairs={{0,8},{8,0},{16,24},{24,16},{32,40},{40,32},{48,56},{56,48},{64,72... | collective-permute-start | bytes 786440 | tf_op jit(solution)/shard_map/ppermute | solution.py:141
  20.0 0.0 collective-permute-start.4
  20.0 0.0 collective-permute-done.1.refs_0_
  20.0 0.5 collective-permute-start.2
  20.5 0.0 collective-permute-done.5.refs_4_
  20.5 3.8 %collective-permute-start.6 = (bf16[2,512,128]{2,1,0:T(8,128)(2,1)S(1)}, bf16[2,512,128]{2,1,0:T(8,128)(2,1)S(1)}, u32[]{:S(2)}, u32[]{:S(2)}) collective-permute-start(bf16[2,512,128]{2,1,0:T(8,128)(2,1)S(1)} %collective-permute-done.5.refs_4_), channel_id=1, source_target_pairs={{0,8},{8,0},{16,24},{24,16},{32,40},{40,32},{48,56},{56,48},{64,72... | collective-permute-start | bytes 786440 | tf_op jit(solution)/shard_map/ppermute | solution.py:158
  24.3 0.0 collective-permute-done.partner
  24.3 0.7 copy-done.11
  25.0 6.3 %shard_map.55 = (f32[4,512,128]{2,1,0:T(8,128)}, f32[4,512,256]{2,1,0:T(8,128)}) custom-call(bf16[512,512]{1,0:T(8,128)(2,1)} %q_ref.1, s32[4,128]{1,0:T(4,128)} %bitcast.38, bf16[2,512,128]{2,1,0:T(8,128)(2,1)} %copy-done.6, bf16[2,512,128]{2,1,0:T(8,128)(2,1)} %copy-done.11), custom_call_target="tpu_custom_call" | custom-call | tf_op jit(solution)/shard_map/pallas_call | solution.py:147
  31.3 0.0 collective-permute-done.4.refs_3_
  31.3 0.0 collective-permute-done.2.refs_1_
  31.4 0.7 copy-done.3
  32.0 0.1 copy-done.4
  32.2 0.1 copy-done.5
  32.2 9.5 %shard_map.56 = (bf16[2,64,2048]{2,1,0:T(8,128)(2,1)}, bf16[2,64,2048]{2,1,0:T(8,128)(2,1)}, bf16[2,64,2048]{2,1,0:T(8,128)(2,1)}, bf16[2,64,2048]{2,1,0:T(8,128)(2,1)}) custom-call(s32[512]{0:T(512)} %doc.3, bf16[8,2,32,512]{3,2,1,0:T(8,128)(2,1)} %bitcast.24, f32[4,8,2,32,128]{4,3,2,1,0:T(8,128)} %bitcast.26, f32[4,8,2,32,256]{4,3,2,1,0:T(8,128)} %bitcast.22, ...), custom_call_target="tpu_custom_call" | custom-call | tf_op jit(solution)/shard_map/pallas_call | solution.py:175
  41.7 1.3 %collective-permute-start.7 = (bf16[2,64,2048]{2,1,0:T(8,128)(2,1)}, bf16[2,64,2048]{2,1,0:T(8,128)(2,1)S(1)}, u32[]{:S(2)}, u32[]{:S(2)}) collective-permute-start(bf16[2,64,2048]{2,1,0:T(8,128)(2,1)} %get-tuple-element.17), channel_id=1, source_target_pairs={{0,2},{1,3},{2,0},{3,1},{4,6},{5,7},{6,4},{7,5},{8,10},{9,11},{10,... | collective-permute-start | bytes 1572872 | tf_op jit(solution)/shard_map/ppermute | solution.py:191
  43.0 1.8 %collective-permute-start.9 = (bf16[2,64,2048]{2,1,0:T(8,128)(2,1)}, bf16[2,64,2048]{2,1,0:T(8,128)(2,1)S(1)}, u32[]{:S(2)}, u32[]{:S(2)}) collective-permute-start(bf16[2,64,2048]{2,1,0:T(8,128)(2,1)} %get-tuple-element.19), channel_id=1, source_target_pairs={{0,6},{1,7},{2,4},{3,5},{4,2},{5,3},{6,0},{7,1},{8,14},{9,15},{10,... | collective-permute-start | bytes 1572872 | tf_op jit(solution)/shard_map/ppermute | solution.py:192
  44.9 9.3 %shard_map.57 = (bf16[2,64,2048]{2,1,0:T(8,128)(2,1)}, bf16[2,64,2048]{2,1,0:T(8,128)(2,1)}, bf16[2,64,2048]{2,1,0:T(8,128)(2,1)}, bf16[2,64,2048]{2,1,0:T(8,128)(2,1)}) custom-call(s32[512]{0:T(512)} %doc.3, bf16[8,2,32,512]{3,2,1,0:T(8,128)(2,1)} %bitcast.25, f32[4,8,2,32,128]{4,3,2,1,0:T(8,128)} %bitcast.27, f32[4,8,2,32,256]{4,3,2,1,0:T(8,128)} %bitcast.23, ...), custom_call_target="tpu_custom_call" | custom-call | tf_op jit(solution)/shard_map/pallas_call | solution.py:175
  54.2 0.4 collective-permute-start.12
  54.6 0.7 collective-permute-start.14
  55.3 0.1 fusion.2
  55.3 2.1 %collective-permute-start.8 = (bf16[64,2048]{1,0:T(8,128)(2,1)S(1)}, bf16[64,2048]{1,0:T(8,128)(2,1)S(1)}, u32[]{:S(2)}, u32[]{:S(2)}) collective-permute-start(bf16[64,2048]{1,0:T(8,128)(2,1)S(1)} %fusion.2), channel_id=1, source_target_pairs={{0,6},{1,7},{2,4},{3,5},{4,2},{5,3},{6,0},{7,1},{8,14},{9,15},{10,... | collective-permute-start | bytes 786440 | tf_op jit(solution)/shard_map/ppermute | solution.py:195
  57.5 0.1 fusion.3
  57.5 0.4 collective-permute-start.10
  57.9 10.5 %collective-permute-done.12 = bf16[2,64,2048]{2,1,0:T(8,128)(2,1)S(1)} collective-permute-done((bf16[2,64,2048]{2,1,0:T(8,128)(2,1)}, bf16[2,64,2048]{2,1,0:T(8,128)(2,1)S(1)}, u32[]{:S(2)}, u32[]{:S(2)}) %collective-permute-start.12) | collective-permute-done | bytes 524320 | tf_op jit(solution)/shard_map/ppermute | solution.py:191
  68.5 1.0 %fusion.4 = bf16[64,2048]{1,0:T(8,128)(2,1)S(1)} fusion(bf16[2,64,2048]{2,1,0:T(8,128)(2,1)S(1)} %collective-permute-done.12, bf16[2,64,2048]{2,1,0:T(8,128)(2,1)} %get-tuple-element.22), kind=kLoop, calls=%fused_computation.11 | loop fusion | flops 524288 | bytes 786432 | tf_op jit(solution)/shard_map/convert_element_type | solution.py:193
  69.5 0.9 %collective-permute-start.13 = (bf16[64,2048]{1,0:T(8,128)(2,1)S(1)}, bf16[64,2048]{1,0:T(8,128)(2,1)S(1)}, u32[]{:S(2)}, u32[]{:S(2)}) collective-permute-start(bf16[64,2048]{1,0:T(8,128)(2,1)S(1)} %fusion.4), channel_id=1, source_target_pairs={{0,6},{1,7},{2,4},{3,5},{4,2},{5,3},{6,0},{7,1},{8,14},{9,15},{10,... | collective-permute-start | bytes 786440 | tf_op jit(solution)/shard_map/ppermute | solution.py:195
  70.4 1.0 %fusion.5 = bf16[64,2048]{1,0:T(8,128)(2,1)S(1)} fusion(bf16[2,64,2048]{2,1,0:T(8,128)(2,1)S(1)} %collective-permute-done.14, bf16[2,64,2048]{2,1,0:T(8,128)(2,1)} %get-tuple-element.24), kind=kLoop, calls=%fused_computation.12 | loop fusion | flops 524288 | bytes 786432 | tf_op jit(solution)/shard_map/convert_element_type | solution.py:194
  71.4 0.1 collective-permute-start.15
  71.5 4.1 %collective-permute-done.8 = bf16[64,2048]{1,0:T(8,128)(2,1)S(1)} collective-permute-done((bf16[64,2048]{1,0:T(8,128)(2,1)S(1)}, bf16[64,2048]{1,0:T(8,128)(2,1)S(1)}, u32[]{:S(2)}, u32[]{:S(2)}) %collective-permute-start.8) | collective-permute-done | bytes 262176 | tf_op jit(solution)/shard_map/ppermute | solution.py:195
  75.6 0.1 add_convert_fusion.7
  75.7 0.1 add_convert_fusion.6
  75.9 2.7 %collective-permute-start.11 = (bf16[32,4096]{1,0:T(8,128)(2,1)S(1)}, bf16[32,4096]{1,0:T(8,128)(2,1)S(1)}, u32[]{:S(2)}, u32[]{:S(2)}) collective-permute-start(bf16[32,4096]{1,0:T(8,128)(2,1)S(1)} %pad_maximum_fusion.2), channel_id=1, source_target_pairs={{0,1},{1,0},{2,3},{3,2},{4,5},{5,4},{6,7},{7,6},{8,9},{9,8},{10,11... | collective-permute-start | bytes 786440 | tf_op jit(solution)/shard_map/ppermute | solution.py:205
  78.6 2.1 %collective-permute-done.13 = bf16[64,2048]{1,0:T(8,128)(2,1)S(1)} collective-permute-done((bf16[64,2048]{1,0:T(8,128)(2,1)S(1)}, bf16[64,2048]{1,0:T(8,128)(2,1)S(1)}, u32[]{:S(2)}, u32[]{:S(2)}) %collective-permute-start.13) | collective-permute-done | bytes 262176 | tf_op jit(solution)/shard_map/ppermute | solution.py:195
  80.7 0.1 add_convert_fusion.5
  80.8 0.1 add_convert_fusion.4
  81.0 2.6 %collective-permute-start.16 = (bf16[32,4096]{1,0:T(8,128)(2,1)S(1)}, bf16[32,4096]{1,0:T(8,128)(2,1)S(1)}, u32[]{:S(2)}, u32[]{:S(2)}) collective-permute-start(bf16[32,4096]{1,0:T(8,128)(2,1)S(1)} %pad_maximum_fusion.3), channel_id=1, source_target_pairs={{0,1},{1,0},{2,3},{3,2},{4,5},{5,4},{6,7},{7,6},{8,9},{9,8},{10,11... | collective-permute-start | bytes 786440 | tf_op jit(solution)/shard_map/ppermute | solution.py:205
  83.5 1.9 %collective-permute-done.11 = bf16[32,4096]{1,0:T(8,128)(2,1)S(1)} collective-permute-done((bf16[32,4096]{1,0:T(8,128)(2,1)S(1)}, bf16[32,4096]{1,0:T(8,128)(2,1)S(1)}, u32[]{:S(2)}, u32[]{:S(2)}) %collective-permute-start.11) | collective-permute-done | bytes 262176 | tf_op jit(solution)/shard_map/ppermute | solution.py:205
  85.4 0.1 fusion
  85.5 5.7 %collective-permute-done.16 = bf16[32,4096]{1,0:T(8,128)(2,1)S(1)} collective-permute-done((bf16[32,4096]{1,0:T(8,128)(2,1)S(1)}, bf16[32,4096]{1,0:T(8,128)(2,1)S(1)}, u32[]{:S(2)}, u32[]{:S(2)}) %collective-permute-start.16) | collective-permute-done | bytes 262176 | tf_op jit(solution)/shard_map/ppermute | solution.py:205
  91.2 0.1 fusion.1
  91.3 0.8 pad_maximum_fusion
  (27 shorter events, 0.1 us)
Async XLA Ops:
  1.0 23.3 %copy-start.6 = (bf16[2,512,128]{2,1,0:T(8,128)(2,1)}, bf16[2,512,128]{2,1,0:T(8,128)(2,1)S(1)}, u32[]{:S(2)}) copy-start(bf16[2,512,128]{2,1,0:T(8,128)(2,1)S(1)} %pad_maximum_fusion.1.own) | copy-start | bytes 786436
  1.0 9.1 %collective-permute-start.3 = (bf16[2,512,128]{2,1,0:T(8,128)(2,1)S(1)}, bf16[2,512,128]{2,1,0:T(8,128)(2,1)S(1)}, u32[]{:S(2)}, u32[]{:S(2)}) collective-permute-start(bf16[2,512,128]{2,1,0:T(8,128)(2,1)S(1)} %pad_maximum_fusion.1.own), channel_id=1, source_target_pairs={{0,32},{8,40},{16,48},{24,56},{32,64},{40,72},{48,80},{56,88},{64,... | collective-permute-start | bytes 786440 | tf_op jit(solution)/shard_map/ppermute | solution.py:138
  3.7 16.3 %collective-permute-start.1 = (bf16[2,512,128]{2,1,0:T(8,128)(2,1)S(1)}, bf16[2,512,128]{2,1,0:T(8,128)(2,1)S(1)}, u32[]{:S(2)}, u32[]{:S(2)}) collective-permute-start(bf16[2,512,128]{2,1,0:T(8,128)(2,1)S(1)} %pad_maximum_fusion.1.own), channel_id=1, source_target_pairs={{0,16},{8,24},{16,64},{24,72},{32,48},{40,56},{48,96},{56,104},{64... | collective-permute-start | bytes 786440 | tf_op jit(solution)/shard_map/ppermute | solution.py:140
  10.1 21.3 %copy-start = (bf16[2,512,128]{2,1,0:T(8,128)(2,1)}, bf16[2,512,128]{2,1,0:T(8,128)(2,1)S(1)}, u32[]{:S(2)}) copy-start(bf16[2,512,128]{2,1,0:T(8,128)(2,1)S(1)} %collective-permute-done.3.refs_2_) | copy-start | bytes 786436
  10.1 10.4 %collective-permute-start.5 = (bf16[2,512,128]{2,1,0:T(8,128)(2,1)S(1)}, bf16[2,512,128]{2,1,0:T(8,128)(2,1)S(1)}, u32[]{:S(2)}, u32[]{:S(2)}) collective-permute-start(bf16[2,512,128]{2,1,0:T(8,128)(2,1)S(1)} %collective-permute-done.3.refs_2_), channel_id=1, source_target_pairs={{0,16},{8,24},{16,0},{24,8},{32,48},{40,56},{48,32},{56,40},{64,80... | collective-permute-start | bytes 786440 | tf_op jit(solution)/shard_map/ppermute | solution.py:155
  11.4 12.9 %collective-permute-start = (bf16[2,512,128]{2,1,0:T(8,128)(2,1)S(1)}, bf16[2,512,128]{2,1,0:T(8,128)(2,1)S(1)}, u32[]{:S(2)}, u32[]{:S(2)}) collective-permute-start(bf16[2,512,128]{2,1,0:T(8,128)(2,1)S(1)} %pad_maximum_fusion.1.own), channel_id=1, source_target_pairs={{0,8},{8,0},{16,24},{24,16},{32,40},{40,32},{48,56},{56,48},{64,72... | collective-permute-start | bytes 786440 | tf_op jit(solution)/shard_map/ppermute | solution.py:141
  20.0 11.4 %collective-permute-start.4 = (bf16[2,512,128]{2,1,0:T(8,128)(2,1)S(1)}, bf16[2,512,128]{2,1,0:T(8,128)(2,1)S(1)}, u32[]{:S(2)}, u32[]{:S(2)}) collective-permute-start(bf16[2,512,128]{2,1,0:T(8,128)(2,1)S(1)} %collective-permute-done.3.refs_2_), channel_id=1, source_target_pairs={{0,8},{8,0},{16,24},{24,16},{32,40},{40,32},{48,56},{56,48},{64,72... | collective-permute-start | bytes 786440 | tf_op jit(solution)/shard_map/ppermute | solution.py:157
  20.0 11.4 %copy-start.1 = (bf16[2,512,128]{2,1,0:T(8,128)(2,1)}, bf16[2,512,128]{2,1,0:T(8,128)(2,1)S(1)}, u32[]{:S(2)}) copy-start(bf16[2,512,128]{2,1,0:T(8,128)(2,1)S(1)} %collective-permute-done.1.refs_0_) | copy-start | bytes 786436
  20.0 11.4 %collective-permute-start.2 = (bf16[2,512,128]{2,1,0:T(8,128)(2,1)S(1)}, bf16[2,512,128]{2,1,0:T(8,128)(2,1)S(1)}, u32[]{:S(2)}, u32[]{:S(2)}) collective-permute-start(bf16[2,512,128]{2,1,0:T(8,128)(2,1)S(1)} %collective-permute-done.1.refs_0_), channel_id=1, source_target_pairs={{0,8},{8,0},{16,24},{24,16},{32,40},{40,32},{48,56},{56,48},{64,72... | collective-permute-start | bytes 786440 | tf_op jit(solution)/shard_map/ppermute | solution.py:156
  20.5 10.9 %copy-start.2 = (bf16[2,512,128]{2,1,0:T(8,128)(2,1)}, bf16[2,512,128]{2,1,0:T(8,128)(2,1)S(1)}, u32[]{:S(2)}) copy-start(bf16[2,512,128]{2,1,0:T(8,128)(2,1)S(1)} %collective-permute-done.5.refs_4_) | copy-start | bytes 786436
  20.5 10.9 %collective-permute-start.6 = (bf16[2,512,128]{2,1,0:T(8,128)(2,1)S(1)}, bf16[2,512,128]{2,1,0:T(8,128)(2,1)S(1)}, u32[]{:S(2)}, u32[]{:S(2)}) collective-permute-start(bf16[2,512,128]{2,1,0:T(8,128)(2,1)S(1)} %collective-permute-done.5.refs_4_), channel_id=1, source_target_pairs={{0,8},{8,0},{16,24},{24,16},{32,40},{40,32},{48,56},{56,48},{64,72... | collective-permute-start | bytes 786440 | tf_op jit(solution)/shard_map/ppermute | solution.py:158
  24.3 0.7 copy-start.11
  31.3 0.7 copy-start.3
  31.3 0.8 copy-start.4
  31.4 0.9 copy-start.5
  41.7 13.6 %collective-permute-start.7 = (bf16[2,64,2048]{2,1,0:T(8,128)(2,1)}, bf16[2,64,2048]{2,1,0:T(8,128)(2,1)S(1)}, u32[]{:S(2)}, u32[]{:S(2)}) collective-permute-start(bf16[2,64,2048]{2,1,0:T(8,128)(2,1)} %get-tuple-element.17), channel_id=1, source_target_pairs={{0,2},{1,3},{2,0},{3,1},{4,6},{5,7},{6,4},{7,5},{8,10},{9,11},{10,... | collective-permute-start | bytes 1572872 | tf_op jit(solution)/shard_map/ppermute | solution.py:191
  43.0 14.4 %collective-permute-start.9 = (bf16[2,64,2048]{2,1,0:T(8,128)(2,1)}, bf16[2,64,2048]{2,1,0:T(8,128)(2,1)S(1)}, u32[]{:S(2)}, u32[]{:S(2)}) collective-permute-start(bf16[2,64,2048]{2,1,0:T(8,128)(2,1)} %get-tuple-element.19), channel_id=1, source_target_pairs={{0,6},{1,7},{2,4},{3,5},{4,2},{5,3},{6,0},{7,1},{8,14},{9,15},{10,... | collective-permute-start | bytes 1572872 | tf_op jit(solution)/shard_map/ppermute | solution.py:192
  44.8 10.4 %copy-start.8 = (bf16[2,64,2048]{2,1,0:T(8,128)(2,1)S(1)}, bf16[2,64,2048]{2,1,0:T(8,128)(2,1)}, u32[]{:S(2)}) copy-start(bf16[2,64,2048]{2,1,0:T(8,128)(2,1)} %get-tuple-element.18) | copy-start | bytes 1572868
  44.8 12.6 %copy-start.7 = (bf16[2,64,2048]{2,1,0:T(8,128)(2,1)S(1)}, bf16[2,64,2048]{2,1,0:T(8,128)(2,1)}, u32[]{:S(2)}) copy-start(bf16[2,64,2048]{2,1,0:T(8,128)(2,1)} %get-tuple-element.20) | copy-start | bytes 1572868
  54.2 26.5 %copy-start.10 = (bf16[2,64,2048]{2,1,0:T(8,128)(2,1)S(1)}, bf16[2,64,2048]{2,1,0:T(8,128)(2,1)}, u32[]{:S(2)}) copy-start(bf16[2,64,2048]{2,1,0:T(8,128)(2,1)} %get-tuple-element.22) | copy-start | bytes 1572868
  54.2 26.6 %copy-start.9 = (bf16[2,64,2048]{2,1,0:T(8,128)(2,1)S(1)}, bf16[2,64,2048]{2,1,0:T(8,128)(2,1)}, u32[]{:S(2)}) copy-start(bf16[2,64,2048]{2,1,0:T(8,128)(2,1)} %get-tuple-element.24) | copy-start | bytes 1572868
  54.2 14.2 %collective-permute-start.12 = (bf16[2,64,2048]{2,1,0:T(8,128)(2,1)}, bf16[2,64,2048]{2,1,0:T(8,128)(2,1)S(1)}, u32[]{:S(2)}, u32[]{:S(2)}) collective-permute-start(bf16[2,64,2048]{2,1,0:T(8,128)(2,1)} %get-tuple-element.21), channel_id=1, source_target_pairs={{0,2},{1,3},{2,0},{3,1},{4,6},{5,7},{6,4},{7,5},{8,10},{9,11},{10,... | collective-permute-start | bytes 1572872 | tf_op jit(solution)/shard_map/ppermute | solution.py:191
  54.6 15.8 %collective-permute-start.14 = (bf16[2,64,2048]{2,1,0:T(8,128)(2,1)}, bf16[2,64,2048]{2,1,0:T(8,128)(2,1)S(1)}, u32[]{:S(2)}, u32[]{:S(2)}) collective-permute-start(bf16[2,64,2048]{2,1,0:T(8,128)(2,1)} %get-tuple-element.23), channel_id=1, source_target_pairs={{0,6},{1,7},{2,4},{3,5},{4,2},{5,3},{6,0},{7,1},{8,14},{9,15},{10,... | collective-permute-start | bytes 1572872 | tf_op jit(solution)/shard_map/ppermute | solution.py:192
  55.3 20.3 %collective-permute-start.8 = (bf16[64,2048]{1,0:T(8,128)(2,1)S(1)}, bf16[64,2048]{1,0:T(8,128)(2,1)S(1)}, u32[]{:S(2)}, u32[]{:S(2)}) collective-permute-start(bf16[64,2048]{1,0:T(8,128)(2,1)S(1)} %fusion.2), channel_id=1, source_target_pairs={{0,6},{1,7},{2,4},{3,5},{4,2},{5,3},{6,0},{7,1},{8,14},{9,15},{10,... | collective-permute-start | bytes 786440 | tf_op jit(solution)/shard_map/ppermute | solution.py:195
  57.5 18.2 %collective-permute-start.10 = (bf16[64,2048]{1,0:T(8,128)(2,1)S(1)}, bf16[64,2048]{1,0:T(8,128)(2,1)S(1)}, u32[]{:S(2)}, u32[]{:S(2)}) collective-permute-start(bf16[64,2048]{1,0:T(8,128)(2,1)S(1)} %fusion.3), channel_id=1, source_target_pairs={{0,2},{1,3},{2,0},{3,1},{4,6},{5,7},{6,4},{7,5},{8,10},{9,11},{10,... | collective-permute-start | bytes 786440 | tf_op jit(solution)/shard_map/ppermute | solution.py:196
  69.5 11.2 %collective-permute-start.13 = (bf16[64,2048]{1,0:T(8,128)(2,1)S(1)}, bf16[64,2048]{1,0:T(8,128)(2,1)S(1)}, u32[]{:S(2)}, u32[]{:S(2)}) collective-permute-start(bf16[64,2048]{1,0:T(8,128)(2,1)S(1)} %fusion.4), channel_id=1, source_target_pairs={{0,6},{1,7},{2,4},{3,5},{4,2},{5,3},{6,0},{7,1},{8,14},{9,15},{10,... | collective-permute-start | bytes 786440 | tf_op jit(solution)/shard_map/ppermute | solution.py:195
  71.4 9.4 %collective-permute-start.15 = (bf16[64,2048]{1,0:T(8,128)(2,1)S(1)}, bf16[64,2048]{1,0:T(8,128)(2,1)S(1)}, u32[]{:S(2)}, u32[]{:S(2)}) collective-permute-start(bf16[64,2048]{1,0:T(8,128)(2,1)S(1)} %fusion.5), channel_id=1, source_target_pairs={{0,2},{1,3},{2,0},{3,1},{4,6},{5,7},{6,4},{7,5},{8,10},{9,11},{10,... | collective-permute-start | bytes 786440 | tf_op jit(solution)/shard_map/ppermute | solution.py:196
  75.9 9.6 %collective-permute-start.11 = (bf16[32,4096]{1,0:T(8,128)(2,1)S(1)}, bf16[32,4096]{1,0:T(8,128)(2,1)S(1)}, u32[]{:S(2)}, u32[]{:S(2)}) collective-permute-start(bf16[32,4096]{1,0:T(8,128)(2,1)S(1)} %pad_maximum_fusion.2), channel_id=1, source_target_pairs={{0,1},{1,0},{2,3},{3,2},{4,5},{5,4},{6,7},{7,6},{8,9},{9,8},{10,11... | collective-permute-start | bytes 786440 | tf_op jit(solution)/shard_map/ppermute | solution.py:205
  81.0 10.2 %collective-permute-start.16 = (bf16[32,4096]{1,0:T(8,128)(2,1)S(1)}, bf16[32,4096]{1,0:T(8,128)(2,1)S(1)}, u32[]{:S(2)}, u32[]{:S(2)}) collective-permute-start(bf16[32,4096]{1,0:T(8,128)(2,1)S(1)} %pad_maximum_fusion.3), channel_id=1, source_target_pairs={{0,1},{1,0},{2,3},{3,2},{4,5},{5,4},{6,7},{7,6},{8,9},{9,8},{10,11... | collective-permute-start | bytes 786440 | tf_op jit(solution)/shard_map/ppermute | solution.py:205

commit v8 on v7

--- a/solution.py
+++ b/solution.py
@@ -51,25 +51,45 @@
         m_sc[g] = m_new
 
 
-def own_kernel(q_ref, doc_ref, own, partner, m_ref, acc_ref):
-    rows = q_ref.shape[0]
-    ctx = lax.axis_index("ctx")
-    r = lax.broadcasted_iota(jnp.int32, (rows, rows), 0)
-    c = lax.broadcasted_iota(jnp.int32, (rows, rows), 1)
+def own_docs(doc_ref, rows):
     groups, lanes = doc_ref.shape
     doc = jnp.concatenate([
         jnp.broadcast_to(doc_ref[i:i + 1], (lanes, lanes)).T for i in range(groups)
-    ]) - ctx * rows
-    doc = jnp.tile(doc, (1, rows // lanes))
+    ]) - lax.axis_index("ctx") * rows
+    return jnp.tile(doc, (1, rows // lanes))
+
+
+def own_kernel(q_ref, doc_ref, own, m_ref, acc_ref):
+    rows = q_ref.shape[0]
+    r = lax.broadcasted_iota(jnp.int32, (rows, rows), 0)
+    c = lax.broadcasted_iota(jnp.int32, (rows, rows), 1)
+    doc = own_docs(doc_ref, rows)
     visit(q_ref, own[0], own[1], (c >= doc) & (c <= r), m_ref, acc_ref, True)
+
+
+def middle_kernel(first, q_ref, doc_ref, m_in, acc_in, partner, near, near_o, m_ref, acc_ref):
+    rows = q_ref.shape[0]
+    m_ref[...] = m_in[...]
+    acc_ref[...] = acc_in[...]
+    ctx = lax.axis_index("ctx")
 
     @pl.when(lax.rem(ctx, 2) == 1)
     def _():
-        visit(q_ref, partner[0], partner[1], c - rows >= doc, m_ref, acc_ref, False)
+        c = lax.broadcasted_iota(jnp.int32, (rows, rows), 1)
+        seen = c - rows >= own_docs(doc_ref, rows)
+        visit(q_ref, partner[0], partner[1], seen, m_ref, acc_ref, False)
+
+    other = lax.div(ctx, 2) - 2
+
+    @pl.when((other >= 0) & (other * 2 * rows >= first[0]))
+    def _():
+        k = jnp.concatenate([near[0], near_o[0]], axis=0)
+        v = jnp.concatenate([near[1], near_o[1]], axis=0)
+        visit(q_ref, k, v, None, m_ref, acc_ref, False)
 
 
 def rest_kernel(doc, q_ref, m_in, acc_in, *refs):
-    blocks, refs = refs[:6], refs[6:]
+    blocks, refs = refs[:4], refs[4:]
     w_hbm, p_send, p_keep, q_send, q_keep, q_sc, m_sc, acc_sc, w_ref, a_sc, o_sc, w_sem, o_sem = refs
     step = w_ref.shape[1] // W_STEPS
     loads = [
@@ -86,7 +106,7 @@
     cell = lax.div(lax.axis_index("ctx"), 2)
     odd = lax.rem(cell, 2)
     size = blocks[0].shape[1] * 2
-    for i, other in enumerate((cell - 3 + 2 * odd, cell - 2, cell - 1 - 2 * odd)):
+    for i, other in enumerate((cell - 3 + 2 * odd, cell - 1 - 2 * odd)):
         a, b = blocks[2 * i:2 * i + 2]
 
         @pl.when((other >= 0) & (other * size >= doc[0]))
@@ -131,31 +151,40 @@
 
 def on_device(queries, keys, values, doc_start, out_weight):
     rows = queries.shape[0]
+    ctx = lax.axis_index("ctx")
     n_ctx = lax.axis_size("ctx")
     swap = [(c, c ^ 1) for c in range(n_ctx)]
     own = jnp.stack([keys, values])
 
     near = lax.ppermute(own, "ctx", [(c, c + 4) for c in range(n_ctx - 4)])
-    jump = [(c, c + (6 if c // 2 % 2 else 2)) for c in range(n_ctx)]
-    far = lax.ppermute(own, "ctx", [(c, t) for c, t in jump if t < n_ctx])
+    passed = jnp.where(ctx // 2 % 2 == 1, near, own)
+    far = lax.ppermute(passed, "ctx", [(c, c + 2) for c in range(n_ctx - 2)])
     partner = lax.ppermute(own, "ctx", swap)
 
     state = (
         jax.ShapeDtypeStruct((GROUP, rows, HD), F32),
         jax.ShapeDtypeStruct((GROUP, rows, 2 * HD), F32),
     )
+    docs = doc_start.reshape(-1, HD)
     m, acc = pl.pallas_call(
         own_kernel,
         out_shape=state,
-        in_specs=[VMEM] * 4,
+        in_specs=[VMEM] * 3,
         out_specs=[VMEM] * 2,
         compiler_params=PARAMS,
-    )(queries, doc_start.reshape(-1, HD), own, partner)
+    )(queries, docs, own)
 
     cross = lax.ppermute(near, "ctx", [(c, c ^ 2) for c in range(n_ctx)])
     far_o = lax.ppermute(far, "ctx", swap)
     near_o = lax.ppermute(near, "ctx", swap)
     cross_o = lax.ppermute(cross, "ctx", swap)
+    m, acc = pl.pallas_call(
+        middle_kernel,
+        out_shape=state,
+        in_specs=[SMEM] + [VMEM] * 7,
+        out_specs=[VMEM] * 2,
+        compiler_params=PARAMS,
+    )(doc_start, queries, docs, m, acc, partner, near, near_o)
     part = lax.axis_index("head") % 2
     half = out_weight.shape[1] // 2
     block = rows // NHEAD // 2
@@ -176,7 +205,7 @@
             rest_kernel,
             grid=(1,),
             out_shape=[quad] * 4,
-            in_specs=[SMEM] + specs + [VMEM] * 6 + [pl.BlockSpec(memory_space=pl.ANY)],
+            in_specs=[SMEM] + specs + [VMEM] * 4 + [pl.BlockSpec(memory_space=pl.ANY)],
             out_specs=[pl.BlockSpec(memory_space=pl.ANY)] * 4,
             scratch_shapes=vmem(
                 ((rows // 2, GROUP * HD), BF16),
@@ -187,7 +216,7 @@
                 ((W_STEPS, 2, 2, 2 * block, 2 * half // W_STEPS), BF16),
             ) + [pltpu.SemaphoreType.DMA((W_STEPS,)), pltpu.SemaphoreType.DMA((2 * W_STEPS,))],
             compiler_params=PARAMS,
-        )(doc_start, *shaped, far, far_o, near, near_o, cross, cross_o, out_weight)
+        )(doc_start, *shaped, far, far_o, cross, cross_o, out_weight)
         p_got = lax.ppermute(p_send, "head", to_near)
         q_got = lax.ppermute(q_send, "head", to_far)
         p_next = add(p_got[1], p_keep[1]).astype(BF16)
@@ -205,7 +234,10 @@
         got = lax.ppermute(total(1 - part).astype(BF16), "head", to_part)
         return (total(part) + got.astype(F32)).astype(BF16)
 
-    return jnp.concatenate([chunk(0), chunk(1)])
+    mixed = jnp.zeros((2 * block, 2 * half), BF16)
+    for k in range(2):
+        mixed = lax.dynamic_update_slice(mixed, chunk(k), (k * block, 0))
+    return mixed
 
 
 def solution(mesh):

time: 92.4 us -> 99.7 us (1.079)
  waiting for transfers between devices: 27.6 us -> 38.1 us
  starting transfers between devices: 33 us -> 26.3 us
  Pallas kernels: 25.1 us -> 28.5 us
    ppermute x2, waiting for transfers between devices: 0.01 us -> 10.2 us  [chunk(): q_got = lax.ppermute(q_send, 'head', to_far)]
    ppermute x2, waiting for transfers between devices: 10.5 us -> 2.65 us  [chunk(): p_got = lax.ppermute(p_send, 'head', to_near)]
    pallas_call x1 -> x2, Pallas kernels: 6.32 us -> 12.9 us  [the longest x1 8.85 us: on_device(): pl.pallas_call(middle_kernel, out_shape=state, in_specs=[SMEM] + [VMEM] *...]
    ppermute x1, starting transfers between devices: 8.56 us -> 2.09 us  [on_device(): partner = lax.ppermute(own, 'ctx', swap)]
    ppermute x2, waiting for transfers between devices: 6.2 us -> 0.01 us  [chunk(): p_last = lax.ppermute(p_next, 'head', to_far)]
    ppermute x1, waiting for transfers between devices: 0.01 us -> 4.94 us  [on_device(): cross = lax.ppermute(near, 'ctx', [(c, c ^ 2) for c in range(n_ctx)])]
    ppermute x2, waiting for transfers between devices: 0.01 us -> 4.33 us  [chunk(): q_last = lax.ppermute(q_next, 'head', to_near)]
    ppermute x1, starting transfers between devices: 3.83 us -> 0.49 us  [on_device(): cross_o = lax.ppermute(cross, 'ctx', swap)]
  transfers between devices with their start and end apart: 17 -> 17, of which waited for: 6 -> 11; matrix products, arithmetic and copies ran while one was open for 3% -> 2% of each run, Pallas kernels for 17% -> 21%
where the time goes in v8:
time: 99.7 us; the launch traced here: 99.5 us
  waiting for transfers between devices  38.1 us (38%)
  Pallas kernels  28.5 us (29%)
  starting transfers between devices  26.3 us (26%)
  other arithmetic  4.78 us (5%)
  local copies, waits for them, and re-layouts  1.61 us (2%)
    pallas_call x2, Pallas kernels, chunk(): pl.pallas_call(rest_kernel, grid=(1,), out_shape=[quad] * 4, in_specs=[SM...  15.6 us
    ppermute x2, waiting for transfers between devices, chunk(): q_got = lax.ppermute(q_send, 'head', to_far)  10.2 us
    pallas_call x1, Pallas kernels, on_device(): pl.pallas_call(middle_kernel, out_shape=state, in_specs=[SMEM] + [VMEM] *...  8.85 us
    ppermute x2, waiting for transfers between devices, chunk(): got = lax.ppermute(total(1 - part).astype(BF16), 'head', to_part)  6.42 us
    ppermute x1, waiting for transfers between devices, on_device(): near = lax.ppermute(own, 'ctx', [(c, c + 4) for c in range(n_ctx - 4)])  6.4 us
    ppermute x2, starting transfers between devices, chunk(): got = lax.ppermute(total(1 - part).astype(BF16), 'head', to_part)  6 us
    ppermute x1, waiting for transfers between devices, on_device(): cross = lax.ppermute(near, 'ctx', [(c, c ^ 2) for c in range(n_ctx)])  4.94 us
    ppermute x2, waiting for transfers between devices, chunk(): q_last = lax.ppermute(q_next, 'head', to_near)  4.33 us
  transfers between devices with their start and end apart: 17, of which 11 were waited for; matrix products, arithmetic and copies ran while one was open for 2% of the time, Pallas kernels for 21%

profile of v8, /device:TPU:193, one launch (start us, length us, event | category | flops | bytes accessed | tf_op | source)
XLA Modules:
  0.0 99.5 jit_solution(6387856012642346317)
XLA Ops:
  0.0 1.0 pad_maximum_fusion.1.own
  1.0 0.0 copy-start.4
  1.0 2.6 %collective-permute-start.1 = (bf16[2,512,128]{2,1,0:T(8,128)(2,1)S(1)}, bf16[2,512,128]{2,1,0:T(8,128)(2,1)S(1)}, u32[]{:S(2)}, u32[]{:S(2)}) collective-permute-start(bf16[2,512,128]{2,1,0:T(8,128)(2,1)S(1)} %pad_maximum_fusion.1.own), channel_id=1, source_target_pairs={{0,32},{8,40},{16,48},{24,56},{32,64},{40,72},{48,80},{56,88},{64,... | collective-permute-start | bytes 786440 | tf_op jit(solution)/shard_map/ppermute | solution.py:159
  3.7 6.4 %collective-permute-done.1.near = bf16[2,512,128]{2,1,0:T(8,128)(2,1)S(1)} collective-permute-done((bf16[2,512,128]{2,1,0:T(8,128)(2,1)S(1)}, bf16[2,512,128]{2,1,0:T(8,128)(2,1)S(1)}, u32[]{:S(2)}, u32[]{:S(2)}) %collective-permute-start.1) | collective-permute-done | bytes 262176 | tf_op jit(solution)/shard_map/ppermute | solution.py:159
  10.1 1.1 %broadcast_select_fusion = bf16[2,512,128]{2,1,0:T(8,128)(2,1)S(1)} fusion(bf16[2,512,128]{2,1,0:T(8,128)(2,1)S(1)} %collective-permute-done.1.near, pred[]{:T(512)S(6)} %eq.6, bf16[1,512,128]{2,1,0:T(8,128)(2,1)} %bitcast.37, bf16[1,512,128]{2,1,0:T(8,128)(2,1)} %bitcast.39), kind=kLoop, calls=%fused_computation.24 | loop fusion | flops 262144 | bytes 786433 | tf_op jit(solution)/shard_map/jit(_where)/select_n | solution.py:160
  11.2 3.2 %collective-permute-start.3 = (bf16[2,512,128]{2,1,0:T(8,128)(2,1)S(1)}, bf16[2,512,128]{2,1,0:T(8,128)(2,1)S(1)}, u32[]{:S(2)}, u32[]{:S(2)}) collective-permute-start(bf16[2,512,128]{2,1,0:T(8,128)(2,1)S(1)} %broadcast_select_fusion), channel_id=1, source_target_pairs={{0,16},{8,24},{16,32},{24,40},{32,48},{40,56},{48,64},{56,72},{64,... | collective-permute-start | bytes 786440 | tf_op jit(solution)/shard_map/ppermute | solution.py:161
  14.4 0.7 collective-permute-start.5
  15.1 2.1 %collective-permute-start = (bf16[2,512,128]{2,1,0:T(8,128)(2,1)S(1)}, bf16[2,512,128]{2,1,0:T(8,128)(2,1)S(1)}, u32[]{:S(2)}, u32[]{:S(2)}) collective-permute-start(bf16[2,512,128]{2,1,0:T(8,128)(2,1)S(1)} %pad_maximum_fusion.1.own), channel_id=1, source_target_pairs={{0,8},{8,0},{16,24},{24,16},{32,40},{40,32},{48,56},{56,48},{64,72... | collective-permute-start | bytes 786440 | tf_op jit(solution)/shard_map/ppermute | solution.py:162
  17.2 3.2 %collective-permute-done.3.refs_0_ = bf16[2,512,128]{2,1,0:T(8,128)(2,1)S(1)} collective-permute-done((bf16[2,512,128]{2,1,0:T(8,128)(2,1)S(1)}, bf16[2,512,128]{2,1,0:T(8,128)(2,1)S(1)}, u32[]{:S(2)}, u32[]{:S(2)}) %collective-permute-start.3) | collective-permute-done | bytes 262176 | tf_op jit(solution)/shard_map/ppermute | solution.py:161
  20.4 2.5 %collective-permute-start.4 = (bf16[2,512,128]{2,1,0:T(8,128)(2,1)S(1)}, bf16[2,512,128]{2,1,0:T(8,128)(2,1)S(1)}, u32[]{:S(2)}, u32[]{:S(2)}) collective-permute-start(bf16[2,512,128]{2,1,0:T(8,128)(2,1)S(1)} %collective-permute-done.3.refs_0_), channel_id=1, source_target_pairs={{0,8},{8,0},{16,24},{24,16},{32,40},{40,32},{48,56},{56,48},{64,72... | collective-permute-start | bytes 786440 | tf_op jit(solution)/shard_map/ppermute | solution.py:178
  22.9 4.9 %collective-permute-done.5.refs_2_ = bf16[2,512,128]{2,1,0:T(8,128)(2,1)S(1)} collective-permute-done((bf16[2,512,128]{2,1,0:T(8,128)(2,1)S(1)}, bf16[2,512,128]{2,1,0:T(8,128)(2,1)S(1)}, u32[]{:S(2)}, u32[]{:S(2)}) %collective-permute-start.5) | collective-permute-done | bytes 262176 | tf_op jit(solution)/shard_map/ppermute | solution.py:177
  27.8 0.5 collective-permute-start.6
  28.3 4.1 %shard_map.55 = (f32[4,512,128]{2,1,0:T(8,128)}, f32[4,512,256]{2,1,0:T(8,128)}) custom-call(bf16[512,512]{1,0:T(8,128)(2,1)} %q_ref.3, s32[4,128]{1,0:T(4,128)} %bitcast.40, bf16[2,512,128]{2,1,0:T(8,128)(2,1)} %copy-done.4), custom_call_target="tpu_custom_call" | custom-call | tf_op jit(solution)/shard_map/pallas_call | solution.py:169
  32.4 0.7 copy-done.10
  33.1 0.1 copy-done.11
  33.2 8.8 %shard_map.56 = (f32[4,512,128]{2,1,0:T(8,128)}, f32[4,512,256]{2,1,0:T(8,128)}) custom-call(s32[512]{0:T(512)} %doc.3, bf16[512,512]{1,0:T(8,128)(2,1)} %q_ref.3, s32[4,128]{1,0:T(4,128)} %bitcast.41, f32[4,512,128]{2,1,0:T(8,128)} %get-tuple-element.17.m_in, f32[4,512,256]{2,1,0:T(8,128)} %get-tuple-element.18.acc_in, bf16[2,512,128]{2,1,0:T(8,128)(2,1)} %copy-done.10, ...), custom_call_target="tpu_custom_call" | custom-call | tf_op jit(solution)/shard_map/pallas_call | solution.py:181
  42.1 0.7 copy-done.2
  42.8 0.1 copy-done.3
  42.9 7.8 %shard_map.58 = (bf16[2,64,2048]{2,1,0:T(8,128)(2,1)}, bf16[2,64,2048]{2,1,0:T(8,128)(2,1)}, bf16[2,64,2048]{2,1,0:T(8,128)(2,1)}, bf16[2,64,2048]{2,1,0:T(8,128)(2,1)}) custom-call(s32[512]{0:T(512)} %doc.3, bf16[8,2,32,512]{3,2,1,0:T(8,128)(2,1)} %bitcast.24, f32[4,8,2,32,128]{4,3,2,1,0:T(8,128)} %bitcast.26, f32[4,8,2,32,256]{4,3,2,1,0:T(8,128)} %bitcast.22, ...), custom_call_target="tpu_custom_call" | custom-call | tf_op jit(solution)/shard_map/pallas_call | solution.py:204
  50.7 2.6 %collective-permute-start.14 = (bf16[2,64,2048]{2,1,0:T(8,128)(2,1)}, bf16[2,64,2048]{2,1,0:T(8,128)(2,1)S(1)}, u32[]{:S(2)}, u32[]{:S(2)}) collective-permute-start(bf16[2,64,2048]{2,1,0:T(8,128)(2,1)} %get-tuple-element.27), channel_id=1, source_target_pairs={{0,6},{1,7},{2,4},{3,5},{4,2},{5,3},{6,0},{7,1},{8,14},{9,15},{10,... | collective-permute-start | bytes 1572872 | tf_op jit(solution)/shard_map/ppermute | solution.py:221
  53.3 7.8 %shard_map.57 = (bf16[2,64,2048]{2,1,0:T(8,128)(2,1)}, bf16[2,64,2048]{2,1,0:T(8,128)(2,1)}, bf16[2,64,2048]{2,1,0:T(8,128)(2,1)}, bf16[2,64,2048]{2,1,0:T(8,128)(2,1)}) custom-call(s32[512]{0:T(512)} %doc.3, bf16[8,2,32,512]{3,2,1,0:T(8,128)(2,1)} %bitcast.25, f32[4,8,2,32,128]{4,3,2,1,0:T(8,128)} %bitcast.27, f32[4,8,2,32,256]{4,3,2,1,0:T(8,128)} %bitcast.23, ...), custom_call_target="tpu_custom_call" | custom-call | tf_op jit(solution)/shard_map/pallas_call | solution.py:204
  61.1 0.9 collective-permute-start.9
  61.9 0.8 collective-permute-start.7
  62.7 2.6 %collective-permute-done.14 = bf16[2,64,2048]{2,1,0:T(8,128)(2,1)S(1)} collective-permute-done((bf16[2,64,2048]{2,1,0:T(8,128)(2,1)}, bf16[2,64,2048]{2,1,0:T(8,128)(2,1)S(1)}, u32[]{:S(2)}, u32[]{:S(2)}) %collective-permute-start.14) | collective-permute-done | bytes 524320 | tf_op jit(solution)/shard_map/ppermute | solution.py:221
  65.3 0.1 fusion.5
  65.4 0.1 collective-permute-start.15
  65.5 1.9 %collective-permute-done.12 = bf16[2,64,2048]{2,1,0:T(8,128)(2,1)S(1)} collective-permute-done((bf16[2,64,2048]{2,1,0:T(8,128)(2,1)}, bf16[2,64,2048]{2,1,0:T(8,128)(2,1)S(1)}, u32[]{:S(2)}, u32[]{:S(2)}) %collective-permute-start.12) | collective-permute-done | bytes 524320 | tf_op jit(solution)/shard_map/ppermute | solution.py:220
  67.4 0.1 fusion.4
  67.5 1.5 %collective-permute-start.13 = (bf16[64,2048]{1,0:T(8,128)(2,1)S(1)}, bf16[64,2048]{1,0:T(8,128)(2,1)S(1)}, u32[]{:S(2)}, u32[]{:S(2)}) collective-permute-start(bf16[64,2048]{1,0:T(8,128)(2,1)S(1)} %fusion.4), channel_id=1, source_target_pairs={{0,6},{1,7},{2,4},{3,5},{4,2},{5,3},{6,0},{7,1},{8,14},{9,15},{10,... | collective-permute-start | bytes 786440 | tf_op jit(solution)/shard_map/ppermute | solution.py:224
  69.0 7.6 %collective-permute-done.9 = bf16[2,64,2048]{2,1,0:T(8,128)(2,1)S(1)} collective-permute-done((bf16[2,64,2048]{2,1,0:T(8,128)(2,1)}, bf16[2,64,2048]{2,1,0:T(8,128)(2,1)S(1)}, u32[]{:S(2)}, u32[]{:S(2)}) %collective-permute-start.9) | collective-permute-done | bytes 524320 | tf_op jit(solution)/shard_map/ppermute | solution.py:221
  76.6 1.1 %fusion.3 = bf16[64,2048]{1,0:T(8,128)(2,1)S(1)} fusion(bf16[2,64,2048]{2,1,0:T(8,128)(2,1)S(1)} %collective-permute-done.9, bf16[2,64,2048]{2,1,0:T(8,128)(2,1)} %get-tuple-element.24), kind=kLoop, calls=%fused_computation.10 | loop fusion | flops 524288 | bytes 786432 | tf_op jit(solution)/shard_map/convert_element_type | solution.py:223
  77.7 0.3 collective-permute-start.10
  77.9 0.7 collective-permute-done.7
  78.7 0.1 fusion.2
  78.7 2.5 %collective-permute-start.8 = (bf16[64,2048]{1,0:T(8,128)(2,1)S(1)}, bf16[64,2048]{1,0:T(8,128)(2,1)S(1)}, u32[]{:S(2)}, u32[]{:S(2)}) collective-permute-start(bf16[64,2048]{1,0:T(8,128)(2,1)S(1)} %fusion.2), channel_id=1, source_target_pairs={{0,6},{1,7},{2,4},{3,5},{4,2},{5,3},{6,0},{7,1},{8,14},{9,15},{10,... | collective-permute-start | bytes 786440 | tf_op jit(solution)/shard_map/ppermute | solution.py:224
  81.3 3.0 %collective-permute-done.15 = bf16[64,2048]{1,0:T(8,128)(2,1)S(1)} collective-permute-done((bf16[64,2048]{1,0:T(8,128)(2,1)S(1)}, bf16[64,2048]{1,0:T(8,128)(2,1)S(1)}, u32[]{:S(2)}, u32[]{:S(2)}) %collective-permute-start.15) | collective-permute-done | bytes 262176 | tf_op jit(solution)/shard_map/ppermute | solution.py:225
  84.3 0.1 add_convert_fusion.4
  84.4 0.1 add_convert_fusion.5
  84.5 3.0 %collective-permute-start.16 = (bf16[32,4096]{1,0:T(8,128)(2,1)S(1)}, bf16[32,4096]{1,0:T(8,128)(2,1)S(1)}, u32[]{:S(2)}, u32[]{:S(2)}) collective-permute-start(bf16[32,4096]{1,0:T(8,128)(2,1)S(1)} %pad_maximum_fusion.3), channel_id=1, source_target_pairs={{0,1},{1,0},{2,3},{3,2},{4,5},{5,4},{6,7},{7,6},{8,9},{9,8},{10,11... | collective-permute-start | bytes 786440 | tf_op jit(solution)/shard_map/ppermute | solution.py:234
  87.5 1.3 %collective-permute-done.10 = bf16[64,2048]{1,0:T(8,128)(2,1)S(1)} collective-permute-done((bf16[64,2048]{1,0:T(8,128)(2,1)S(1)}, bf16[64,2048]{1,0:T(8,128)(2,1)S(1)}, u32[]{:S(2)}, u32[]{:S(2)}) %collective-permute-start.10) | collective-permute-done | bytes 262176 | tf_op jit(solution)/shard_map/ppermute | solution.py:225
  88.8 0.1 add_convert_fusion.6
  89.0 0.1 add_convert_fusion.7
  89.1 3.0 %collective-permute-start.11 = (bf16[32,4096]{1,0:T(8,128)(2,1)S(1)}, bf16[32,4096]{1,0:T(8,128)(2,1)S(1)}, u32[]{:S(2)}, u32[]{:S(2)}) collective-permute-start(bf16[32,4096]{1,0:T(8,128)(2,1)S(1)} %pad_maximum_fusion.2), channel_id=1, source_target_pairs={{0,1},{1,0},{2,3},{3,2},{4,5},{5,4},{6,7},{7,6},{8,9},{9,8},{10,11... | collective-permute-start | bytes 786440 | tf_op jit(solution)/shard_map/ppermute | solution.py:234
  92.1 0.8 collective-permute-done.16
  92.9 0.1 fusion.1
  93.0 5.6 %collective-permute-done.11 = bf16[32,4096]{1,0:T(8,128)(2,1)S(1)} collective-permute-done((bf16[32,4096]{1,0:T(8,128)(2,1)S(1)}, bf16[32,4096]{1,0:T(8,128)(2,1)S(1)}, u32[]{:S(2)}, u32[]{:S(2)}) %collective-permute-start.11) | collective-permute-done | bytes 262176 | tf_op jit(solution)/shard_map/ppermute | solution.py:234
  98.6 0.1 fusion
  98.6 0.8 pad_maximum_fusion
  (29 shorter events, 0.1 us)
Async XLA Ops:
  1.0 27.3 %copy-start.4 = (bf16[2,512,128]{2,1,0:T(8,128)(2,1)}, bf16[2,512,128]{2,1,0:T(8,128)(2,1)S(1)}, u32[]{:S(2)}) copy-start(bf16[2,512,128]{2,1,0:T(8,128)(2,1)S(1)} %pad_maximum_fusion.1.own) | copy-start | bytes 786436
  1.0 9.1 %collective-permute-start.1 = (bf16[2,512,128]{2,1,0:T(8,128)(2,1)S(1)}, bf16[2,512,128]{2,1,0:T(8,128)(2,1)S(1)}, u32[]{:S(2)}, u32[]{:S(2)}) collective-permute-start(bf16[2,512,128]{2,1,0:T(8,128)(2,1)S(1)} %pad_maximum_fusion.1.own), channel_id=1, source_target_pairs={{0,32},{8,40},{16,48},{24,56},{32,64},{40,72},{48,80},{56,88},{64,... | collective-permute-start | bytes 786440 | tf_op jit(solution)/shard_map/ppermute | solution.py:159
  10.1 22.3 %copy-start.5 = (bf16[2,512,128]{2,1,0:T(8,128)(2,1)}, bf16[2,512,128]{2,1,0:T(8,128)(2,1)S(1)}, u32[]{:S(2)}) copy-start(bf16[2,512,128]{2,1,0:T(8,128)(2,1)S(1)} %collective-permute-done.1.near) | copy-start | bytes 786436
  11.2 9.2 %collective-permute-start.3 = (bf16[2,512,128]{2,1,0:T(8,128)(2,1)S(1)}, bf16[2,512,128]{2,1,0:T(8,128)(2,1)S(1)}, u32[]{:S(2)}, u32[]{:S(2)}) collective-permute-start(bf16[2,512,128]{2,1,0:T(8,128)(2,1)S(1)} %broadcast_select_fusion), channel_id=1, source_target_pairs={{0,16},{8,24},{16,32},{24,40},{32,48},{40,56},{48,64},{56,72},{64,... | collective-permute-start | bytes 786440 | tf_op jit(solution)/shard_map/ppermute | solution.py:161
  14.4 13.4 %collective-permute-start.5 = (bf16[2,512,128]{2,1,0:T(8,128)(2,1)S(1)}, bf16[2,512,128]{2,1,0:T(8,128)(2,1)S(1)}, u32[]{:S(2)}, u32[]{:S(2)}) collective-permute-start(bf16[2,512,128]{2,1,0:T(8,128)(2,1)S(1)} %collective-permute-done.1.near), channel_id=1, source_target_pairs={{0,16},{8,24},{16,0},{24,8},{32,48},{40,56},{48,32},{56,40},{64,80... | collective-permute-start | bytes 786440 | tf_op jit(solution)/shard_map/ppermute | solution.py:177
  15.1 17.3 %collective-permute-start = (bf16[2,512,128]{2,1,0:T(8,128)(2,1)S(1)}, bf16[2,512,128]{2,1,0:T(8,128)(2,1)S(1)}, u32[]{:S(2)}, u32[]{:S(2)}) collective-permute-start(bf16[2,512,128]{2,1,0:T(8,128)(2,1)S(1)} %pad_maximum_fusion.1.own), channel_id=1, source_target_pairs={{0,8},{8,0},{16,24},{24,16},{32,40},{40,32},{48,56},{56,48},{64,72... | collective-permute-start | bytes 786440 | tf_op jit(solution)/shard_map/ppermute | solution.py:162
  17.2 15.2 %collective-permute-start.2 = (bf16[2,512,128]{2,1,0:T(8,128)(2,1)S(1)}, bf16[2,512,128]{2,1,0:T(8,128)(2,1)S(1)}, u32[]{:S(2)}, u32[]{:S(2)}) collective-permute-start(bf16[2,512,128]{2,1,0:T(8,128)(2,1)S(1)} %collective-permute-done.1.near), channel_id=1, source_target_pairs={{0,8},{8,0},{16,24},{24,16},{32,40},{40,32},{48,56},{56,48},{64,72... | collective-permute-start | bytes 786440 | tf_op jit(solution)/shard_map/ppermute | solution.py:179
  20.4 21.7 %copy-start = (bf16[2,512,128]{2,1,0:T(8,128)(2,1)}, bf16[2,512,128]{2,1,0:T(8,128)(2,1)S(1)}, u32[]{:S(2)}) copy-start(bf16[2,512,128]{2,1,0:T(8,128)(2,1)S(1)} %collective-permute-done.3.refs_0_) | copy-start | bytes 786436
  20.4 21.7 %collective-permute-start.4 = (bf16[2,512,128]{2,1,0:T(8,128)(2,1)S(1)}, bf16[2,512,128]{2,1,0:T(8,128)(2,1)S(1)}, u32[]{:S(2)}, u32[]{:S(2)}) collective-permute-start(bf16[2,512,128]{2,1,0:T(8,128)(2,1)S(1)} %collective-permute-done.3.refs_0_), channel_id=1, source_target_pairs={{0,8},{8,0},{16,24},{24,16},{32,40},{40,32},{48,56},{56,48},{64,72... | collective-permute-start | bytes 786440 | tf_op jit(solution)/shard_map/ppermute | solution.py:178
  27.8 14.2 %copy-start.1 = (bf16[2,512,128]{2,1,0:T(8,128)(2,1)}, bf16[2,512,128]{2,1,0:T(8,128)(2,1)S(1)}, u32[]{:S(2)}) copy-start(bf16[2,512,128]{2,1,0:T(8,128)(2,1)S(1)} %collective-permute-done.5.refs_2_) | copy-start | bytes 786436
  27.8 14.2 %collective-permute-start.6 = (bf16[2,512,128]{2,1,0:T(8,128)(2,1)S(1)}, bf16[2,512,128]{2,1,0:T(8,128)(2,1)S(1)}, u32[]{:S(2)}, u32[]{:S(2)}) collective-permute-start(bf16[2,512,128]{2,1,0:T(8,128)(2,1)S(1)} %collective-permute-done.5.refs_2_), channel_id=1, source_target_pairs={{0,8},{8,0},{16,24},{24,16},{32,40},{40,32},{48,56},{56,48},{64,72... | collective-permute-start | bytes 786440 | tf_op jit(solution)/shard_map/ppermute | solution.py:180
  32.4 0.7 copy-start.10
  32.4 0.8 copy-start.11
  42.1 0.7 copy-start.2
  42.1 0.8 copy-start.3
  50.7 14.6 %collective-permute-start.14 = (bf16[2,64,2048]{2,1,0:T(8,128)(2,1)}, bf16[2,64,2048]{2,1,0:T(8,128)(2,1)S(1)}, u32[]{:S(2)}, u32[]{:S(2)}) collective-permute-start(bf16[2,64,2048]{2,1,0:T(8,128)(2,1)} %get-tuple-element.27), channel_id=1, source_target_pairs={{0,6},{1,7},{2,4},{3,5},{4,2},{5,3},{6,0},{7,1},{8,14},{9,15},{10,... | collective-permute-start | bytes 1572872 | tf_op jit(solution)/shard_map/ppermute | solution.py:221
  53.3 14.2 %collective-permute-start.12 = (bf16[2,64,2048]{2,1,0:T(8,128)(2,1)}, bf16[2,64,2048]{2,1,0:T(8,128)(2,1)S(1)}, u32[]{:S(2)}, u32[]{:S(2)}) collective-permute-start(bf16[2,64,2048]{2,1,0:T(8,128)(2,1)} %get-tuple-element.25), channel_id=1, source_target_pairs={{0,2},{1,3},{2,0},{3,1},{4,6},{5,7},{6,4},{7,5},{8,10},{9,11},{10,... | collective-permute-start | bytes 1572872 | tf_op jit(solution)/shard_map/ppermute | solution.py:220
  53.3 12.1 %copy-start.7 = (bf16[2,64,2048]{2,1,0:T(8,128)(2,1)S(1)}, bf16[2,64,2048]{2,1,0:T(8,128)(2,1)}, u32[]{:S(2)}) copy-start(bf16[2,64,2048]{2,1,0:T(8,128)(2,1)} %get-tuple-element.28) | copy-start | bytes 1572868
  53.3 14.1 %copy-start.6 = (bf16[2,64,2048]{2,1,0:T(8,128)(2,1)S(1)}, bf16[2,64,2048]{2,1,0:T(8,128)(2,1)}, u32[]{:S(2)}) copy-start(bf16[2,64,2048]{2,1,0:T(8,128)(2,1)} %get-tuple-element.26) | copy-start | bytes 1572868
  61.1 17.6 %copy-start.8 = (bf16[2,64,2048]{2,1,0:T(8,128)(2,1)S(1)}, bf16[2,64,2048]{2,1,0:T(8,128)(2,1)}, u32[]{:S(2)}) copy-start(bf16[2,64,2048]{2,1,0:T(8,128)(2,1)} %get-tuple-element.22) | copy-start | bytes 1572868
  61.1 15.5 %collective-permute-start.9 = (bf16[2,64,2048]{2,1,0:T(8,128)(2,1)}, bf16[2,64,2048]{2,1,0:T(8,128)(2,1)S(1)}, u32[]{:S(2)}, u32[]{:S(2)}) collective-permute-start(bf16[2,64,2048]{2,1,0:T(8,128)(2,1)} %get-tuple-element.23), channel_id=1, source_target_pairs={{0,6},{1,7},{2,4},{3,5},{4,2},{5,3},{6,0},{7,1},{8,14},{9,15},{10,... | collective-permute-start | bytes 1572872 | tf_op jit(solution)/shard_map/ppermute | solution.py:221
  61.9 16.7 %collective-permute-start.7 = (bf16[2,64,2048]{2,1,0:T(8,128)(2,1)}, bf16[2,64,2048]{2,1,0:T(8,128)(2,1)S(1)}, u32[]{:S(2)}, u32[]{:S(2)}) collective-permute-start(bf16[2,64,2048]{2,1,0:T(8,128)(2,1)} %get-tuple-element.21), channel_id=1, source_target_pairs={{0,2},{1,3},{2,0},{3,1},{4,6},{5,7},{6,4},{7,5},{8,10},{9,11},{10,... | collective-permute-start | bytes 1572872 | tf_op jit(solution)/shard_map/ppermute | solution.py:220
  65.4 18.9 %collective-permute-start.15 = (bf16[64,2048]{1,0:T(8,128)(2,1)S(1)}, bf16[64,2048]{1,0:T(8,128)(2,1)S(1)}, u32[]{:S(2)}, u32[]{:S(2)}) collective-permute-start(bf16[64,2048]{1,0:T(8,128)(2,1)S(1)} %fusion.5), channel_id=1, source_target_pairs={{0,2},{1,3},{2,0},{3,1},{4,6},{5,7},{6,4},{7,5},{8,10},{9,11},{10,... | collective-permute-start | bytes 786440 | tf_op jit(solution)/shard_map/ppermute | solution.py:225
  67.5 16.9 %collective-permute-start.13 = (bf16[64,2048]{1,0:T(8,128)(2,1)S(1)}, bf16[64,2048]{1,0:T(8,128)(2,1)S(1)}, u32[]{:S(2)}, u32[]{:S(2)}) collective-permute-start(bf16[64,2048]{1,0:T(8,128)(2,1)S(1)} %fusion.4), channel_id=1, source_target_pairs={{0,6},{1,7},{2,4},{3,5},{4,2},{5,3},{6,0},{7,1},{8,14},{9,15},{10,... | collective-permute-start | bytes 786440 | tf_op jit(solution)/shard_map/ppermute | solution.py:224
  76.6 12.3 %copy-start.9 = (bf16[2,64,2048]{2,1,0:T(8,128)(2,1)S(1)}, bf16[2,64,2048]{2,1,0:T(8,128)(2,1)}, u32[]{:S(2)}) copy-start(bf16[2,64,2048]{2,1,0:T(8,128)(2,1)} %get-tuple-element.24) | copy-start | bytes 1572868
  77.7 11.2 %collective-permute-start.10 = (bf16[64,2048]{1,0:T(8,128)(2,1)S(1)}, bf16[64,2048]{1,0:T(8,128)(2,1)S(1)}, u32[]{:S(2)}, u32[]{:S(2)}) collective-permute-start(bf16[64,2048]{1,0:T(8,128)(2,1)S(1)} %fusion.3), channel_id=1, source_target_pairs={{0,2},{1,3},{2,0},{3,1},{4,6},{5,7},{6,4},{7,5},{8,10},{9,11},{10,... | collective-permute-start | bytes 786440 | tf_op jit(solution)/shard_map/ppermute | solution.py:225
  78.7 10.2 %collective-permute-start.8 = (bf16[64,2048]{1,0:T(8,128)(2,1)S(1)}, bf16[64,2048]{1,0:T(8,128)(2,1)S(1)}, u32[]{:S(2)}, u32[]{:S(2)}) collective-permute-start(bf16[64,2048]{1,0:T(8,128)(2,1)S(1)} %fusion.2), channel_id=1, source_target_pairs={{0,6},{1,7},{2,4},{3,5},{4,2},{5,3},{6,0},{7,1},{8,14},{9,15},{10,... | collective-permute-start | bytes 786440 | tf_op jit(solution)/shard_map/ppermute | solution.py:224
  84.5 8.3 %collective-permute-start.16 = (bf16[32,4096]{1,0:T(8,128)(2,1)S(1)}, bf16[32,4096]{1,0:T(8,128)(2,1)S(1)}, u32[]{:S(2)}, u32[]{:S(2)}) collective-permute-start(bf16[32,4096]{1,0:T(8,128)(2,1)S(1)} %pad_maximum_fusion.3), channel_id=1, source_target_pairs={{0,1},{1,0},{2,3},{3,2},{4,5},{5,4},{6,7},{7,6},{8,9},{9,8},{10,11... | collective-permute-start | bytes 786440 | tf_op jit(solution)/shard_map/ppermute | solution.py:234
  89.1 9.5 %collective-permute-start.11 = (bf16[32,4096]{1,0:T(8,128)(2,1)S(1)}, bf16[32,4096]{1,0:T(8,128)(2,1)S(1)}, u32[]{:S(2)}, u32[]{:S(2)}) collective-permute-start(bf16[32,4096]{1,0:T(8,128)(2,1)S(1)} %pad_maximum_fusion.2), channel_id=1, source_target_pairs={{0,1},{1,0},{2,3},{3,2},{4,5},{5,4},{6,7},{7,6},{8,9},{9,8},{10,11... | collective-permute-start | bytes 786440 | tf_op jit(solution)/shard_map/ppermute | solution.py:234

commit v9 on v7

--- a/solution.py
+++ b/solution.py
@@ -131,13 +131,14 @@
 
 def on_device(queries, keys, values, doc_start, out_weight):
     rows = queries.shape[0]
+    ctx = lax.axis_index("ctx")
     n_ctx = lax.axis_size("ctx")
     swap = [(c, c ^ 1) for c in range(n_ctx)]
     own = jnp.stack([keys, values])
 
     near = lax.ppermute(own, "ctx", [(c, c + 4) for c in range(n_ctx - 4)])
-    jump = [(c, c + (6 if c // 2 % 2 else 2)) for c in range(n_ctx)]
-    far = lax.ppermute(own, "ctx", [(c, t) for c, t in jump if t < n_ctx])
+    passed = jnp.where(ctx // 2 % 2 == 1, near, own)
+    far = lax.ppermute(passed, "ctx", [(c, c + 2) for c in range(n_ctx - 2)])
     partner = lax.ppermute(own, "ctx", swap)
 
     state = (

time: 92.4 us -> 96.5 us (1.044)
  waiting for transfers between devices: 27.6 us -> 38.3 us
  starting transfers between devices: 33 us -> 25.2 us
  other arithmetic: 4.56 us -> 5.66 us
    ppermute x1, starting transfers between devices: 8.56 us -> 2.09 us  [on_device(): partner = lax.ppermute(own, 'ctx', swap)]
    ppermute x1, waiting for transfers between devices: 0.01 us -> 4.94 us  [on_device(): cross = lax.ppermute(near, 'ctx', [(c, c ^ 2) for c in range(n_ctx)])]
    ppermute x1, starting transfers between devices: 3.83 us -> 0.49 us  [on_device(): cross_o = lax.ppermute(cross, 'ctx', swap)]
    ppermute x1, waiting for transfers between devices: 3.22 us -> 6.4 us  [on_device(): near = lax.ppermute(own, 'ctx', [(c, c + 4) for c in range(n_ctx - 4)])]
    ppermute x1, waiting for transfers between devices: 0.01 us -> 3.15 us  [on_device(): far = lax.ppermute(passed, 'ctx', [(c, c + 2) for c in range(n_ctx - 2)])]
    ppermute x1, starting transfers between devices: 0.51 us -> 2.53 us  [on_device(): far_o = lax.ppermute(far, 'ctx', swap)]
    select_n x0 -> x1, other arithmetic: none -> 1.1 us  [on_device(): passed = jnp.where(ctx // 2 % 2 == 1, near, own)]
  transfers between devices with their start and end apart: 17 -> 17, of which waited for: 6 -> 8; matrix products, arithmetic and copies ran while one was open for 3% -> 3% of each run, Pallas kernels for 17% -> 16%
where the time goes in v9:
time: 96.5 us; the launch traced here: 96.2 us
  waiting for transfers between devices  38.3 us (40%)
  starting transfers between devices  25.2 us (26%)
  Pallas kernels  25.1 us (26%)
  other arithmetic  5.66 us (6%)
  local copies, waits for them, and re-layouts  1.59 us (2%)
    pallas_call x2, Pallas kernels, chunk(): pl.pallas_call(rest_kernel, grid=(1,), out_shape=[quad] * 4, in_specs=[SM...  18.8 us
    ppermute x2, waiting for transfers between devices, chunk(): p_got = lax.ppermute(p_send, 'head', to_near)  10.5 us
    ppermute x2, waiting for transfers between devices, chunk(): got = lax.ppermute(total(1 - part).astype(BF16), 'head', to_part)  7.34 us
    ppermute x1, waiting for transfers between devices, on_device(): near = lax.ppermute(own, 'ctx', [(c, c + 4) for c in range(n_ctx - 4)])  6.4 us
    pallas_call x1, Pallas kernels, on_device(): pl.pallas_call(own_kernel, out_shape=state, in_specs=[VMEM] * 4, out_spec...  6.32 us
    ppermute x2, waiting for transfers between devices, chunk(): p_last = lax.ppermute(p_next, 'head', to_far)  5.94 us
    ppermute x2, starting transfers between devices, chunk(): got = lax.ppermute(total(1 - part).astype(BF16), 'head', to_part)  5.84 us
    ppermute x1, waiting for transfers between devices, on_device(): cross = lax.ppermute(near, 'ctx', [(c, c ^ 2) for c in range(n_ctx)])  4.94 us
  transfers between devices with their start and end apart: 17, of which 8 were waited for; matrix products, arithmetic and copies ran while one was open for 3% of the time, Pallas kernels for 16%

profile of v9, /device:TPU:193, one launch (start us, length us, event | category | flops | bytes accessed | tf_op | source)
XLA Modules:
  0.0 96.2 jit_solution(10475181770991656121)
XLA Ops:
  0.0 1.0 %pad_maximum_fusion.1.own = bf16[2,512,128]{2,1,0:T(8,128)(2,1)S(1)} fusion(bf16[1,512,128]{2,1,0:T(8,128)(2,1)} %bitcast.36, bf16[1,512,128]{2,1,0:T(8,128)(2,1)} %bitcast.38), kind=kLoop, calls=%fused_computation.13 | loop fusion | flops 131072 | bytes 524288 | tf_op jit(solution)/shard_map/stack | solution.py:137
  1.0 0.0 copy-start.6
  1.0 2.6 %collective-permute-start.1 = (bf16[2,512,128]{2,1,0:T(8,128)(2,1)S(1)}, bf16[2,512,128]{2,1,0:T(8,128)(2,1)S(1)}, u32[]{:S(2)}, u32[]{:S(2)}) collective-permute-start(bf16[2,512,128]{2,1,0:T(8,128)(2,1)S(1)} %pad_maximum_fusion.1.own), channel_id=1, source_target_pairs={{0,32},{8,40},{16,48},{24,56},{32,64},{40,72},{48,80},{56,88},{64,... | collective-permute-start | bytes 786440 | tf_op jit(solution)/shard_map/ppermute | solution.py:139
  3.7 6.4 %collective-permute-done.1.refs_2_ = bf16[2,512,128]{2,1,0:T(8,128)(2,1)S(1)} collective-permute-done((bf16[2,512,128]{2,1,0:T(8,128)(2,1)S(1)}, bf16[2,512,128]{2,1,0:T(8,128)(2,1)S(1)}, u32[]{:S(2)}, u32[]{:S(2)}) %collective-permute-start.1) | collective-permute-done | bytes 262176 | tf_op jit(solution)/shard_map/ppermute | solution.py:139
  10.1 1.1 %broadcast_select_fusion = bf16[2,512,128]{2,1,0:T(8,128)(2,1)S(1)} fusion(bf16[2,512,128]{2,1,0:T(8,128)(2,1)S(1)} %collective-permute-done.1.refs_2_, pred[]{:T(512)S(6)} %eq.6, bf16[1,512,128]{2,1,0:T(8,128)(2,1)} %bitcast.37, bf16[1,512,128]{2,1,0:T(8,128)(2,1)} %bitcast.39), kind=kLoop, calls=%fused_computation.24 | loop fusion | flops 262144 | bytes 786433 | tf_op jit(solution)/shard_map/jit(_where)/select_n | solution.py:140
  11.2 3.2 %collective-permute-start.2 = (bf16[2,512,128]{2,1,0:T(8,128)(2,1)S(1)}, bf16[2,512,128]{2,1,0:T(8,128)(2,1)S(1)}, u32[]{:S(2)}, u32[]{:S(2)}) collective-permute-start(bf16[2,512,128]{2,1,0:T(8,128)(2,1)S(1)} %broadcast_select_fusion), channel_id=1, source_target_pairs={{0,16},{8,24},{16,32},{24,40},{32,48},{40,56},{48,64},{56,72},{64,... | collective-permute-start | bytes 786440 | tf_op jit(solution)/shard_map/ppermute | solution.py:141
  14.4 0.7 collective-permute-start.5
  15.1 2.1 %collective-permute-start = (bf16[2,512,128]{2,1,0:T(8,128)(2,1)S(1)}, bf16[2,512,128]{2,1,0:T(8,128)(2,1)S(1)}, u32[]{:S(2)}, u32[]{:S(2)}) collective-permute-start(bf16[2,512,128]{2,1,0:T(8,128)(2,1)S(1)} %pad_maximum_fusion.1.own), channel_id=1, source_target_pairs={{0,8},{8,0},{16,24},{24,16},{32,40},{40,32},{48,56},{56,48},{64,72... | collective-permute-start | bytes 786440 | tf_op jit(solution)/shard_map/ppermute | solution.py:142
  17.2 0.0 collective-permute-start.4
  17.2 3.2 %collective-permute-done.2.refs_0_ = bf16[2,512,128]{2,1,0:T(8,128)(2,1)S(1)} collective-permute-done((bf16[2,512,128]{2,1,0:T(8,128)(2,1)S(1)}, bf16[2,512,128]{2,1,0:T(8,128)(2,1)S(1)}, u32[]{:S(2)}, u32[]{:S(2)}) %collective-permute-start.2) | collective-permute-done | bytes 262176 | tf_op jit(solution)/shard_map/ppermute | solution.py:141
  20.4 2.5 %collective-permute-start.3 = (bf16[2,512,128]{2,1,0:T(8,128)(2,1)S(1)}, bf16[2,512,128]{2,1,0:T(8,128)(2,1)S(1)}, u32[]{:S(2)}, u32[]{:S(2)}) collective-permute-start(bf16[2,512,128]{2,1,0:T(8,128)(2,1)S(1)} %collective-permute-done.2.refs_0_), channel_id=1, source_target_pairs={{0,8},{8,0},{16,24},{24,16},{32,40},{40,32},{48,56},{56,48},{64,72... | collective-permute-start | bytes 786440 | tf_op jit(solution)/shard_map/ppermute | solution.py:157
  22.9 4.9 %collective-permute-done.5.refs_4_ = bf16[2,512,128]{2,1,0:T(8,128)(2,1)S(1)} collective-permute-done((bf16[2,512,128]{2,1,0:T(8,128)(2,1)S(1)}, bf16[2,512,128]{2,1,0:T(8,128)(2,1)S(1)}, u32[]{:S(2)}, u32[]{:S(2)}) %collective-permute-start.5) | collective-permute-done | bytes 262176 | tf_op jit(solution)/shard_map/ppermute | solution.py:156
  27.8 0.5 collective-permute-start.6
  28.3 0.7 copy-done.11
  29.0 6.3 %shard_map.55 = (f32[4,512,128]{2,1,0:T(8,128)}, f32[4,512,256]{2,1,0:T(8,128)}) custom-call(bf16[512,512]{1,0:T(8,128)(2,1)} %q_ref.1, s32[4,128]{1,0:T(4,128)} %bitcast.40, bf16[2,512,128]{2,1,0:T(8,128)(2,1)} %copy-done.6, bf16[2,512,128]{2,1,0:T(8,128)(2,1)} %copy-done.11), custom_call_target="tpu_custom_call" | custom-call | tf_op jit(solution)/shard_map/pallas_call | solution.py:148
  35.4 0.0 collective-permute-done.4.refs_3_
  35.4 0.0 collective-permute-done.3.refs_1_
  35.4 0.7 copy-done.3
  36.1 0.1 copy-done.4
  36.2 0.1 copy-done.5
  36.3 9.5 %shard_map.56 = (bf16[2,64,2048]{2,1,0:T(8,128)(2,1)}, bf16[2,64,2048]{2,1,0:T(8,128)(2,1)}, bf16[2,64,2048]{2,1,0:T(8,128)(2,1)}, bf16[2,64,2048]{2,1,0:T(8,128)(2,1)}) custom-call(s32[512]{0:T(512)} %doc.3, bf16[8,2,32,512]{3,2,1,0:T(8,128)(2,1)} %bitcast.24, f32[4,8,2,32,128]{4,3,2,1,0:T(8,128)} %bitcast.26, f32[4,8,2,32,256]{4,3,2,1,0:T(8,128)} %bitcast.22, ...), custom_call_target="tpu_custom_call" | custom-call | tf_op jit(solution)/shard_map/pallas_call | solution.py:176
  45.8 1.3 %collective-permute-start.7 = (bf16[2,64,2048]{2,1,0:T(8,128)(2,1)}, bf16[2,64,2048]{2,1,0:T(8,128)(2,1)S(1)}, u32[]{:S(2)}, u32[]{:S(2)}) collective-permute-start(bf16[2,64,2048]{2,1,0:T(8,128)(2,1)} %get-tuple-element.17), channel_id=1, source_target_pairs={{0,2},{1,3},{2,0},{3,1},{4,6},{5,7},{6,4},{7,5},{8,10},{9,11},{10,... | collective-permute-start | bytes 1572872 | tf_op jit(solution)/shard_map/ppermute | solution.py:192
  47.1 1.8 %collective-permute-start.9 = (bf16[2,64,2048]{2,1,0:T(8,128)(2,1)}, bf16[2,64,2048]{2,1,0:T(8,128)(2,1)S(1)}, u32[]{:S(2)}, u32[]{:S(2)}) collective-permute-start(bf16[2,64,2048]{2,1,0:T(8,128)(2,1)} %get-tuple-element.19), channel_id=1, source_target_pairs={{0,6},{1,7},{2,4},{3,5},{4,2},{5,3},{6,0},{7,1},{8,14},{9,15},{10,... | collective-permute-start | bytes 1572872 | tf_op jit(solution)/shard_map/ppermute | solution.py:193
  48.9 9.3 %shard_map.57 = (bf16[2,64,2048]{2,1,0:T(8,128)(2,1)}, bf16[2,64,2048]{2,1,0:T(8,128)(2,1)}, bf16[2,64,2048]{2,1,0:T(8,128)(2,1)}, bf16[2,64,2048]{2,1,0:T(8,128)(2,1)}) custom-call(s32[512]{0:T(512)} %doc.3, bf16[8,2,32,512]{3,2,1,0:T(8,128)(2,1)} %bitcast.25, f32[4,8,2,32,128]{4,3,2,1,0:T(8,128)} %bitcast.27, f32[4,8,2,32,256]{4,3,2,1,0:T(8,128)} %bitcast.23, ...), custom_call_target="tpu_custom_call" | custom-call | tf_op jit(solution)/shard_map/pallas_call | solution.py:176
  58.2 0.4 collective-permute-start.12
  58.7 0.6 collective-permute-start.14
  59.3 0.1 fusion.2
  59.4 2.1 %collective-permute-start.8 = (bf16[64,2048]{1,0:T(8,128)(2,1)S(1)}, bf16[64,2048]{1,0:T(8,128)(2,1)S(1)}, u32[]{:S(2)}, u32[]{:S(2)}) collective-permute-start(bf16[64,2048]{1,0:T(8,128)(2,1)S(1)} %fusion.2), channel_id=1, source_target_pairs={{0,6},{1,7},{2,4},{3,5},{4,2},{5,3},{6,0},{7,1},{8,14},{9,15},{10,... | collective-permute-start | bytes 786440 | tf_op jit(solution)/shard_map/ppermute | solution.py:196
  61.5 0.1 fusion.3
  61.6 0.4 collective-permute-start.10
  62.0 10.5 %collective-permute-done.12 = bf16[2,64,2048]{2,1,0:T(8,128)(2,1)S(1)} collective-permute-done((bf16[2,64,2048]{2,1,0:T(8,128)(2,1)}, bf16[2,64,2048]{2,1,0:T(8,128)(2,1)S(1)}, u32[]{:S(2)}, u32[]{:S(2)}) %collective-permute-start.12) | collective-permute-done | bytes 524320 | tf_op jit(solution)/shard_map/ppermute | solution.py:192
  72.5 1.0 %fusion.4 = bf16[64,2048]{1,0:T(8,128)(2,1)S(1)} fusion(bf16[2,64,2048]{2,1,0:T(8,128)(2,1)S(1)} %collective-permute-done.12, bf16[2,64,2048]{2,1,0:T(8,128)(2,1)} %get-tuple-element.22), kind=kLoop, calls=%fused_computation.11 | loop fusion | flops 524288 | bytes 786432 | tf_op jit(solution)/shard_map/convert_element_type | solution.py:194
  73.5 0.9 collective-permute-start.13
  74.5 1.0 %fusion.5 = bf16[64,2048]{1,0:T(8,128)(2,1)S(1)} fusion(bf16[2,64,2048]{2,1,0:T(8,128)(2,1)S(1)} %collective-permute-done.14, bf16[2,64,2048]{2,1,0:T(8,128)(2,1)} %get-tuple-element.24), kind=kLoop, calls=%fused_computation.12 | loop fusion | flops 524288 | bytes 786432 | tf_op jit(solution)/shard_map/convert_element_type | solution.py:195
  75.5 0.1 collective-permute-start.15
  75.6 4.1 %collective-permute-done.8 = bf16[64,2048]{1,0:T(8,128)(2,1)S(1)} collective-permute-done((bf16[64,2048]{1,0:T(8,128)(2,1)S(1)}, bf16[64,2048]{1,0:T(8,128)(2,1)S(1)}, u32[]{:S(2)}, u32[]{:S(2)}) %collective-permute-start.8) | collective-permute-done | bytes 262176 | tf_op jit(solution)/shard_map/ppermute | solution.py:196
  79.6 0.1 add_convert_fusion.7
  79.7 0.1 add_convert_fusion.6
  79.9 3.0 %collective-permute-start.11 = (bf16[32,4096]{1,0:T(8,128)(2,1)S(1)}, bf16[32,4096]{1,0:T(8,128)(2,1)S(1)}, u32[]{:S(2)}, u32[]{:S(2)}) collective-permute-start(bf16[32,4096]{1,0:T(8,128)(2,1)S(1)} %pad_maximum_fusion.2), channel_id=1, source_target_pairs={{0,1},{1,0},{2,3},{3,2},{4,5},{5,4},{6,7},{7,6},{8,9},{9,8},{10,11... | collective-permute-start | bytes 786440 | tf_op jit(solution)/shard_map/ppermute | solution.py:206
  82.9 1.9 %collective-permute-done.13 = bf16[64,2048]{1,0:T(8,128)(2,1)S(1)} collective-permute-done((bf16[64,2048]{1,0:T(8,128)(2,1)S(1)}, bf16[64,2048]{1,0:T(8,128)(2,1)S(1)}, u32[]{:S(2)}, u32[]{:S(2)}) %collective-permute-start.13) | collective-permute-done | bytes 262176 | tf_op jit(solution)/shard_map/ppermute | solution.py:196
  84.8 0.1 add_convert_fusion.5
  84.9 0.1 add_convert_fusion.4
  85.0 2.8 %collective-permute-start.16 = (bf16[32,4096]{1,0:T(8,128)(2,1)S(1)}, bf16[32,4096]{1,0:T(8,128)(2,1)S(1)}, u32[]{:S(2)}, u32[]{:S(2)}) collective-permute-start(bf16[32,4096]{1,0:T(8,128)(2,1)S(1)} %pad_maximum_fusion.3), channel_id=1, source_target_pairs={{0,1},{1,0},{2,3},{3,2},{4,5},{5,4},{6,7},{7,6},{8,9},{9,8},{10,11... | collective-permute-start | bytes 786440 | tf_op jit(solution)/shard_map/ppermute | solution.py:206
  87.9 1.7 %collective-permute-done.11 = bf16[32,4096]{1,0:T(8,128)(2,1)S(1)} collective-permute-done((bf16[32,4096]{1,0:T(8,128)(2,1)S(1)}, bf16[32,4096]{1,0:T(8,128)(2,1)S(1)}, u32[]{:S(2)}, u32[]{:S(2)}) %collective-permute-start.11) | collective-permute-done | bytes 262176 | tf_op jit(solution)/shard_map/ppermute | solution.py:206
  89.5 0.1 fusion
  89.6 5.7 %collective-permute-done.16 = bf16[32,4096]{1,0:T(8,128)(2,1)S(1)} collective-permute-done((bf16[32,4096]{1,0:T(8,128)(2,1)S(1)}, bf16[32,4096]{1,0:T(8,128)(2,1)S(1)}, u32[]{:S(2)}, u32[]{:S(2)}) %collective-permute-start.16) | collective-permute-done | bytes 262176 | tf_op jit(solution)/shard_map/ppermute | solution.py:206
  95.3 0.1 fusion.1
  95.3 0.8 pad_maximum_fusion
  (28 shorter events, 0.1 us)
Async XLA Ops:
  1.0 27.3 %copy-start.6 = (bf16[2,512,128]{2,1,0:T(8,128)(2,1)}, bf16[2,512,128]{2,1,0:T(8,128)(2,1)S(1)}, u32[]{:S(2)}) copy-start(bf16[2,512,128]{2,1,0:T(8,128)(2,1)S(1)} %pad_maximum_fusion.1.own) | copy-start | bytes 786436
  1.0 9.1 %collective-permute-start.1 = (bf16[2,512,128]{2,1,0:T(8,128)(2,1)S(1)}, bf16[2,512,128]{2,1,0:T(8,128)(2,1)S(1)}, u32[]{:S(2)}, u32[]{:S(2)}) collective-permute-start(bf16[2,512,128]{2,1,0:T(8,128)(2,1)S(1)} %pad_maximum_fusion.1.own), channel_id=1, source_target_pairs={{0,32},{8,40},{16,48},{24,56},{32,64},{40,72},{48,80},{56,88},{64,... | collective-permute-start | bytes 786440 | tf_op jit(solution)/shard_map/ppermute | solution.py:139
  10.1 25.3 %copy-start = (bf16[2,512,128]{2,1,0:T(8,128)(2,1)}, bf16[2,512,128]{2,1,0:T(8,128)(2,1)S(1)}, u32[]{:S(2)}) copy-start(bf16[2,512,128]{2,1,0:T(8,128)(2,1)S(1)} %collective-permute-done.1.refs_2_) | copy-start | bytes 786436
  11.2 9.2 %collective-permute-start.2 = (bf16[2,512,128]{2,1,0:T(8,128)(2,1)S(1)}, bf16[2,512,128]{2,1,0:T(8,128)(2,1)S(1)}, u32[]{:S(2)}, u32[]{:S(2)}) collective-permute-start(bf16[2,512,128]{2,1,0:T(8,128)(2,1)S(1)} %broadcast_select_fusion), channel_id=1, source_target_pairs={{0,16},{8,24},{16,32},{24,40},{32,48},{40,56},{48,64},{56,72},{64,... | collective-permute-start | bytes 786440 | tf_op jit(solution)/shard_map/ppermute | solution.py:141
  14.4 13.4 %collective-permute-start.5 = (bf16[2,512,128]{2,1,0:T(8,128)(2,1)S(1)}, bf16[2,512,128]{2,1,0:T(8,128)(2,1)S(1)}, u32[]{:S(2)}, u32[]{:S(2)}) collective-permute-start(bf16[2,512,128]{2,1,0:T(8,128)(2,1)S(1)} %collective-permute-done.1.refs_2_), channel_id=1, source_target_pairs={{0,16},{8,24},{16,0},{24,8},{32,48},{40,56},{48,32},{56,40},{64,80... | collective-permute-start | bytes 786440 | tf_op jit(solution)/shard_map/ppermute | solution.py:156
  15.1 13.2 %collective-permute-start = (bf16[2,512,128]{2,1,0:T(8,128)(2,1)S(1)}, bf16[2,512,128]{2,1,0:T(8,128)(2,1)S(1)}, u32[]{:S(2)}, u32[]{:S(2)}) collective-permute-start(bf16[2,512,128]{2,1,0:T(8,128)(2,1)S(1)} %pad_maximum_fusion.1.own), channel_id=1, source_target_pairs={{0,8},{8,0},{16,24},{24,16},{32,40},{40,32},{48,56},{56,48},{64,72... | collective-permute-start | bytes 786440 | tf_op jit(solution)/shard_map/ppermute | solution.py:142
  17.2 18.1 %collective-permute-start.4 = (bf16[2,512,128]{2,1,0:T(8,128)(2,1)S(1)}, bf16[2,512,128]{2,1,0:T(8,128)(2,1)S(1)}, u32[]{:S(2)}, u32[]{:S(2)}) collective-permute-start(bf16[2,512,128]{2,1,0:T(8,128)(2,1)S(1)} %collective-permute-done.1.refs_2_), channel_id=1, source_target_pairs={{0,8},{8,0},{16,24},{24,16},{32,40},{40,32},{48,56},{56,48},{64,72... | collective-permute-start | bytes 786440 | tf_op jit(solution)/shard_map/ppermute | solution.py:158
  20.4 15.0 %copy-start.1 = (bf16[2,512,128]{2,1,0:T(8,128)(2,1)}, bf16[2,512,128]{2,1,0:T(8,128)(2,1)S(1)}, u32[]{:S(2)}) copy-start(bf16[2,512,128]{2,1,0:T(8,128)(2,1)S(1)} %collective-permute-done.2.refs_0_) | copy-start | bytes 786436
  20.4 15.0 %collective-permute-start.3 = (bf16[2,512,128]{2,1,0:T(8,128)(2,1)S(1)}, bf16[2,512,128]{2,1,0:T(8,128)(2,1)S(1)}, u32[]{:S(2)}, u32[]{:S(2)}) collective-permute-start(bf16[2,512,128]{2,1,0:T(8,128)(2,1)S(1)} %collective-permute-done.2.refs_0_), channel_id=1, source_target_pairs={{0,8},{8,0},{16,24},{24,16},{32,40},{40,32},{48,56},{56,48},{64,72... | collective-permute-start | bytes 786440 | tf_op jit(solution)/shard_map/ppermute | solution.py:157
  27.8 7.6 %copy-start.2 = (bf16[2,512,128]{2,1,0:T(8,128)(2,1)}, bf16[2,512,128]{2,1,0:T(8,128)(2,1)S(1)}, u32[]{:S(2)}) copy-start(bf16[2,512,128]{2,1,0:T(8,128)(2,1)S(1)} %collective-permute-done.5.refs_4_) | copy-start | bytes 786436
  27.8 7.5 %collective-permute-start.6 = (bf16[2,512,128]{2,1,0:T(8,128)(2,1)S(1)}, bf16[2,512,128]{2,1,0:T(8,128)(2,1)S(1)}, u32[]{:S(2)}, u32[]{:S(2)}) collective-permute-start(bf16[2,512,128]{2,1,0:T(8,128)(2,1)S(1)} %collective-permute-done.5.refs_4_), channel_id=1, source_target_pairs={{0,8},{8,0},{16,24},{24,16},{32,40},{40,32},{48,56},{56,48},{64,72... | collective-permute-start | bytes 786440 | tf_op jit(solution)/shard_map/ppermute | solution.py:159
  28.3 0.7 copy-start.11
  35.4 0.7 copy-start.3
  35.4 0.8 copy-start.4
  35.4 0.9 copy-start.5
  45.8 13.5 %collective-permute-start.7 = (bf16[2,64,2048]{2,1,0:T(8,128)(2,1)}, bf16[2,64,2048]{2,1,0:T(8,128)(2,1)S(1)}, u32[]{:S(2)}, u32[]{:S(2)}) collective-permute-start(bf16[2,64,2048]{2,1,0:T(8,128)(2,1)} %get-tuple-element.17), channel_id=1, source_target_pairs={{0,2},{1,3},{2,0},{3,1},{4,6},{5,7},{6,4},{7,5},{8,10},{9,11},{10,... | collective-permute-start | bytes 1572872 | tf_op jit(solution)/shard_map/ppermute | solution.py:192
  47.1 14.4 %collective-permute-start.9 = (bf16[2,64,2048]{2,1,0:T(8,128)(2,1)}, bf16[2,64,2048]{2,1,0:T(8,128)(2,1)S(1)}, u32[]{:S(2)}, u32[]{:S(2)}) collective-permute-start(bf16[2,64,2048]{2,1,0:T(8,128)(2,1)} %get-tuple-element.19), channel_id=1, source_target_pairs={{0,6},{1,7},{2,4},{3,5},{4,2},{5,3},{6,0},{7,1},{8,14},{9,15},{10,... | collective-permute-start | bytes 1572872 | tf_op jit(solution)/shard_map/ppermute | solution.py:193
  48.9 10.4 %copy-start.8 = (bf16[2,64,2048]{2,1,0:T(8,128)(2,1)S(1)}, bf16[2,64,2048]{2,1,0:T(8,128)(2,1)}, u32[]{:S(2)}) copy-start(bf16[2,64,2048]{2,1,0:T(8,128)(2,1)} %get-tuple-element.18) | copy-start | bytes 1572868
  48.9 12.6 %copy-start.7 = (bf16[2,64,2048]{2,1,0:T(8,128)(2,1)S(1)}, bf16[2,64,2048]{2,1,0:T(8,128)(2,1)}, u32[]{:S(2)}) copy-start(bf16[2,64,2048]{2,1,0:T(8,128)(2,1)} %get-tuple-element.20) | copy-start | bytes 1572868
  58.2 26.5 %copy-start.10 = (bf16[2,64,2048]{2,1,0:T(8,128)(2,1)S(1)}, bf16[2,64,2048]{2,1,0:T(8,128)(2,1)}, u32[]{:S(2)}) copy-start(bf16[2,64,2048]{2,1,0:T(8,128)(2,1)} %get-tuple-element.22) | copy-start | bytes 1572868
  58.2 26.6 %copy-start.9 = (bf16[2,64,2048]{2,1,0:T(8,128)(2,1)S(1)}, bf16[2,64,2048]{2,1,0:T(8,128)(2,1)}, u32[]{:S(2)}) copy-start(bf16[2,64,2048]{2,1,0:T(8,128)(2,1)} %get-tuple-element.24) | copy-start | bytes 1572868
  58.2 14.2 %collective-permute-start.12 = (bf16[2,64,2048]{2,1,0:T(8,128)(2,1)}, bf16[2,64,2048]{2,1,0:T(8,128)(2,1)S(1)}, u32[]{:S(2)}, u32[]{:S(2)}) collective-permute-start(bf16[2,64,2048]{2,1,0:T(8,128)(2,1)} %get-tuple-element.21), channel_id=1, source_target_pairs={{0,2},{1,3},{2,0},{3,1},{4,6},{5,7},{6,4},{7,5},{8,10},{9,11},{10,... | collective-permute-start | bytes 1572872 | tf_op jit(solution)/shard_map/ppermute | solution.py:192
  58.7 15.8 %collective-permute-start.14 = (bf16[2,64,2048]{2,1,0:T(8,128)(2,1)}, bf16[2,64,2048]{2,1,0:T(8,128)(2,1)S(1)}, u32[]{:S(2)}, u32[]{:S(2)}) collective-permute-start(bf16[2,64,2048]{2,1,0:T(8,128)(2,1)} %get-tuple-element.23), channel_id=1, source_target_pairs={{0,6},{1,7},{2,4},{3,5},{4,2},{5,3},{6,0},{7,1},{8,14},{9,15},{10,... | collective-permute-start | bytes 1572872 | tf_op jit(solution)/shard_map/ppermute | solution.py:193
  59.4 20.3 %collective-permute-start.8 = (bf16[64,2048]{1,0:T(8,128)(2,1)S(1)}, bf16[64,2048]{1,0:T(8,128)(2,1)S(1)}, u32[]{:S(2)}, u32[]{:S(2)}) collective-permute-start(bf16[64,2048]{1,0:T(8,128)(2,1)S(1)} %fusion.2), channel_id=1, source_target_pairs={{0,6},{1,7},{2,4},{3,5},{4,2},{5,3},{6,0},{7,1},{8,14},{9,15},{10,... | collective-permute-start | bytes 786440 | tf_op jit(solution)/shard_map/ppermute | solution.py:196
  61.6 18.2 %collective-permute-start.10 = (bf16[64,2048]{1,0:T(8,128)(2,1)S(1)}, bf16[64,2048]{1,0:T(8,128)(2,1)S(1)}, u32[]{:S(2)}, u32[]{:S(2)}) collective-permute-start(bf16[64,2048]{1,0:T(8,128)(2,1)S(1)} %fusion.3), channel_id=1, source_target_pairs={{0,2},{1,3},{2,0},{3,1},{4,6},{5,7},{6,4},{7,5},{8,10},{9,11},{10,... | collective-permute-start | bytes 786440 | tf_op jit(solution)/shard_map/ppermute | solution.py:197
  73.5 11.3 %collective-permute-start.13 = (bf16[64,2048]{1,0:T(8,128)(2,1)S(1)}, bf16[64,2048]{1,0:T(8,128)(2,1)S(1)}, u32[]{:S(2)}, u32[]{:S(2)}) collective-permute-start(bf16[64,2048]{1,0:T(8,128)(2,1)S(1)} %fusion.4), channel_id=1, source_target_pairs={{0,6},{1,7},{2,4},{3,5},{4,2},{5,3},{6,0},{7,1},{8,14},{9,15},{10,... | collective-permute-start | bytes 786440 | tf_op jit(solution)/shard_map/ppermute | solution.py:196
  75.5 9.4 %collective-permute-start.15 = (bf16[64,2048]{1,0:T(8,128)(2,1)S(1)}, bf16[64,2048]{1,0:T(8,128)(2,1)S(1)}, u32[]{:S(2)}, u32[]{:S(2)}) collective-permute-start(bf16[64,2048]{1,0:T(8,128)(2,1)S(1)} %fusion.5), channel_id=1, source_target_pairs={{0,2},{1,3},{2,0},{3,1},{4,6},{5,7},{6,4},{7,5},{8,10},{9,11},{10,... | collective-permute-start | bytes 786440 | tf_op jit(solution)/shard_map/ppermute | solution.py:197
  79.9 9.7 %collective-permute-start.11 = (bf16[32,4096]{1,0:T(8,128)(2,1)S(1)}, bf16[32,4096]{1,0:T(8,128)(2,1)S(1)}, u32[]{:S(2)}, u32[]{:S(2)}) collective-permute-start(bf16[32,4096]{1,0:T(8,128)(2,1)S(1)} %pad_maximum_fusion.2), channel_id=1, source_target_pairs={{0,1},{1,0},{2,3},{3,2},{4,5},{5,4},{6,7},{7,6},{8,9},{9,8},{10,11... | collective-permute-start | bytes 786440 | tf_op jit(solution)/shard_map/ppermute | solution.py:206
  85.0 10.2 %collective-permute-start.16 = (bf16[32,4096]{1,0:T(8,128)(2,1)S(1)}, bf16[32,4096]{1,0:T(8,128)(2,1)S(1)}, u32[]{:S(2)}, u32[]{:S(2)}) collective-permute-start(bf16[32,4096]{1,0:T(8,128)(2,1)S(1)} %pad_maximum_fusion.3), channel_id=1, source_target_pairs={{0,1},{1,0},{2,3},{3,2},{4,5},{5,4},{6,7},{7,6},{8,9},{9,8},{10,11... | collective-permute-start | bytes 786440 | tf_op jit(solution)/shard_map/ppermute | solution.py:206
